TPU v7x, 512 devices: a whole 4x8x8 slice. The times are simulated.
512 devices in a mesh: expert: 64 (over y, x, core), fsdp: 8 (over z).
Axes of the slice: x: 4, y: 8, z: 8, core: 2. Of those that a mesh axis runs over, the one named last changes fastest.
Arguments:
- tokens: bfloat16 [1024, 6144], P('expert', 'fsdp'), may hold values from -6 to 6
- expert_ids: int32 [1024, 2], P('expert'), may hold values from 0 to 3, all different within a row; in each aligned block of 16 rows (0 to 15, 16 to 31, ...) at most 10 rows name the same one
- route_logits: float32 [1024, 2], P('expert'), may hold values from -6 to 6
- w_gate: bfloat16 [6144, 32768], P('fsdp', 'expert'), may hold values from -0.078125 to 0.078125
- w_up: bfloat16 [6144, 32768], P('fsdp', 'expert'), may hold values from -0.078125 to 0.078125
- w_down: bfloat16 [32768, 6144], P('expert', 'fsdp'), may hold values from -0.0625 to 0.0625
- out_grad: bfloat16 [1024, 6144], P('expert', 'fsdp'), may hold values from -6 to 6
Outputs:
- layer_out: bfloat16 [1024, 6144], P('expert', 'fsdp')
- tokens_grad: bfloat16 [1024, 6144], P('expert', 'fsdp')
- gate_grad: bfloat16 [6144, 32768], P('fsdp', 'expert')
- up_grad: bfloat16 [6144, 32768], P('fsdp', 'expert')
- down_grad: bfloat16 [32768, 6144], P('expert', 'fsdp')
- logits_grad: float32 [1024, 2], P('expert')
Inputs may be any that keep to these rules, and one draw needn't show every extreme that they name: `expert_ids`: each token names 2 different experts; among the 16 tokens of one index of the expert axis no expert is named by more than 10 tokens, a bound that some block reaches.
All inputs are finite; a program needn't handle non-finite values.
Results may differ from a plain program's by a relative error of at most 0.033.
Values may be sent and summed in bfloat16 or wider, within the bound.
No kernel may reach another device: no remote copies, remote signals or barrier semaphores. Data moves between devices by JAX's collectives and lax.ppermute only.
A program may use at most 64 MiB of HBM per device.

v0:
```python
import jax
import jax.numpy as jnp
from jax import lax
from jax.sharding import PartitionSpec as P

EXPERTS = 4
MOST = 10


def contract(left, right, left_dim, right_dim):
    return lax.dot_general(
        left, right, (((left_dim,), (right_dim,)), ((), ())), preferred_element_type=jnp.float32
    )


def hidden_units(rows, w_gate, w_up):
    gate_part = jnp.dot(rows, w_gate, preferred_element_type=jnp.float32)
    up_part = jnp.dot(rows, w_up, preferred_element_type=jnp.float32)
    gate, upper = (
        lax.psum(gate_part.astype(jnp.bfloat16), "fsdp").astype(jnp.float32),
        lax.psum(up_part.astype(jnp.bfloat16), "fsdp").astype(jnp.float32),
    )
    sig = jax.nn.sigmoid(gate)
    hidden = (gate * sig * upper).astype(jnp.bfloat16)
    return (hidden, gate, upper, sig)


def hidden_grads(route_cot, w_down, gate, upper, sig):
    cot_part = contract(route_cot, w_down, 1, 1)
    hidden_cot = lax.psum(cot_part.astype(jnp.bfloat16), "fsdp").astype(jnp.float32)
    gate_cot = (hidden_cot * upper * sig * (1.0 + gate * (1.0 - sig))).astype(jnp.bfloat16)
    up_cot = (hidden_cot * gate * sig).astype(jnp.bfloat16)
    return (gate_cot, up_cot)


def on_device(tokens, expert_ids, route_logits, w_gate, w_up, w_down, out_grad):
    count = tokens.shape[0]
    top = expert_ids.shape[1]
    width = tokens.shape[1]
    peers = lax.axis_size("expert")
    group = peers // EXPERTS
    flat_ids = expert_ids.reshape(-1)
    onehot = (flat_ids[:, None] == jnp.arange(EXPERTS, dtype=jnp.int32)[None, :]).astype(jnp.int32)
    rank = jnp.sum((jnp.cumsum(onehot, axis=0) - onehot) * onehot, axis=1)
    place = flat_ids * MOST + rank
    first = jax.nn.sigmoid(route_logits[:, 0] - route_logits[:, 1])
    route_weight = jnp.stack([first, 1.0 - first], axis=1)
    cot = out_grad.astype(jnp.float32)

    def pack(rows):
        slots = jnp.zeros((EXPERTS * MOST, width), rows.dtype).at[place].set(rows)
        return jnp.repeat(slots.reshape(EXPERTS, MOST, width), group, axis=0).reshape(
            peers * MOST, width
        )

    def unpack(back):
        widened = back.astype(jnp.float32)
        merged = (
            widened.reshape(EXPERTS, group, MOST, width).sum(axis=1).reshape(EXPERTS * MOST, width)
        )
        return jnp.take(merged, place, axis=0).reshape(count, top, width)

    token_rows = jnp.repeat(tokens, top, axis=0)
    cot_rows = (route_weight.reshape(-1, 1) * jnp.repeat(cot, top, axis=0)).astype(jnp.bfloat16)
    arrived = lax.all_to_all(pack(token_rows), "expert", split_axis=0, concat_axis=0, tiled=True)
    hidden, gate, upper, sig = hidden_units(arrived, w_gate, w_up)
    output = jnp.dot(hidden, w_down, preferred_element_type=jnp.float32).astype(jnp.bfloat16)
    out_back = lax.all_to_all(output, "expert", split_axis=0, concat_axis=0, tiled=True)
    arrived_cot = lax.all_to_all(pack(cot_rows), "expert", split_axis=0, concat_axis=0, tiled=True)
    hidden, gate, upper, sig = (hidden, gate, upper, sig)
    gate_cot, up_cot = hidden_grads(arrived_cot, w_down, gate, upper, sig)
    down_grad = contract(hidden, arrived_cot, 0, 0).astype(jnp.bfloat16)
    gate_grad = contract(arrived, gate_cot, 0, 0).astype(jnp.bfloat16)
    up_grad = contract(arrived, up_cot, 0, 0).astype(jnp.bfloat16)
    tokens_part = (contract(gate_cot, w_gate, 1, 1) + contract(up_cot, w_up, 1, 1)).astype(
        jnp.bfloat16
    )
    tokens_part, gate_grad, up_grad, down_grad = (tokens_part, gate_grad, up_grad, down_grad)
    tokens_back = lax.all_to_all(tokens_part, "expert", split_axis=0, concat_axis=0, tiled=True)
    route_out = unpack(out_back)
    layer_out = jnp.sum(route_weight[:, :, None] * route_out, axis=1).astype(jnp.bfloat16)
    tokens_grad = jnp.sum(unpack(tokens_back), axis=1).astype(jnp.bfloat16)
    local_products = jnp.sum(cot[:, None, :] * route_out, axis=2)
    weight_cot = lax.psum(local_products, "fsdp")
    change = (weight_cot[:, 0] - weight_cot[:, 1]) * first * (1.0 - first)
    logits_grad = jnp.stack([change, -change], axis=1)
    return (layer_out, tokens_grad, gate_grad, up_grad, down_grad, logits_grad)


def solution(mesh):
    return jax.shard_map(
        on_device,
        mesh=mesh,
        in_specs=(
            P("expert", "fsdp"),
            P("expert", None),
            P("expert", None),
            P("fsdp", "expert"),
            P("fsdp", "expert"),
            P("expert", "fsdp"),
            P("expert", "fsdp"),
        ),
        out_specs=(
            P("expert", "fsdp"),
            P("expert", "fsdp"),
            P("fsdp", "expert"),
            P("fsdp", "expert"),
            P("expert", "fsdp"),
            P("expert", None),
        ),
        check_vma=False,
    )
```

profile of v0, /device:TPU:2, one launch (start us, length us, event | category | flops | bytes accessed | tf_op | source)
XLA Modules:
  0.0 328.9 jit_solution(18352824655502011391)
XLA Ops:
  7.2 0.8 broadcast_multiply_fusion
  7.9 0.8 copy.40
  9.3 0.8 broadcast_in_dim.26
  10.1 0.7 scatter_custom_fusion
  10.9 1.3 broadcast_in_dim.27
  12.2 10.8 %all-to-all-start = ((bf16[64,10,768]{2,1,0:T(8,128)(2,1)}), bf16[64,10,768]{2,1,0:T(8,128)(2,1)S(1)}, u32[]{:S(2)}, u32[]{:S(2)}) async-start(bf16[64,10,768]{2,1,0:T(8,128)(2,1)} %bitcast.30), calls=%async_computation | async-start | bytes 3145728 | tf_op jit(solution)/shard_map/all_to_all | solution.py:65
  23.3 0.8 scatter_custom_fusion.1
  24.1 38.8 %all-to-all-done = bf16[64,10,768]{2,1,0:T(8,128)(2,1)S(1)} async-done(((bf16[64,10,768]{2,1,0:T(8,128)(2,1)}), bf16[64,10,768]{2,1,0:T(8,128)(2,1)S(1)}, u32[]{:S(2)}, u32[]{:S(2)}) %all-to-all-start) | async-done | bytes 983072 | tf_op jit(solution)/shard_map/all_to_all | solution.py:65
  63.0 1.3 broadcast_in_dim.29
  64.2 5.6 %all-to-all-start.2 = ((bf16[64,10,768]{2,1,0:T(8,128)(2,1)}), bf16[64,10,768]{2,1,0:T(8,128)(2,1)}, u32[]{:S(2)}, u32[]{:S(2)}) async-start(bf16[64,10,768]{2,1,0:T(8,128)(2,1)} %bitcast.31), calls=%async_computation.2 | async-start | bytes 3145728 | tf_op jit(solution)/shard_map/all_to_all | solution.py:69
  70.3 3.0 convolution_convert_fusion.5
  73.3 1.5 convolution_convert_fusion.6
  74.8 35.0 %all-to-all-done.2 = bf16[64,10,768]{2,1,0:T(8,128)(2,1)} async-done(((bf16[64,10,768]{2,1,0:T(8,128)(2,1)}), bf16[64,10,768]{2,1,0:T(8,128)(2,1)}, u32[]{:S(2)}, u32[]{:S(2)}) %all-to-all-start.2) | async-done | bytes 983072 | tf_op jit(solution)/shard_map/all_to_all | solution.py:69
  109.8 2.3 all_to_all.35
  112.1 1.5 convolution_convert_fusion.4
  113.7 87.1 %all-reduce.3.cloned.1.call-done = (bf16[640,512]{1,0:T(8,128)(2,1)}, bf16[640,512]{1,0:T(8,128)(2,1)}, bf16[640,512]{1,0:T(8,128)(2,1)}) async-done(((bf16[640,512]{1,0:T(8,128)(2,1)}, bf16[640,512]{1,0:T(8,128)(2,1)}, bf16[640,512]{1,0:T(8,128)(2,1)}), (bf16[640,512]{1,0:T(8,128)(2,1)}, bf16[640,512]{1,0:T(8,128)(2,1)}, bf16[640,512]{1,0:T(8,128)(2,1)})) %all-reduce.3.cloned.1.call-update) | async-done | bytes 1966096 | tf_op jit(solution)/shard_map/psum | solution.py:21
  200.7 2.2 convolution_convert_fusion
  202.9 1.3 all_to_all.31
  204.3 10.3 %all-to-all-start.1 = ((bf16[64,10,768]{2,1,0:T(8,128)(2,1)}), bf16[64,10,768]{2,1,0:T(8,128)(2,1)S(1)}, u32[]{:S(2)}, u32[]{:S(2)}) async-start(bf16[64,10,768]{2,1,0:T(8,128)(2,1)} %all_to_all.31), calls=%async_computation.1 | async-start | bytes 3145728 | tf_op jit(solution)/shard_map/all_to_all | solution.py:68
  214.6 2.2 fusion.3
  218.3 1.9 add_convert_fusion
  220.2 2.9 all_to_all.36
  223.1 31.5 %all-to-all-done.1 = bf16[64,10,768]{2,1,0:T(8,128)(2,1)S(1)} async-done(((bf16[64,10,768]{2,1,0:T(8,128)(2,1)}), bf16[64,10,768]{2,1,0:T(8,128)(2,1)S(1)}, u32[]{:S(2)}, u32[]{:S(2)}) %all-to-all-start.1) | async-done | bytes 983072 | tf_op jit(solution)/shard_map/all_to_all | solution.py:68
  254.6 5.6 %all-to-all-start.3 = ((bf16[64,10,768]{2,1,0:T(8,128)(2,1)}), bf16[64,10,768]{2,1,0:T(8,128)(2,1)}, u32[]{:S(2)}, u32[]{:S(2)}) async-start(bf16[64,10,768]{2,1,0:T(8,128)(2,1)} %all_to_all.36), calls=%async_computation.3 | async-start | bytes 3145728 | tf_op jit(solution)/shard_map/all_to_all | solution.py:79
  260.2 3.0 convolution_convert_fusion.3
  263.3 1.8 convolution_convert_fusion.1
  265.2 1.8 convolution_convert_fusion.2
  267.2 32.9 %all-to-all-done.3 = bf16[64,10,768]{2,1,0:T(8,128)(2,1)} async-done(((bf16[64,10,768]{2,1,0:T(8,128)(2,1)}), bf16[64,10,768]{2,1,0:T(8,128)(2,1)}, u32[]{:S(2)}, u32[]{:S(2)}) %all-to-all-start.3) | async-done | bytes 983072 | tf_op jit(solution)/shard_map/all_to_all | solution.py:79
  300.1 1.7 convert_reduce_fusion
  303.5 16.4 %psum.31 = f32[16,2]{0,1:T(2,128)S(1)} all-reduce(f32[16,2]{0,1:T(2,128)S(1)} %copy.43), channel_id=1, replica_groups=mesh['expert'=64,'fsdp'=8] {'fsdp'}, use_global_device_ids=true, to_apply=%region_12.14 | all-reduce | flops 32 | bytes 256 | tf_op jit(solution)/shard_map/psum | solution.py:84
  319.9 0.8 multiply_reduce_fusion.1
  321.3 0.7 reduce_sum.63
  (64 shorter events, 5.5 us)
Async XLA Ops:
  7.2 104.9 %copy-start = (bf16[512,768]{1,0:T(8,128)(2,1)S(1)}, bf16[512,768]{1,0:T(8,128)(2,1)}, u32[]{:S(2)}) copy-start(bf16[512,768]{1,0:T(8,128)(2,1)} %param.14) | copy-start | bytes 2359300
  12.1 10.8 %copy-start.13 = (f32[16,2]{0,1:T(2,128)S(1)}, f32[16,2]{0,1:T(2,128)}, u32[]{:S(2)}) copy-start(f32[16,2]{0,1:T(2,128)} %param.11) | copy-start | bytes 388
  12.1 11.0 %copy-start.12 = (bf16[16,768]{1,0:T(8,128)(2,1)S(1)}, bf16[16,768]{1,0:T(8,128)(2,1)}, u32[]{:S(2)}) copy-start(bf16[16,768]{1,0:T(8,128)(2,1)} %param.15) | copy-start | bytes 73732
  12.2 50.8 %all-to-all-start = ((bf16[64,10,768]{2,1,0:T(8,128)(2,1)}), bf16[64,10,768]{2,1,0:T(8,128)(2,1)S(1)}, u32[]{:S(2)}, u32[]{:S(2)}) async-start(bf16[64,10,768]{2,1,0:T(8,128)(2,1)} %bitcast.30), calls=%async_computation | async-start | bytes 3145728 | tf_op jit(solution)/shard_map/all_to_all | solution.py:65
  64.2 45.6 %all-to-all-start.2 = ((bf16[64,10,768]{2,1,0:T(8,128)(2,1)}), bf16[64,10,768]{2,1,0:T(8,128)(2,1)}, u32[]{:S(2)}, u32[]{:S(2)}) async-start(bf16[64,10,768]{2,1,0:T(8,128)(2,1)} %bitcast.31), calls=%async_computation.2 | async-start | bytes 3145728 | tf_op jit(solution)/shard_map/all_to_all | solution.py:69
  69.8 130.9 %all-reduce.3.cloned.1.call-start = ((), (), s32[]{:S(2)}) async-start(), calls=%async_computation.4 | async-start | bytes 3932160 | tf_op jit(solution)/shard_map/psum | solution.py:21
  70.3 3.0 copy-start.1
  70.3 3.0 copy-start.5
  112.1 1.6 copy-start.3
  204.3 50.3 %all-to-all-start.1 = ((bf16[64,10,768]{2,1,0:T(8,128)(2,1)}), bf16[64,10,768]{2,1,0:T(8,128)(2,1)S(1)}, u32[]{:S(2)}, u32[]{:S(2)}) async-start(bf16[64,10,768]{2,1,0:T(8,128)(2,1)} %all_to_all.31), calls=%async_computation.1 | async-start | bytes 3145728 | tf_op jit(solution)/shard_map/all_to_all | solution.py:68
  214.5 2.2 copy-start.6
  216.7 1.1 copy-start.7
  216.7 1.3 copy-start.9
  216.7 1.5 copy-start.14
  254.6 45.6 %all-to-all-start.3 = ((bf16[64,10,768]{2,1,0:T(8,128)(2,1)}), bf16[64,10,768]{2,1,0:T(8,128)(2,1)}, u32[]{:S(2)}, u32[]{:S(2)}) async-start(bf16[64,10,768]{2,1,0:T(8,128)(2,1)} %all_to_all.36), calls=%async_computation.3 | async-start | bytes 3145728 | tf_op jit(solution)/shard_map/all_to_all | solution.py:79
  260.2 3.1 copy-start.4
  260.2 3.1 copy-start.8
  260.2 3.1 copy-start.11
  263.3 1.9 copy-start.2
  263.3 1.8 copy-start.10
Sparse Core Ops, SparseCore 0:
  113.8 86.9 all-reduce.2
where the time goes:
time: 330 us; the launch traced here: 329 us
  waiting for transfers between devices  225 us (68%)
  starting transfers between devices  32.3 us (10%)
  matrix products  17.5 us (5%)
  blocking collectives  16.4 us (5%)
  local copies, waits for them, and re-layouts  14.7 us (4%)
  between operations  14.4 us (4%)
  other arithmetic  8.31 us (3%)
    psum x1, waiting for transfers between devices, hidden_units(): lax.psum(up_part.astype(jnp.bfloat16), 'fsdp').astype(jnp.float32)  87.1 us
    all_to_all x1, waiting for transfers between devices, on_device(): lax.all_to_all(pack(token_rows), 'expert', split_axis=0, concat_axis=0, t...  38.8 us
    all_to_all x1, waiting for transfers between devices, on_device(): lax.all_to_all(pack(cot_rows), 'expert', split_axis=0, concat_axis=0, til...  35 us
    all_to_all x1, waiting for transfers between devices, on_device(): lax.all_to_all(tokens_part, 'expert', split_axis=0, concat_axis=0, tiled=...  32.9 us
    all_to_all x1, waiting for transfers between devices, on_device(): lax.all_to_all(output, 'expert', split_axis=0, concat_axis=0, tiled=True)  31.5 us
    psum x1, blocking collectives, on_device(): weight_cot = lax.psum(local_products, 'fsdp')  16.4 us
    dot_general x6, matrix products, contract(): lax.dot_general(left, right, (((left_dim,), (right_dim,)), ((), ())), pre...  10.8 us
    all_to_all x1, starting transfers between devices, on_device(): lax.all_to_all(pack(token_rows), 'expert', split_axis=0, concat_axis=0, t...  10.8 us
  transfers between devices with their start and end apart: 5, of which 5 were waited for; matrix products, arithmetic and copies ran while one was open for 5% of the time, Pallas kernels for 0%

commit v1 on v0

v1 whole, which is shorter than its diff:
```python
import jax
import jax.numpy as jnp
from jax import lax
from jax.sharding import PartitionSpec as P

EXPERTS = 4
MOST = 10
CORES = 2
LANES = 128


def contract(left, right, left_dim, right_dim):
    return lax.dot_general(
        left, right, (((left_dim,), (right_dim,)), ((), ())), preferred_element_type=jnp.float32
    )


def on_device(tokens, expert_ids, route_logits, w_gate, w_up, w_down, out_grad):
    count, width = tokens.shape
    hidden_width = w_gate.shape[1]
    peers = lax.axis_size("expert")
    planes = lax.axis_size("fsdp")
    chips = peers // CORES
    slab = MOST * width // LANES
    half = chips * MOST
    rows = CORES * half
    own = rows // planes
    same_core = [[CORES * p + c for p in range(chips)] for c in range(CORES)]
    other_core = [(i, i ^ 1) for i in range(peers)]

    def across_chips(blocks):
        return lax.all_to_all(
            blocks, "expert", split_axis=0, concat_axis=0, axis_index_groups=same_core, tiled=True
        )

    def swap(value):
        return lax.ppermute(value, "expert", other_core)

    def across_planes(blocks):
        return lax.all_to_all(blocks, "fsdp", split_axis=0, concat_axis=0, tiled=True)

    experts = jnp.arange(EXPERTS, dtype=jnp.int32)
    named = expert_ids[:, :, None] == experts[None, None, :]
    chosen = jnp.any(named, axis=1)
    before = jnp.arange(count)[:, None, None] < jnp.arange(count)[None, :, None]
    rank = jnp.sum((before & chosen[:, None, :]).astype(jnp.int32), axis=0)
    first = jax.nn.sigmoid(route_logits[:, 0] - route_logits[:, 1])
    route_weight = jnp.stack([first, 1.0 - first], axis=1)
    scale = jnp.sum(jnp.where(named, route_weight[:, :, None], 0.0), axis=1)
    slots = jnp.arange(MOST, dtype=jnp.int32)
    picked = (chosen.T[:, None, :]) & (rank.T[:, None, :] == slots[None, :, None])
    select = picked.reshape(EXPERTS * MOST, count)
    slot_scale = jnp.sum(
        jnp.where(picked, scale.T[:, None, :], 0.0), axis=2
    ).reshape(EXPERTS * MOST, 1)
    token_slots = contract(select.astype(jnp.bfloat16), tokens, 1, 0).astype(jnp.bfloat16)
    cot_slots = (slot_scale * contract(select.astype(jnp.bfloat16), out_grad, 1, 0)).astype(
        jnp.bfloat16
    )

    def blocks_for_all(slot_rows):
        blocks = slot_rows.reshape(EXPERTS, slab, LANES)
        return jnp.repeat(blocks, chips // EXPERTS, axis=0)

    def rows_of(blocks):
        return blocks.reshape(half, width)

    def gather_rows(slot_rows):
        mine = across_chips(blocks_for_all(slot_rows))
        return jnp.concatenate([rows_of(mine), rows_of(swap(mine))], axis=0)

    def give_back(part):
        mine = part[:half].astype(jnp.float32) + swap(part[half:]).astype(jnp.float32)
        sent = mine.astype(jnp.bfloat16).reshape(chips, slab, LANES)
        back = across_chips(sent).astype(jnp.float32)
        return (
            back.reshape(EXPERTS, chips // EXPERTS, slab, LANES)
            .sum(axis=1)
            .reshape(EXPERTS * MOST, width)
        )

    def plane_sum(parts):
        return across_planes(parts.reshape(planes, own, -1)).astype(jnp.float32).sum(axis=0)

    def to_all_planes(value):
        copies = jnp.broadcast_to(value[None], (planes,) + value.shape)
        return across_planes(copies).reshape(rows, -1)

    arrived = gather_rows(token_slots)
    arrived_cot = gather_rows(cot_slots)
    gate_part = jnp.dot(arrived, w_gate, preferred_element_type=jnp.float32).astype(jnp.bfloat16)
    up_part = jnp.dot(arrived, w_up, preferred_element_type=jnp.float32).astype(jnp.bfloat16)
    both = plane_sum(jnp.concatenate([gate_part, up_part], axis=1))
    gate, upper = both[:, :hidden_width], both[:, hidden_width:]
    sig = jax.nn.sigmoid(gate)
    hidden_own = (gate * sig * upper).astype(jnp.bfloat16)
    hidden_cot = plane_sum(contract(arrived_cot, w_down, 1, 1).astype(jnp.bfloat16))
    gate_cot_own = (hidden_cot * upper * sig * (1.0 + gate * (1.0 - sig))).astype(jnp.bfloat16)
    up_cot_own = (hidden_cot * gate * sig).astype(jnp.bfloat16)
    hidden = to_all_planes(hidden_own)
    cots = to_all_planes(jnp.concatenate([gate_cot_own, up_cot_own], axis=1))
    gate_cot, up_cot = cots[:, :hidden_width], cots[:, hidden_width:]

    out_part = jnp.dot(hidden, w_down, preferred_element_type=jnp.float32).astype(jnp.bfloat16)
    out_slots = give_back(out_part)
    tokens_part = (contract(gate_cot, w_gate, 1, 1) + contract(up_cot, w_up, 1, 1)).astype(
        jnp.bfloat16
    )
    grad_slots = give_back(tokens_part)
    down_grad = contract(hidden, arrived_cot, 0, 0).astype(jnp.bfloat16)
    gate_grad = contract(arrived, gate_cot, 0, 0).astype(jnp.bfloat16)
    up_grad = contract(arrived, up_cot, 0, 0).astype(jnp.bfloat16)

    rank_of_route = jnp.sum(jnp.where(named, rank[:, None, :], 0), axis=2)
    place = (expert_ids * MOST + rank_of_route).reshape(-1)
    route_out = jnp.take(out_slots, place, axis=0).reshape(count, -1, width)
    layer_out = jnp.sum(route_weight[:, :, None] * route_out, axis=1).astype(jnp.bfloat16)
    route_grad = jnp.take(grad_slots, place, axis=0).reshape(count, -1, width)
    tokens_grad = jnp.sum(route_grad, axis=1).astype(jnp.bfloat16)
    local_products = jnp.sum(out_grad.astype(jnp.float32)[:, None, :] * route_out, axis=2)
    copies = jnp.broadcast_to(local_products[None], (planes,) + local_products.shape)
    weight_cot = across_planes(copies).sum(axis=0)
    change = (weight_cot[:, 0] - weight_cot[:, 1]) * first * (1.0 - first)
    logits_grad = jnp.stack([change, -change], axis=1)
    return (layer_out, tokens_grad, gate_grad, up_grad, down_grad, logits_grad)


def solution(mesh):
    return jax.shard_map(
        on_device,
        mesh=mesh,
        in_specs=(
            P("expert", "fsdp"),
            P("expert", None),
            P("expert", None),
            P("fsdp", "expert"),
            P("fsdp", "expert"),
            P("expert", "fsdp"),
            P("expert", "fsdp"),
        ),
        out_specs=(
            P("expert", "fsdp"),
            P("expert", "fsdp"),
            P("fsdp", "expert"),
            P("fsdp", "expert"),
            P("expert", "fsdp"),
            P("expert", None),
        ),
        check_vma=False,
    )
```

time: 330 us -> 272 us (0.82)
  the two profiles are of different devices: /device:TPU:2 before, /device:TPU:8 now
where the time goes in v1:
time: 272 us; the launch traced here: 271 us
  blocking collectives  185 us (68%)
  waiting for transfers between devices  31.7 us (12%)
  starting transfers between devices  18.1 us (7%)
  matrix products  14.5 us (5%)
  local copies, waits for them, and re-layouts  14.2 us (5%)
  other arithmetic  6.27 us (2%)
    all_to_all x5, blocking collectives, across_planes(): lax.all_to_all(blocks, 'fsdp', split_axis=0, concat_axis=0, tiled=True)  137 us
    all_to_all x2, blocking collectives, across_chips(): lax.all_to_all(blocks, 'expert', split_axis=0, concat_axis=0, axis_index_...  47.5 us
    all_to_all x2, waiting for transfers between devices, across_chips(): lax.all_to_all(blocks, 'expert', split_axis=0, concat_axis=0, axis_index_...  27.7 us
    dot_general x8, matrix products, contract(): lax.dot_general(left, right, (((left_dim,), (right_dim,)), ((), ())), pre...  10.8 us
    all_to_all x2, starting transfers between devices, across_chips(): lax.all_to_all(blocks, 'expert', split_axis=0, concat_axis=0, axis_index_...  10.3 us
    ppermute x4, starting transfers between devices, swap(): return lax.ppermute(value, 'expert', other_core)  7.83 us
  transfers between devices with their start and end apart: 6, of which 6 were waited for; matrix products, arithmetic and copies ran while one was open for 4% of the time, Pallas kernels for 0%

profile of v1, /device:TPU:8, one launch (start us, length us, event | category | flops | bytes accessed | tf_op | source)
XLA Modules:
  0.0 270.8 jit_solution(1375900614920526283)
XLA Ops:
  2.2 1.0 convolution_convert_fusion.7
  3.3 27.2 %all_to_all.45 = bf16[32,60,128]{2,1,0:T(8,128)(2,1)S(1)} all-to-all(bf16[32,60,128]{2,1,0:T(8,128)(2,1)S(1)} %bitcast.42), channel_id=1, replica_groups={{0,16,32,48,64,80,96,112,128,144,160,176,192,208,224,240,256,272,288,30..., dimensions={0} | all-to-all | bytes 983040 | tf_op jit(solution)/shard_map/all_to_all | solution.py:32
  30.5 1.9 collective-permute-start
  32.9 0.8 constant_dynamic-update-slice_fusion.1
  34.7 0.8 constant_dynamic-update-slice_fusion
  35.6 2.2 convolution_convert_fusion.5
  37.8 0.8 convolution_convert_fusion.6
  39.4 44.8 %all_to_all.46 = bf16[8,80,1024]{2,1,0:T(8,128)(2,1)S(1)} all-to-all(bf16[8,80,1024]{2,1,0:T(8,128)(2,1)S(1)} %bitcast.37), channel_id=1, replica_groups=mesh['expert'=64,'fsdp'=8] {'fsdp'}, dimensions={0} | all-to-all | bytes 2621440 | tf_op jit(solution)/shard_map/all_to_all | solution.py:40
  84.5 21.9 %all_to_all.47 = bf16[8,80,512]{2,1,0:T(8,128)(2,1)S(1)} all-to-all(bf16[8,80,512]{2,1,0:T(8,128)(2,1)S(1)} %broadcast_in_dim.85), channel_id=1, replica_groups=mesh['expert'=64,'fsdp'=8] {'fsdp'}, dimensions={0} | all-to-all | bytes 1310720 | tf_op jit(solution)/shard_map/all_to_all | solution.py:40
  107.3 1.9 collective-permute-start.1
  109.2 1.8 collective-permute-done.1
  111.2 1.3 reshape.127
  112.5 5.2 %all-to-all-start.3 = ((bf16[32,60,128]{2,1,0:T(8,128)(2,1)}), bf16[32,60,128]{2,1,0:T(8,128)(2,1)S(1)}, u32[]{:S(2)}, u32[]{:S(2)}) async-start(bf16[32,60,128]{2,1,0:T(8,128)(2,1)} %reshape.127), calls=%async_computation.3 | async-start | bytes 1048576 | tf_op jit(solution)/shard_map/all_to_all | solution.py:32
  118.0 17.1 %all-to-all-done.3 = bf16[32,60,128]{2,1,0:T(8,128)(2,1)S(1)} async-done(((bf16[32,60,128]{2,1,0:T(8,128)(2,1)}), bf16[32,60,128]{2,1,0:T(8,128)(2,1)S(1)}, u32[]{:S(2)}, u32[]{:S(2)}) %all-to-all-start.3) | async-done | bytes 491552 | tf_op jit(solution)/shard_map/all_to_all | solution.py:32
  136.2 10.1 %all_to_all.48 = f32[8,16,2]{1,2,0:T(2,128)S(1)} all-to-all(f32[8,16,2]{1,2,0:T(2,128)S(1)} %broadcast_in_dim.95), channel_id=1, replica_groups=mesh['expert'=64,'fsdp'=8] {'fsdp'}, dimensions={0} | all-to-all | bytes 2048 | tf_op jit(solution)/shard_map/all_to_all | solution.py:40
  147.1 20.3 %all_to_all.49 = bf16[32,60,128]{2,1,0:T(8,128)(2,1)S(1)} all-to-all(bf16[32,60,128]{2,1,0:T(8,128)(2,1)S(1)} %bitcast.43), channel_id=1, replica_groups={{0,16,32,48,64,80,96,112,128,144,160,176,192,208,224,240,256,272,288,30..., dimensions={0} | all-to-all | bytes 983040 | tf_op jit(solution)/shard_map/all_to_all | solution.py:32
  167.4 1.9 collective-permute-start.2
  169.8 0.8 constant_dynamic-update-slice_fusion.3
  171.7 0.8 constant_dynamic-update-slice_fusion.2
  172.5 1.9 convolution_convert_fusion.4
  174.4 23.3 %all_to_all.50 = bf16[8,80,512]{2,1,0:T(8,128)(2,1)S(1)} all-to-all(bf16[8,80,512]{2,1,0:T(8,128)(2,1)S(1)} %bitcast.46), channel_id=1, replica_groups=mesh['expert'=64,'fsdp'=8] {'fsdp'}, dimensions={0} | all-to-all | bytes 1310720 | tf_op jit(solution)/shard_map/all_to_all | solution.py:40
  198.1 37.4 %all_to_all.51 = bf16[8,80,1024]{2,1,0:T(8,128)(2,1)S(1)} all-to-all(bf16[8,80,1024]{2,1,0:T(8,128)(2,1)S(1)} %broadcast_in_dim.93), channel_id=1, replica_groups=mesh['expert'=64,'fsdp'=8] {'fsdp'}, dimensions={0} | all-to-all | bytes 2621440 | tf_op jit(solution)/shard_map/all_to_all | solution.py:40
  237.3 0.8 slice.59
  238.1 2.1 collective-permute-start.3
  241.2 1.0 collective-permute-done.3
  242.2 1.9 add_convert_fusion.1
  244.2 2.4 reshape.139
  246.5 5.1 %all-to-all-start.7 = ((bf16[32,60,128]{2,1,0:T(8,128)(2,1)}), bf16[32,60,128]{2,1,0:T(8,128)(2,1)S(1)}, u32[]{:S(2)}, u32[]{:S(2)}) async-start(bf16[32,60,128]{2,1,0:T(8,128)(2,1)} %reshape.139), calls=%async_computation.7 | async-start | bytes 1048576 | tf_op jit(solution)/shard_map/all_to_all | solution.py:32
  252.2 3.0 %convolution_convert_fusion.1 = bf16[512,768]{1,0:T(8,128)(2,1)} fusion(bf16[640,512]{1,0:T(8,128)(2,1)S(1)} %bitcast.45, bf16[640,768]{1,0:T(8,128)(2,1)} %constant_dynamic-update-slice_fusion.2), kind=kOutput, calls=%fused_computation.5 | convolution fusion | flops 503709696 | bytes 2424832 | tf_op jit(solution)/shard_map/dot_general | solution.py:13
  255.2 1.7 convolution_convert_fusion.2
  256.9 1.7 convolution_convert_fusion.3
  258.6 10.6 %all-to-all-done.7 = bf16[32,60,128]{2,1,0:T(8,128)(2,1)S(1)} async-done(((bf16[32,60,128]{2,1,0:T(8,128)(2,1)}), bf16[32,60,128]{2,1,0:T(8,128)(2,1)S(1)}, u32[]{:S(2)}, u32[]{:S(2)}) %all-to-all-start.7) | async-done | bytes 491552 | tf_op jit(solution)/shard_map/all_to_all | solution.py:32
  (95 shorter events, 14.3 us)
Async XLA Ops:
  0.6 105.8 %copy-start = (bf16[512,768]{1,0:T(8,128)(2,1)S(1)}, bf16[512,768]{1,0:T(8,128)(2,1)}, u32[]{:S(2)}) copy-start(bf16[512,768]{1,0:T(8,128)(2,1)} %param.14) | copy-start | bytes 2359300
  30.5 3.8 %collective-permute-start = (bf16[32,60,128]{2,1,0:T(8,128)(2,1)S(1)}, bf16[32,60,128]{2,1,0:T(8,128)(2,1)S(1)}, u32[]{:S(2)}, u32[]{:S(2)}) collective-permute-start(bf16[32,60,128]{2,1,0:T(8,128)(2,1)S(1)} %all_to_all.45), channel_id=1, source_target_pairs={{0,8},{8,0},{16,24},{24,16},{32,40},{40,32},{48,56},{56,48},{64,72... | collective-permute-start | bytes 1474568 | tf_op jit(solution)/shard_map/ppermute | solution.py:37
  32.9 2.7 copy-start.3
  35.6 2.2 copy-start.1
  35.6 2.2 copy-start.7
  106.4 0.8 copy-start.5
  107.3 3.8 %collective-permute-start.1 = (bf16[320,768]{1,0:T(8,128)(2,1)S(1)}, bf16[320,768]{1,0:T(8,128)(2,1)S(1)}, u32[]{:S(2)}, u32[]{:S(2)}) collective-permute-start(bf16[320,768]{1,0:T(8,128)(2,1)S(1)} %slice.55), channel_id=1, source_target_pairs={{0,8},{8,0},{16,24},{24,16},{32,40},{40,32},{48,56},{56,48},{64,72... | collective-permute-start | bytes 1474568 | tf_op jit(solution)/shard_map/ppermute | solution.py:37
  111.2 6.4 %copy-start.10 = (s32[16,2]{0,1:T(2,128)S(1)}, s32[16,2]{0,1:T(2,128)}, u32[]{:S(2)}) copy-start(s32[16,2]{0,1:T(2,128)} %param.10) | copy-start | bytes 388
  111.2 6.7 %copy-start.9 = (bf16[16,768]{1,0:T(8,128)(2,1)S(1)}, bf16[16,768]{1,0:T(8,128)(2,1)}, u32[]{:S(2)}) copy-start(bf16[16,768]{1,0:T(8,128)(2,1)} %param.15) | copy-start | bytes 73732
  112.5 22.7 %all-to-all-start.3 = ((bf16[32,60,128]{2,1,0:T(8,128)(2,1)}), bf16[32,60,128]{2,1,0:T(8,128)(2,1)S(1)}, u32[]{:S(2)}, u32[]{:S(2)}) async-start(bf16[32,60,128]{2,1,0:T(8,128)(2,1)} %reshape.127), calls=%async_computation.3 | async-start | bytes 1048576 | tf_op jit(solution)/shard_map/all_to_all | solution.py:32
  117.6 28.7 %copy-start.11 = (f32[16,2]{0,1:T(2,128)S(1)}, f32[16,2]{0,1:T(2,128)}, u32[]{:S(2)}) copy-start(f32[16,2]{0,1:T(2,128)} %param.11) | copy-start | bytes 388
  167.4 3.8 %collective-permute-start.2 = (bf16[32,60,128]{2,1,0:T(8,128)(2,1)S(1)}, bf16[32,60,128]{2,1,0:T(8,128)(2,1)S(1)}, u32[]{:S(2)}, u32[]{:S(2)}) collective-permute-start(bf16[32,60,128]{2,1,0:T(8,128)(2,1)S(1)} %all_to_all.49), channel_id=1, source_target_pairs={{0,8},{8,0},{16,24},{24,16},{32,40},{40,32},{48,56},{56,48},{64,72... | collective-permute-start | bytes 1474568 | tf_op jit(solution)/shard_map/ppermute | solution.py:37
  198.1 37.4 %copy-start.2 = (bf16[768,512]{1,0:T(8,128)(2,1)S(1)}, bf16[768,512]{1,0:T(8,128)(2,1)}, u32[]{:S(2)}) copy-start(bf16[768,512]{1,0:T(8,128)(2,1)} %param.12) | copy-start | bytes 2359300
  235.5 1.1 copy-start.4
  238.1 4.1 %collective-permute-start.3 = (bf16[320,768]{1,0:T(8,128)(2,1)}, bf16[320,768]{1,0:T(8,128)(2,1)}, u32[]{:S(2)}, u32[]{:S(2)}) collective-permute-start(bf16[320,768]{1,0:T(8,128)(2,1)} %slice.59), channel_id=1, source_target_pairs={{0,8},{8,0},{16,24},{24,16},{32,40},{40,32},{48,56},{56,48},{64,72... | collective-permute-start | bytes 1474568 | tf_op jit(solution)/shard_map/ppermute | solution.py:37
  244.2 8.1 %copy-start.6 = (bf16[8,80,512]{2,1,0:T(8,128)(2,1)S(1)}, bf16[8,80,512]{2,1,0:T(8,128)(2,1)}, u32[]{:S(2)}) copy-start(bf16[8,80,512]{2,1,0:T(8,128)(2,1)} %copy-done.5) | copy-start | bytes 1966084
  246.5 22.6 %all-to-all-start.7 = ((bf16[32,60,128]{2,1,0:T(8,128)(2,1)}), bf16[32,60,128]{2,1,0:T(8,128)(2,1)S(1)}, u32[]{:S(2)}, u32[]{:S(2)}) async-start(bf16[32,60,128]{2,1,0:T(8,128)(2,1)} %reshape.139), calls=%async_computation.7 | async-start | bytes 1048576 | tf_op jit(solution)/shard_map/all_to_all | solution.py:32
  252.2 3.0 %copy-start.8 = (bf16[640,768]{1,0:T(8,128)(2,1)S(1)}, bf16[640,768]{1,0:T(8,128)(2,1)}, u32[]{:S(2)}) copy-start(bf16[640,768]{1,0:T(8,128)(2,1)} %constant_dynamic-update-slice_fusion) | copy-start | bytes 2949124

commit v2 on v1

--- a/solution.py
+++ b/solution.py
@@ -38,6 +38,9 @@
 
     def across_planes(blocks):
         return lax.all_to_all(blocks, "fsdp", split_axis=0, concat_axis=0, tiled=True)
+
+    def after(value, *earlier):
+        return lax.optimization_barrier((value,) + earlier)[0]
 
     experts = jnp.arange(EXPERTS, dtype=jnp.int32)
     named = expert_ids[:, :, None] == experts[None, None, :]
@@ -87,39 +90,44 @@
         return across_planes(copies).reshape(rows, -1)
 
     arrived = gather_rows(token_slots)
-    arrived_cot = gather_rows(cot_slots)
     gate_part = jnp.dot(arrived, w_gate, preferred_element_type=jnp.float32).astype(jnp.bfloat16)
     up_part = jnp.dot(arrived, w_up, preferred_element_type=jnp.float32).astype(jnp.bfloat16)
-    both = plane_sum(jnp.concatenate([gate_part, up_part], axis=1))
+    parts = jnp.concatenate([gate_part, up_part], axis=1)
+    both = lax.psum_scatter(parts, "fsdp", scatter_dimension=0, tiled=True).astype(jnp.float32)
+
+    arrived_cot = gather_rows(after(cot_slots, parts))
+    hidden_cot = plane_sum(contract(arrived_cot, w_down, 1, 1).astype(jnp.bfloat16))
+    both = after(both, hidden_cot)
     gate, upper = both[:, :hidden_width], both[:, hidden_width:]
     sig = jax.nn.sigmoid(gate)
     hidden_own = (gate * sig * upper).astype(jnp.bfloat16)
-    hidden_cot = plane_sum(contract(arrived_cot, w_down, 1, 1).astype(jnp.bfloat16))
     gate_cot_own = (hidden_cot * upper * sig * (1.0 + gate * (1.0 - sig))).astype(jnp.bfloat16)
     up_cot_own = (hidden_cot * gate * sig).astype(jnp.bfloat16)
-    hidden = to_all_planes(hidden_own)
-    cots = to_all_planes(jnp.concatenate([gate_cot_own, up_cot_own], axis=1))
-    gate_cot, up_cot = cots[:, :hidden_width], cots[:, hidden_width:]
+    cots_own = jnp.concatenate([gate_cot_own, up_cot_own], axis=1)
+    cots = lax.all_gather(cots_own, "fsdp", axis=0, tiled=True)
 
+    hidden = to_all_planes(after(hidden_own, cots_own))
     out_part = jnp.dot(hidden, w_down, preferred_element_type=jnp.float32).astype(jnp.bfloat16)
     out_slots = give_back(out_part)
+    down_grad = contract(hidden, arrived_cot, 0, 0).astype(jnp.bfloat16)
+
+    gate_cot, up_cot = cots[:, :hidden_width], cots[:, hidden_width:]
     tokens_part = (contract(gate_cot, w_gate, 1, 1) + contract(up_cot, w_up, 1, 1)).astype(
         jnp.bfloat16
     )
     grad_slots = give_back(tokens_part)
-    down_grad = contract(hidden, arrived_cot, 0, 0).astype(jnp.bfloat16)
     gate_grad = contract(arrived, gate_cot, 0, 0).astype(jnp.bfloat16)
     up_grad = contract(arrived, up_cot, 0, 0).astype(jnp.bfloat16)
 
     rank_of_route = jnp.sum(jnp.where(named, rank[:, None, :], 0), axis=2)
-    place = (expert_ids * MOST + rank_of_route).reshape(-1)
+    place = after((expert_ids * MOST + rank_of_route).reshape(-1), tokens_part)
     route_out = jnp.take(out_slots, place, axis=0).reshape(count, -1, width)
     layer_out = jnp.sum(route_weight[:, :, None] * route_out, axis=1).astype(jnp.bfloat16)
-    route_grad = jnp.take(grad_slots, place, axis=0).reshape(count, -1, width)
-    tokens_grad = jnp.sum(route_grad, axis=1).astype(jnp.bfloat16)
     local_products = jnp.sum(out_grad.astype(jnp.float32)[:, None, :] * route_out, axis=2)
     copies = jnp.broadcast_to(local_products[None], (planes,) + local_products.shape)
     weight_cot = across_planes(copies).sum(axis=0)
+    route_grad = jnp.take(after(grad_slots, weight_cot), place, axis=0).reshape(count, -1, width)
+    tokens_grad = jnp.sum(route_grad, axis=1).astype(jnp.bfloat16)
     change = (weight_cot[:, 0] - weight_cot[:, 1]) * first * (1.0 - first)
     logits_grad = jnp.stack([change, -change], axis=1)
     return (layer_out, tokens_grad, gate_grad, up_grad, down_grad, logits_grad)

time: 272 us -> 219 us (0.81)
  blocking collectives: 185 us -> 35 us
  waiting for transfers between devices: 31.7 us -> 84.4 us
  starting transfers between devices: 18.1 us -> 43.6 us
  between operations: 1.06 us -> 14.5 us
    all_to_all x5 -> x1, blocking collectives: 137 us -> 35 us  [across_planes(): lax.all_to_all(blocks, 'fsdp', split_axis=0, concat_axis=0, tiled=True)]
    all_to_all x2 -> x0, blocking collectives: 47.5 us -> none  [across_chips(): lax.all_to_all(blocks, 'expert', split_axis=0, concat_axis=0, axis_index_...]
    all_to_all x0 -> x2, waiting for transfers between devices: none -> 28.4 us  [across_planes(): lax.all_to_all(blocks, 'fsdp', split_axis=0, concat_axis=0, tiled=True)]
    all_to_all x2 -> x4, waiting for transfers between devices: 27.7 us -> 55.2 us  [across_chips(): lax.all_to_all(blocks, 'expert', split_axis=0, concat_axis=0, axis_index_...]
    all_to_all x2 -> x4, starting transfers between devices: 10.3 us -> 28.6 us  [across_chips(): lax.all_to_all(blocks, 'expert', split_axis=0, concat_axis=0, axis_index_...]
    all_to_all x0 -> x2, starting transfers between devices: none -> 7.33 us  [across_planes(): lax.all_to_all(blocks, 'fsdp', split_axis=0, concat_axis=0, tiled=True)]
    ppermute x4, waiting for transfers between devices: 4.04 us -> 0.59 us  [swap(): return lax.ppermute(value, 'expert', other_core)]
  transfers between devices with their start and end apart: 6 -> 12, of which waited for: 6 -> 8; matrix products, arithmetic and copies ran while one was open for 4% -> 13% of each run, Pallas kernels for 0% -> 0%
where the time goes in v2:
time: 219 us; the launch traced here: 218 us
  waiting for transfers between devices  84.4 us (39%)
  starting transfers between devices  43.6 us (20%)
  blocking collectives  35 us (16%)
  matrix products  16.9 us (8%)
  local copies, waits for them, and re-layouts  16.4 us (7%)
  between operations  14.5 us (7%)
  other arithmetic  6.84 us (3%)
    all_to_all x4, waiting for transfers between devices, across_chips(): lax.all_to_all(blocks, 'expert', split_axis=0, concat_axis=0, axis_index_...  55.2 us
    all_to_all x1, blocking collectives, across_planes(): lax.all_to_all(blocks, 'fsdp', split_axis=0, concat_axis=0, tiled=True)  35 us
    all_to_all x4, starting transfers between devices, across_chips(): lax.all_to_all(blocks, 'expert', split_axis=0, concat_axis=0, axis_index_...  28.6 us
    all_to_all x2, waiting for transfers between devices, across_planes(): lax.all_to_all(blocks, 'fsdp', split_axis=0, concat_axis=0, tiled=True)  28.4 us
    dot_general x8, matrix products, contract(): lax.dot_general(left, right, (((left_dim,), (right_dim,)), ((), ())), pre...  13.2 us
    ppermute x4, starting transfers between devices, swap(): return lax.ppermute(value, 'expert', other_core)  7.65 us
    all_to_all x2, starting transfers between devices, across_planes(): lax.all_to_all(blocks, 'fsdp', split_axis=0, concat_axis=0, tiled=True)  7.33 us
  transfers between devices with their start and end apart: 12, of which 8 were waited for; matrix products, arithmetic and copies ran while one was open for 13% of the time, Pallas kernels for 0%

profile of v2, /device:TPU:8, one launch (start us, length us, event | category | flops | bytes accessed | tf_op | source)
XLA Modules:
  0.0 217.5 jit_solution(12995295178044074715)
XLA Ops:
  8.7 0.9 convolution_convert_fusion.7
  9.8 0.9 broadcast_in_dim.78
  10.7 10.2 %all-to-all-start = ((bf16[32,60,128]{2,1,0:T(8,128)(2,1)}), bf16[32,60,128]{2,1,0:T(8,128)(2,1)S(1)}, u32[]{:S(2)}, u32[]{:S(2)}) async-start(bf16[32,60,128]{2,1,0:T(8,128)(2,1)} %bitcast.3), calls=%async_computation | async-start | bytes 1048576 | tf_op jit(solution)/shard_map/all_to_all | solution.py:32
  20.9 17.1 %all-to-all-done = bf16[32,60,128]{2,1,0:T(8,128)(2,1)S(1)} async-done(((bf16[32,60,128]{2,1,0:T(8,128)(2,1)}), bf16[32,60,128]{2,1,0:T(8,128)(2,1)S(1)}, u32[]{:S(2)}, u32[]{:S(2)}) %all-to-all-start) | async-done | bytes 491552 | tf_op jit(solution)/shard_map/all_to_all | solution.py:32
  38.0 1.9 collective-permute-start
  43.1 2.2 convolution_convert_fusion.5
  46.4 0.9 broadcast_in_dim.83
  47.3 5.2 %all-to-all-start.1 = ((bf16[32,60,128]{2,1,0:T(8,128)(2,1)}), bf16[32,60,128]{2,1,0:T(8,128)(2,1)S(1)}, u32[]{:S(2)}, u32[]{:S(2)}) async-start(bf16[32,60,128]{2,1,0:T(8,128)(2,1)} %bitcast.4), calls=%async_computation.1 | async-start | bytes 1048576 | tf_op jit(solution)/shard_map/all_to_all | solution.py:32
  52.6 1.6 copy.38
  54.2 15.9 %all-to-all-done.1 = bf16[32,60,128]{2,1,0:T(8,128)(2,1)S(1)} async-done(((bf16[32,60,128]{2,1,0:T(8,128)(2,1)}), bf16[32,60,128]{2,1,0:T(8,128)(2,1)S(1)}, u32[]{:S(2)}, u32[]{:S(2)}) %all-to-all-start.1) | async-done | bytes 491552 | tf_op jit(solution)/shard_map/all_to_all | solution.py:32
  70.1 1.9 collective-permute-start.1
  75.2 1.9 convolution_convert_fusion.4
  77.1 35.0 %all_to_all.35 = bf16[8,80,512]{2,1,0:T(8,128)(2,1)S(1)} all-to-all(bf16[8,80,512]{2,1,0:T(8,128)(2,1)S(1)} %bitcast.38), channel_id=1, replica_groups=mesh['expert'=64,'fsdp'=8] {'fsdp'}, dimensions={0} | all-to-all | bytes 1310720 | tf_op jit(solution)/shard_map/all_to_all | solution.py:40
  112.2 0.9 convert_element_type.83
  114.0 0.9 broadcast_in_dim.84
  114.8 3.8 %all-to-all-start.3 = ((bf16[8,80,512]{2,1,0:T(8,128)(2,1)}), bf16[8,80,512]{2,1,0:T(8,128)(2,1)S(1)}, u32[]{:S(2)}, u32[]{:S(2)}) async-start(bf16[8,80,512]{2,1,0:T(8,128)(2,1)} %broadcast_in_dim.84), calls=%async_computation.3 | async-start | bytes 1310720 | tf_op jit(solution)/shard_map/all_to_all | solution.py:40
  118.8 22.3 %all-to-all-done.3 = bf16[8,80,512]{2,1,0:T(8,128)(2,1)S(1)} async-done(((bf16[8,80,512]{2,1,0:T(8,128)(2,1)}), bf16[8,80,512]{2,1,0:T(8,128)(2,1)S(1)}, u32[]{:S(2)}, u32[]{:S(2)}) %all-to-all-start.3) | async-done | bytes 655392 | tf_op jit(solution)/shard_map/all_to_all | solution.py:40
  142.6 1.9 collective-permute-start.2
  144.8 2.9 %convolution_convert_fusion.1 = bf16[512,768]{1,0:T(8,128)(2,1)} fusion(bf16[640,512]{1,0:T(8,128)(2,1)S(1)} %bitcast.37, bf16[640,768]{1,0:T(8,128)(2,1)} %constant_dynamic-update-slice_fusion.2), kind=kOutput, calls=%fused_computation.4 | convolution fusion | flops 503709696 | bytes 2424832 | tf_op jit(solution)/shard_map/dot_general | solution.py:13
  147.7 1.1 add_convert_fusion.2
  148.9 1.3 reshape.124
  150.1 7.7 %all-to-all-start.4 = ((bf16[32,60,128]{2,1,0:T(8,128)(2,1)}), bf16[32,60,128]{2,1,0:T(8,128)(2,1)S(1)}, u32[]{:S(2)}, u32[]{:S(2)}) async-start(bf16[32,60,128]{2,1,0:T(8,128)(2,1)} %reshape.124), calls=%async_computation.4 | async-start | bytes 1048576 | tf_op jit(solution)/shard_map/all_to_all | solution.py:32
  158.0 1.9 fusion.4
  160.7 1.9 collective-permute-start.3
  162.7 12.7 %all-to-all-done.4 = bf16[32,60,128]{2,1,0:T(8,128)(2,1)S(1)} async-done(((bf16[32,60,128]{2,1,0:T(8,128)(2,1)}), bf16[32,60,128]{2,1,0:T(8,128)(2,1)S(1)}, u32[]{:S(2)}, u32[]{:S(2)}) %all-to-all-start.4) | async-done | bytes 491552 | tf_op jit(solution)/shard_map/all_to_all | solution.py:32
  177.1 3.5 %all-to-all-start.6 = ((f32[8,16,2]{1,2,0:T(2,128)}), f32[8,16,2]{1,2,0:T(2,128)S(1)}, u32[]{:S(2)}, u32[]{:S(2)}) async-start(f32[8,16,2]{1,2,0:T(2,128)} %broadcast_in_dim.88), calls=%async_computation.6 | async-start | bytes 16384 | tf_op jit(solution)/shard_map/all_to_all | solution.py:40
  180.8 1.3 reshape.130
  182.1 6.1 %all-to-all-done.6 = f32[8,16,2]{1,2,0:T(2,128)S(1)} async-done(((f32[8,16,2]{1,2,0:T(2,128)}), f32[8,16,2]{1,2,0:T(2,128)S(1)}, u32[]{:S(2)}, u32[]{:S(2)}) %all-to-all-start.6) | async-done | bytes 1056 | tf_op jit(solution)/shard_map/all_to_all | solution.py:40
  188.1 5.5 %all-to-all-start.5 = ((bf16[32,60,128]{2,1,0:T(8,128)(2,1)}), bf16[32,60,128]{2,1,0:T(8,128)(2,1)S(1)}, u32[]{:S(2)}, u32[]{:S(2)}) async-start(bf16[32,60,128]{2,1,0:T(8,128)(2,1)} %reshape.130), calls=%async_computation.5 | async-start | bytes 1048576 | tf_op jit(solution)/shard_map/all_to_all | solution.py:32
  193.6 2.9 %convolution_convert_fusion.3 = bf16[768,512]{1,0:T(8,128)(2,1)} fusion(bf16[640,768]{1,0:T(8,128)(2,1)S(1)} %copy-done.7, bf16[640,1024]{1,0:T(8,128)(2,1)} %all-gather.2.cloned.1.call-done), kind=kOutput, calls=%fused_computation.6 | convolution fusion | flops 503709696 | bytes 2424832 | tf_op jit(solution)/shard_map/dot_general | solution.py:13
  196.5 1.7 convolution_convert_fusion.2
  199.7 9.4 %all-to-all-done.5 = bf16[32,60,128]{2,1,0:T(8,128)(2,1)S(1)} async-done(((bf16[32,60,128]{2,1,0:T(8,128)(2,1)}), bf16[32,60,128]{2,1,0:T(8,128)(2,1)S(1)}, u32[]{:S(2)}, u32[]{:S(2)}) %all-to-all-start.5) | async-done | bytes 491552 | tf_op jit(solution)/shard_map/all_to_all | solution.py:32
  (99 shorter events, 17.7 us)
Async XLA Ops:
  7.2 68.0 %copy-start = (bf16[512,768]{1,0:T(8,128)(2,1)S(1)}, bf16[512,768]{1,0:T(8,128)(2,1)}, u32[]{:S(2)}) copy-start(bf16[512,768]{1,0:T(8,128)(2,1)} %param.14) | copy-start | bytes 2359300
  7.2 32.8 %copy-start.9 = (s32[16,2]{0,1:T(2,128)S(1)}, s32[16,2]{0,1:T(2,128)}, u32[]{:S(2)}) copy-start(s32[16,2]{0,1:T(2,128)} %param.10) | copy-start | bytes 388
  7.2 13.6 %copy-start.10 = (f32[16,2]{0,1:T(2,128)S(1)}, f32[16,2]{0,1:T(2,128)}, u32[]{:S(2)}) copy-start(f32[16,2]{0,1:T(2,128)} %param.11) | copy-start | bytes 388
  7.2 33.1 %copy-start.8 = (bf16[16,768]{1,0:T(8,128)(2,1)S(1)}, bf16[16,768]{1,0:T(8,128)(2,1)}, u32[]{:S(2)}) copy-start(bf16[16,768]{1,0:T(8,128)(2,1)} %param.15) | copy-start | bytes 73732
  10.7 27.4 %all-to-all-start = ((bf16[32,60,128]{2,1,0:T(8,128)(2,1)}), bf16[32,60,128]{2,1,0:T(8,128)(2,1)S(1)}, u32[]{:S(2)}, u32[]{:S(2)}) async-start(bf16[32,60,128]{2,1,0:T(8,128)(2,1)} %bitcast.3), calls=%async_computation | async-start | bytes 1048576 | tf_op jit(solution)/shard_map/all_to_all | solution.py:32
  38.0 3.8 %collective-permute-start = (bf16[32,60,128]{2,1,0:T(8,128)(2,1)S(1)}, bf16[32,60,128]{2,1,0:T(8,128)(2,1)S(1)}, u32[]{:S(2)}, u32[]{:S(2)}) collective-permute-start(bf16[32,60,128]{2,1,0:T(8,128)(2,1)S(1)} %all-to-all-done), channel_id=1, source_target_pairs={{0,8},{8,0},{16,24},{24,16},{32,40},{40,32},{48,56},{56,48},{64,72... | collective-permute-start | bytes 1474568 | tf_op jit(solution)/shard_map/ppermute | solution.py:37
  41.0 2.2 copy-start.4
  43.1 2.2 %copy-start.3 = (bf16[768,512]{1,0:T(8,128)(2,1)S(1)}, bf16[768,512]{1,0:T(8,128)(2,1)}, u32[]{:S(2)}) copy-start(bf16[768,512]{1,0:T(8,128)(2,1)} %param.12) | copy-start | bytes 2359300
  43.1 2.2 %copy-start.6 = (bf16[640,768]{1,0:T(8,128)(2,1)S(1)}, bf16[640,768]{1,0:T(8,128)(2,1)}, u32[]{:S(2)}) copy-start(bf16[640,768]{1,0:T(8,128)(2,1)} %constant_dynamic-update-slice_fusion) | copy-start | bytes 2949124
  47.3 22.8 %all-to-all-start.1 = ((bf16[32,60,128]{2,1,0:T(8,128)(2,1)}), bf16[32,60,128]{2,1,0:T(8,128)(2,1)S(1)}, u32[]{:S(2)}, u32[]{:S(2)}) async-start(bf16[32,60,128]{2,1,0:T(8,128)(2,1)} %bitcast.4), calls=%async_computation.1 | async-start | bytes 1048576 | tf_op jit(solution)/shard_map/all_to_all | solution.py:32
  52.5 59.7 %reduce-scatter.4.cloned.1.call-start = ((), (), s32[]{:S(2)}) async-start(), calls=%async_computation.9 | async-start | bytes 1474560 | tf_op jit(solution)/shard_map/reduce_scatter | solution.py:96
  54.1 103.9 %all-gather.2.cloned.1.call-start = ((), (), s32[]{:S(2)}) async-start(), calls=%async_computation.8 | async-start | bytes 1474560 | tf_op jit(solution)/shard_map/all_gather | solution.py:107
  70.1 3.8 %collective-permute-start.1 = (bf16[32,60,128]{2,1,0:T(8,128)(2,1)S(1)}, bf16[32,60,128]{2,1,0:T(8,128)(2,1)S(1)}, u32[]{:S(2)}, u32[]{:S(2)}) collective-permute-start(bf16[32,60,128]{2,1,0:T(8,128)(2,1)S(1)} %all-to-all-done.1), channel_id=1, source_target_pairs={{0,8},{8,0},{16,24},{24,16},{32,40},{40,32},{48,56},{56,48},{64,72... | collective-permute-start | bytes 1474568 | tf_op jit(solution)/shard_map/ppermute | solution.py:37
  114.8 26.2 %all-to-all-start.3 = ((bf16[8,80,512]{2,1,0:T(8,128)(2,1)}), bf16[8,80,512]{2,1,0:T(8,128)(2,1)S(1)}, u32[]{:S(2)}, u32[]{:S(2)}) async-start(bf16[8,80,512]{2,1,0:T(8,128)(2,1)} %broadcast_in_dim.84), calls=%async_computation.3 | async-start | bytes 1310720 | tf_op jit(solution)/shard_map/all_to_all | solution.py:40
  142.6 5.1 %collective-permute-start.2 = (bf16[320,768]{1,0:T(8,128)(2,1)}, bf16[320,768]{1,0:T(8,128)(2,1)}, u32[]{:S(2)}, u32[]{:S(2)}) collective-permute-start(bf16[320,768]{1,0:T(8,128)(2,1)} %slice.55), channel_id=1, source_target_pairs={{0,8},{8,0},{16,24},{24,16},{32,40},{40,32},{48,56},{56,48},{64,72... | collective-permute-start | bytes 1474568 | tf_op jit(solution)/shard_map/ppermute | solution.py:37
  150.1 25.3 %all-to-all-start.4 = ((bf16[32,60,128]{2,1,0:T(8,128)(2,1)}), bf16[32,60,128]{2,1,0:T(8,128)(2,1)S(1)}, u32[]{:S(2)}, u32[]{:S(2)}) async-start(bf16[32,60,128]{2,1,0:T(8,128)(2,1)} %reshape.124), calls=%async_computation.4 | async-start | bytes 1048576 | tf_op jit(solution)/shard_map/all_to_all | solution.py:32
  158.0 2.0 copy-start.1
  158.0 2.0 copy-start.5
  160.7 19.9 %collective-permute-start.3 = (bf16[320,768]{1,0:T(8,128)(2,1)S(1)}, bf16[320,768]{1,0:T(8,128)(2,1)S(1)}, u32[]{:S(2)}, u32[]{:S(2)}) collective-permute-start(bf16[320,768]{1,0:T(8,128)(2,1)S(1)} %slice.57), channel_id=1, source_target_pairs={{0,8},{8,0},{16,24},{24,16},{32,40},{40,32},{48,56},{56,48},{64,72... | collective-permute-start | bytes 1474568 | tf_op jit(solution)/shard_map/ppermute | solution.py:37
  177.1 11.0 %all-to-all-start.6 = ((f32[8,16,2]{1,2,0:T(2,128)}), f32[8,16,2]{1,2,0:T(2,128)S(1)}, u32[]{:S(2)}, u32[]{:S(2)}) async-start(f32[8,16,2]{1,2,0:T(2,128)} %broadcast_in_dim.88), calls=%async_computation.6 | async-start | bytes 16384 | tf_op jit(solution)/shard_map/all_to_all | solution.py:40
  180.8 12.8 %copy-start.7 = (bf16[640,768]{1,0:T(8,128)(2,1)S(1)}, bf16[640,768]{1,0:T(8,128)(2,1)}, u32[]{:S(2)}) copy-start(bf16[640,768]{1,0:T(8,128)(2,1)} %constant_dynamic-update-slice_fusion) | copy-start | bytes 2949124
  188.1 21.0 %all-to-all-start.5 = ((bf16[32,60,128]{2,1,0:T(8,128)(2,1)}), bf16[32,60,128]{2,1,0:T(8,128)(2,1)S(1)}, u32[]{:S(2)}, u32[]{:S(2)}) async-start(bf16[32,60,128]{2,1,0:T(8,128)(2,1)} %reshape.130), calls=%async_computation.5 | async-start | bytes 1048576 | tf_op jit(solution)/shard_map/all_to_all | solution.py:32
  193.6 2.9 %copy-start.2 = (bf16[640,1024]{1,0:T(8,128)(2,1)S(1)}, bf16[640,1024]{1,0:T(8,128)(2,1)}, u32[]{:S(2)}) copy-start(bf16[640,1024]{1,0:T(8,128)(2,1)} %all-gather.2.cloned.1.call-done) | copy-start | bytes 3932164
Sparse Core Ops, SparseCore 0:
  56.2 54.9 reduce-scatter.3
  114.1 43.8 all-gather.1

commit v3 on v1

v3 whole, which is shorter than its diff:
```python
import jax
import jax.numpy as jnp
from jax import lax
from jax.sharding import PartitionSpec as P

EXPERTS = 4
MOST = 10
CORES = 2
LANES = 128


def contract(left, right, left_dim, right_dim):
    return lax.dot_general(
        left, right, (((left_dim,), (right_dim,)), ((), ())), preferred_element_type=jnp.float32
    )


def on_device(tokens, expert_ids, route_logits, w_gate, w_up, w_down, out_grad):
    count, width = tokens.shape
    hidden_width = w_gate.shape[1]
    peers = lax.axis_size("expert")
    planes = lax.axis_size("fsdp")
    group = peers // EXPERTS
    chips = group // CORES
    half = peers // CORES * MOST
    rows = CORES * half
    own = rows // planes
    matching = [[group * e + i for e in range(EXPERTS)] for i in range(group)]
    same_core = [
        [group * e + CORES * p + c for p in range(chips)]
        for e in range(EXPERTS)
        for c in range(CORES)
    ]
    other_core = [(i, i ^ 1) for i in range(peers)]

    def across(blocks, groups):
        return lax.all_to_all(
            blocks, "expert", split_axis=0, concat_axis=0, axis_index_groups=groups, tiled=True
        )

    def swap(value):
        return lax.ppermute(value, "expert", other_core)

    experts = jnp.arange(EXPERTS, dtype=jnp.int32)
    named = expert_ids[:, :, None] == experts[None, None, :]
    chosen = jnp.any(named, axis=1)
    before = jnp.arange(count)[:, None, None] < jnp.arange(count)[None, :, None]
    rank = jnp.sum((before & chosen[:, None, :]).astype(jnp.int32), axis=0)
    first = jax.nn.sigmoid(route_logits[:, 0] - route_logits[:, 1])
    route_weight = jnp.stack([first, 1.0 - first], axis=1)
    scale = jnp.sum(jnp.where(named, route_weight[:, :, None], 0.0), axis=1)
    slots = jnp.arange(MOST, dtype=jnp.int32)
    picked = (chosen.T[:, None, :]) & (rank.T[:, None, :] == slots[None, :, None])
    select = picked.reshape(EXPERTS * MOST, count)
    slot_scale = jnp.sum(
        jnp.where(picked, scale.T[:, None, :], 0.0), axis=2
    ).reshape(EXPERTS * MOST, 1)
    token_slots = contract(select.astype(jnp.bfloat16), tokens, 1, 0).astype(jnp.bfloat16)
    cot_slots = (slot_scale * contract(select.astype(jnp.bfloat16), out_grad, 1, 0)).astype(
        jnp.bfloat16
    )

    def gather_rows(slot_rows):
        mine = across(slot_rows.reshape(EXPERTS, -1, LANES), matching)
        copies = jnp.broadcast_to(mine.reshape(1, -1, LANES), (chips, mine.size // LANES, LANES))
        arrived = across(copies, same_core)
        return jnp.concatenate(
            [arrived.reshape(half, -1), swap(arrived).reshape(half, -1)], axis=0
        )

    def shift(value, by):
        pairs = [(i, (i + by) % planes) for i in range(planes)]
        return lax.ppermute(value, "fsdp", pairs)

    def shift_by_core(value, by):
        pairs = []
        for e in range(peers):
            for z in range(planes):
                there = (z + by) % planes if e % CORES == 0 else (z - by) % planes
                pairs.append((e * planes + z, e * planes + there))
        return lax.ppermute(value, ("expert", "fsdp"), pairs)

    me = lax.axis_index("expert")
    plane = lax.axis_index("fsdp")
    even_core = me % CORES == 0

    def plane_sum(parts):
        chunks = parts.reshape(planes, own, -1)

        def chunk(ahead):
            at = (plane + ahead + planes) % planes
            return lax.dynamic_slice_in_dim(chunks, at, 1, axis=0)[0]

        def wide(value):
            return value.astype(jnp.float32)

        up_three = shift(chunk(3), 1)
        down_three = shift(chunk(-3), -1)
        four = wide(shift_by_core(chunk(4), 2))
        up_one = shift(chunk(1), 1)
        down_one = shift(chunk(-1), -1)
        up_two = wide(chunk(2)) + wide(up_three) + jnp.where(even_core, four, 0.0)
        down_two = wide(chunk(-2)) + wide(down_three) + jnp.where(even_core, 0.0, four)
        up_two = shift(up_two.astype(jnp.bfloat16), 2)
        down_two = shift(down_two.astype(jnp.bfloat16), -2)
        near = wide(chunk(0)) + wide(up_one) + wide(down_one)
        return near + wide(up_two) + wide(down_two)

    def to_all_planes(value):
        next_two, last_two = shift(value, -2), shift(value, 2)
        next_one, last_one = shift(value, -1), shift(value, 1)
        four = shift_by_core(jnp.where(even_core, next_two, last_two), -2)
        next_three, last_three = shift(next_two, -1), shift(last_two, 1)
        chunks = jnp.zeros((planes,) + value.shape, value.dtype)
        order = [value, next_one, next_two, next_three, four, last_three, last_two, last_one]
        for ahead, piece in enumerate(order):
            at = (plane + ahead) % planes
            chunks = lax.dynamic_update_slice_in_dim(chunks, piece[None], at, axis=0)
        return chunks.reshape(rows, -1)

    def two_columns(product):
        near = lax.reduce_precision(product, 8, 7)
        far = product - near
        both = jnp.stack([near, far], axis=1).astype(jnp.bfloat16)
        return jnp.pad(both, ((0, 0), (0, LANES - 2)))

    def narrow(summed):
        product = summed[:, -LANES] + summed[:, 1 - LANES]
        return jnp.concatenate(
            [summed[:, :-LANES].astype(jnp.bfloat16), two_columns(product)], axis=1
        )

    def give_back(part):
        mine = narrow(part[:half].astype(jnp.float32) + swap(part[half:]).astype(jnp.float32))
        arrived = across(mine.reshape(chips, -1, LANES), same_core)
        summed = arrived.astype(jnp.float32).sum(axis=0).reshape(EXPERTS * MOST, -1)
        back = across(narrow(summed).reshape(EXPERTS, -1, LANES), matching)
        return back.reshape(EXPERTS * MOST, -1).astype(jnp.float32)

    experts = jnp.arange(EXPERTS, dtype=jnp.int32)
    named = expert_ids[:, :, None] == experts[None, None, :]
    chosen = jnp.any(named, axis=1)
    before = jnp.arange(count)[:, None, None] < jnp.arange(count)[None, :, None]
    rank = jnp.sum((before & chosen[:, None, :]).astype(jnp.int32), axis=0)
    first = jax.nn.sigmoid(route_logits[:, 0] - route_logits[:, 1])
    route_weight = jnp.stack([first, 1.0 - first], axis=1)
    scale = jnp.sum(jnp.where(named, route_weight[:, :, None], 0.0), axis=1)
    slots = jnp.arange(MOST, dtype=jnp.int32)
    picked = (chosen.T[:, None, :]) & (rank.T[:, None, :] == slots[None, :, None])
    select = picked.reshape(EXPERTS * MOST, count)
    slot_scale = jnp.sum(
        jnp.where(picked, scale.T[:, None, :], 0.0), axis=2
    ).reshape(EXPERTS * MOST, 1)
    token_slots = contract(select.astype(jnp.bfloat16), tokens, 1, 0).astype(jnp.bfloat16)
    cot_slots = (slot_scale * contract(select.astype(jnp.bfloat16), out_grad, 1, 0)).astype(
        jnp.bfloat16
    )

    def gather_rows(slot_rows):
        mine = across(slot_rows.reshape(EXPERTS, -1, LANES), matching)
        copies = jnp.broadcast_to(mine.reshape(1, -1, LANES), (chips, mine.size // LANES, LANES))
        arrived = across(copies, same_core)
        return jnp.concatenate(
            [arrived.reshape(half, -1), swap(arrived).reshape(half, -1)], axis=0
        )

    def give_back(part):
        mine = part[:half].astype(jnp.float32) + swap(part[half:]).astype(jnp.float32)
        sent = mine.astype(jnp.bfloat16).reshape(chips, -1, LANES)
        summed = across(sent, same_core).astype(jnp.float32).sum(axis=0).astype(jnp.bfloat16)
        back = across(summed.reshape(EXPERTS, -1, LANES), matching)
        return back.reshape(EXPERTS * MOST, -1).astype(jnp.float32)

    both = gather_rows(jnp.concatenate([token_slots, cot_slots], axis=1))
    arrived, arrived_cot = both[:, :width], both[:, width:]
    parts = jnp.concatenate(
        [
            jnp.dot(arrived, w_gate, preferred_element_type=jnp.float32).astype(jnp.bfloat16),
            jnp.dot(arrived, w_up, preferred_element_type=jnp.float32).astype(jnp.bfloat16),
            contract(arrived_cot, w_down, 1, 1).astype(jnp.bfloat16),
        ],
        axis=1,
    )
    sums = plane_sum(parts)
    gate = sums[:, :hidden_width]
    upper = sums[:, hidden_width : 2 * hidden_width]
    hidden_cot = sums[:, 2 * hidden_width :]
    sig = jax.nn.sigmoid(gate)
    hidden_own = (gate * sig * upper).astype(jnp.bfloat16)
    gate_cot_own = (hidden_cot * upper * sig * (1.0 + gate * (1.0 - sig))).astype(jnp.bfloat16)
    up_cot_own = (hidden_cot * gate * sig).astype(jnp.bfloat16)
    product = jnp.sum(hidden_own.astype(jnp.float32) * hidden_cot, axis=1)
    gathered = to_all_planes(
        jnp.concatenate([hidden_own, gate_cot_own, up_cot_own, two_columns(product)], axis=1)
    )
    hidden = gathered[:, :hidden_width]
    gate_cot = gathered[:, hidden_width : 2 * hidden_width]
    up_cot = gathered[:, 2 * hidden_width : 3 * hidden_width]

    tokens_part = contract(gate_cot, w_gate, 1, 1) + contract(up_cot, w_up, 1, 1)
    out_part = jnp.dot(hidden, w_down, preferred_element_type=jnp.float32)
    back = give_back(
        jnp.concatenate(
            [
                out_part.astype(jnp.bfloat16),
                tokens_part.astype(jnp.bfloat16),
                gathered[:, 3 * hidden_width :],
            ],
            axis=1,
        )
    )
    out_slots, grad_slots = back[:, :width], back[:, width : 2 * width]
    slot_products = back[:, 2 * width] + back[:, 2 * width + 1]
    down_grad = contract(hidden, arrived_cot, 0, 0).astype(jnp.bfloat16)
    gate_grad = contract(arrived, gate_cot, 0, 0).astype(jnp.bfloat16)
    up_grad = contract(arrived, up_cot, 0, 0).astype(jnp.bfloat16)

    rank_of_route = jnp.sum(jnp.where(named, rank[:, None, :], 0), axis=2)
    place = expert_ids * MOST + rank_of_route
    route_product = jnp.sum(
        jnp.where(
            place[:, :, None] == jnp.arange(EXPERTS * MOST)[None, None, :], slot_products, 0.0
        ),
        axis=2,
    )
    route_out = jnp.take(out_slots, place.reshape(-1), axis=0).reshape(count, -1, width)
    layer_out = jnp.sum(route_weight[:, :, None] * route_out, axis=1).astype(jnp.bfloat16)
    route_grad = jnp.take(grad_slots, place.reshape(-1), axis=0).reshape(count, -1, width)
    tokens_grad = jnp.sum(route_grad, axis=1).astype(jnp.bfloat16)
    change = route_product[:, 0] * route_weight[:, 1] - route_product[:, 1] * route_weight[:, 0]
    logits_grad = jnp.stack([change, -change], axis=1)
    return (layer_out, tokens_grad, gate_grad, up_grad, down_grad, logits_grad)


def solution(mesh):
    return jax.shard_map(
        on_device,
        mesh=mesh,
        in_specs=(
            P("expert", "fsdp"),
            P("expert", None),
            P("expert", None),
            P("fsdp", "expert"),
            P("fsdp", "expert"),
            P("expert", "fsdp"),
            P("expert", "fsdp"),
        ),
        out_specs=(
            P("expert", "fsdp"),
            P("expert", "fsdp"),
            P("fsdp", "expert"),
            P("fsdp", "expert"),
            P("expert", "fsdp"),
            P("expert", None),
        ),
        check_vma=False,
    )
```

time: 272 us -> 194 us (0.71)
  blocking collectives: 185 us -> 32.1 us
  starting transfers between devices: 18.1 us -> 67.4 us
  waiting for transfers between devices: 31.7 us -> 45.1 us
  other arithmetic: 6.27 us -> 13.5 us
  local copies, waits for them, and re-layouts: 14.2 us -> 18.1 us
    all_to_all x7 -> x2, blocking collectives: 185 us -> 32.1 us  [across(): lax.all_to_all(blocks, 'expert', split_axis=0, concat_axis=0, axis_index_...]
    ppermute x0 -> x14, starting transfers between devices: none -> 54.7 us  [the longest x12 43.3 us: shift(): return lax.ppermute(value, 'fsdp', pairs)]
    ppermute x0 -> x14, waiting for transfers between devices: none -> 26.1 us  [the longest x12 23.7 us: shift(): return lax.ppermute(value, 'fsdp', pairs)]
    all_to_all x2, waiting for transfers between devices: 27.7 us -> 15.8 us  [across(): lax.all_to_all(blocks, 'expert', split_axis=0, concat_axis=0, axis_index_...]
    ppermute x4 -> x2, starting transfers between devices: 7.83 us -> 3.83 us  [swap(): return lax.ppermute(value, 'expert', other_core)]
    reshape x13 -> x8, local copies, waits for them, and re-layouts: 5.9 us -> 7.45 us  [the longest x1 3.08 us: give_back(): sent = mine.astype(jnp.bfloat16).reshape(chips, -1, LANES)]
  transfers between devices with their start and end apart: 6 -> 18, of which waited for: 6 -> 11; matrix products, arithmetic and copies ran while one was open for 4% -> 7% of each run, Pallas kernels for 0% -> 0%
where the time goes in v3:
time: 194 us; the launch traced here: 193 us
  starting transfers between devices  67.4 us (35%)
  waiting for transfers between devices  45.1 us (23%)
  blocking collectives  32.1 us (17%)
  local copies, waits for them, and re-layouts  18.1 us (9%)
  matrix products  15.5 us (8%)
  other arithmetic  13.5 us (7%)
    ppermute x12, starting transfers between devices, shift(): return lax.ppermute(value, 'fsdp', pairs)  43.3 us
    all_to_all x2, blocking collectives, across(): lax.all_to_all(blocks, 'expert', split_axis=0, concat_axis=0, axis_index_...  32.1 us
    ppermute x12, waiting for transfers between devices, shift(): return lax.ppermute(value, 'fsdp', pairs)  23.7 us
    all_to_all x2, waiting for transfers between devices, across(): lax.all_to_all(blocks, 'expert', split_axis=0, concat_axis=0, axis_index_...  15.8 us
    dot_general x8, matrix products, contract(): lax.dot_general(left, right, (((left_dim,), (right_dim,)), ((), ())), pre...  13.1 us
    ppermute x2, starting transfers between devices, shift_by_core(): return lax.ppermute(value, ('expert', 'fsdp'), pairs)  11.4 us
    all_to_all x2, starting transfers between devices, across(): lax.all_to_all(blocks, 'expert', split_axis=0, concat_axis=0, axis_index_...  8.9 us
  transfers between devices with their start and end apart: 18, of which 11 were waited for; matrix products, arithmetic and copies ran while one was open for 7% of the time, Pallas kernels for 0%

profile of v3, /device:TPU:8, one launch (start us, length us, event | category | flops | bytes accessed | tf_op | source)
XLA Modules:
  0.0 193.1 jit_solution(7757644604566754578)
XLA Ops:
  6.0 14.4 %all_to_all.20 = bf16[4,120,128]{2,1,0:T(8,128)(2,1)S(1)} all-to-all(bf16[4,120,128]{2,1,0:T(8,128)(2,1)S(1)} %reshape.103), channel_id=1, replica_groups={{0,128,256,384},{8,136,264,392},{16,144,272,400},{24,152,280,408},{32,1..., dimensions={0} | all-to-all | bytes 245760 | tf_op jit(solution)/shard_map/all_to_all | solution.py:37
  20.5 17.8 %all_to_all.21 = bf16[8,480,128]{2,1,0:T(8,128)(2,1)S(1)} all-to-all(bf16[8,480,128]{2,1,0:T(8,128)(2,1)S(1)} %broadcast_in_dim.113), channel_id=1, replica_groups={{0,16,32,48,64,80,96,112},{8,24,40,56,72,88,104,120},{128,144,160,176,1..., dimensions={0} | all-to-all | bytes 1966080 | tf_op jit(solution)/shard_map/all_to_all | solution.py:37
  42.8 2.2 %reshape.105 = bf16[320,1536]{1,0:T(8,128)(2,1)S(1)} reshape(bf16[8,480,128]{2,1,0:T(8,128)(2,1)} %collective-permute-done) | data formatting | bytes 1966080 | tf_op jit(solution)/shard_map/reshape | solution.py:164
  46.1 2.2 %convolution_convert_fusion.4 = bf16[640,512]{0,1:T(8,128)(2,1)S(1)} fusion(bf16[512,768]{1,0:T(8,128)(2,1)S(1)} %copy-done.14, bf16[640,1536]{1,0:T(8,128)(2,1)} %constant_dynamic-update-slice_fusion), kind=kOutput, calls=%fused_computation.10 | convolution fusion | flops 503644160 | bytes 2424832 | tf_op jit(solution)/shard_map/dot_general | solution.py:13
  51.7 2.7 %copy.50 = bf16[640,1536]{1,0:T(8,128)(2,1)S(1)} copy(bf16[640,1536]{0,1:T(8,128)(2,1)} %pad_maximum_fusion.1) | data formatting | bytes 3932160 | tf_op jit(solution)/shard_map/concatenate | solution.py:176
  55.4 4.3 %collective-permute-start.3 = (bf16[80,1536]{1,0:T(8,128)(2,1)}, bf16[80,1536]{1,0:T(8,128)(2,1)}, u32[]{:S(2)}, u32[]{:S(2)}) collective-permute-start(bf16[80,1536]{1,0:T(8,128)(2,1)} %get-tuple-element.18), channel_id=1, source_target_pairs={{0,1},{1,2},{2,3},{3,4},{4,5},{5,6},{6,7},{7,0},{8,9},{9,10},{10,1... | collective-permute-start | bytes 737288 | tf_op jit(solution)/shard_map/ppermute | solution.py:73
  59.7 6.1 %collective-permute-start.4 = (bf16[80,1536]{1,0:T(8,128)(2,1)}, bf16[80,1536]{1,0:T(8,128)(2,1)}, u32[]{:S(2)}, u32[]{:S(2)}) collective-permute-start(bf16[80,1536]{1,0:T(8,128)(2,1)} %get-tuple-element.17), channel_id=1, source_target_pairs={{0,2},{1,3},{2,4},{3,5},{4,6},{5,7},{6,0},{7,1},{8,14},{9,15},{10,... | collective-permute-start | bytes 737288 | tf_op jit(solution)/shard_map/ppermute | solution.py:81
  65.8 4.4 %collective-permute-start.6 = (bf16[80,1536]{1,0:T(8,128)(2,1)S(1)}, bf16[80,1536]{1,0:T(8,128)(2,1)}, u32[]{:S(2)}, u32[]{:S(2)}) collective-permute-start(bf16[80,1536]{1,0:T(8,128)(2,1)S(1)} %get-tuple-element.16), channel_id=1, source_target_pairs={{0,7},{1,0},{2,1},{3,2},{4,3},{5,4},{6,5},{7,6},{8,15},{9,8},{10,9... | collective-permute-start | bytes 737288 | tf_op jit(solution)/shard_map/ppermute | solution.py:73
  70.2 3.0 %collective-permute-start.1 = (bf16[80,1536]{1,0:T(8,128)(2,1)}, bf16[80,1536]{1,0:T(8,128)(2,1)S(1)}, u32[]{:S(2)}, u32[]{:S(2)}) collective-permute-start(bf16[80,1536]{1,0:T(8,128)(2,1)} %get-tuple-element.15), channel_id=1, source_target_pairs={{0,1},{1,2},{2,3},{3,4},{4,5},{5,6},{6,7},{7,0},{8,9},{9,10},{10,1... | collective-permute-start | bytes 737288 | tf_op jit(solution)/shard_map/ppermute | solution.py:73
  73.2 4.1 %collective-permute-start.2 = (bf16[80,1536]{1,0:T(8,128)(2,1)}, bf16[80,1536]{1,0:T(8,128)(2,1)S(1)}, u32[]{:S(2)}, u32[]{:S(2)}) collective-permute-start(bf16[80,1536]{1,0:T(8,128)(2,1)} %get-tuple-element.19), channel_id=1, source_target_pairs={{0,7},{1,0},{2,1},{3,2},{4,3},{5,4},{6,5},{7,6},{8,15},{9,8},{10,9... | collective-permute-start | bytes 737288 | tf_op jit(solution)/shard_map/ppermute | solution.py:73
  77.3 2.4 %collective-permute-done.4 = bf16[80,1536]{1,0:T(8,128)(2,1)} collective-permute-done((bf16[80,1536]{1,0:T(8,128)(2,1)}, bf16[80,1536]{1,0:T(8,128)(2,1)}, u32[]{:S(2)}, u32[]{:S(2)}) %collective-permute-start.4) | collective-permute-done | bytes 245792 | tf_op jit(solution)/shard_map/ppermute | solution.py:81
  79.8 2.1 %fusion.16 = (bf16[80,1536]{1,0:T(8,128)(2,1)}, bf16[80,1536]{1,0:T(8,128)(2,1)}) fusion(bf16[80,1536]{1,0:T(8,128)(2,1)} %collective-permute-done.4, bf16[80,1536]{1,0:T(8,128)(2,1)} %collective-permute-done.3, bf16[8,80,1536]{2,1,0:T(8,128)(2,1)S(1)} %bitcast.59, s32[]{:T(128)S(6)} %select_n.161, pred[]{:T(512)S(6)} %eq.82, ...), kind=kLoop, calls=%fused_computation.34 | loop fusion | flops 1597440 | bytes 1720329 | tf_op jit(solution)/shard_map/convert_element_type | solution.py:104
  81.9 3.3 %collective-permute-start.5 = (bf16[80,1536]{1,0:T(8,128)(2,1)}, bf16[80,1536]{1,0:T(8,128)(2,1)S(1)}, u32[]{:S(2)}, u32[]{:S(2)}) collective-permute-start(bf16[80,1536]{1,0:T(8,128)(2,1)} %get-tuple-element.13), channel_id=1, source_target_pairs={{0,2},{1,3},{2,4},{3,5},{4,6},{5,7},{6,0},{7,1},{8,10},{9,11},{10,... | collective-permute-start | bytes 737288 | tf_op jit(solution)/shard_map/ppermute | solution.py:73
  85.2 4.7 %collective-permute-start.7 = (bf16[80,1536]{1,0:T(8,128)(2,1)}, bf16[80,1536]{1,0:T(8,128)(2,1)}, u32[]{:S(2)}, u32[]{:S(2)}) collective-permute-start(bf16[80,1536]{1,0:T(8,128)(2,1)} %get-tuple-element.14), channel_id=1, source_target_pairs={{0,6},{1,7},{2,0},{3,1},{4,2},{5,3},{6,4},{7,5},{8,14},{9,15},{10,... | collective-permute-start | bytes 737288 | tf_op jit(solution)/shard_map/ppermute | solution.py:73
  89.9 8.4 %collective-permute-done.5 = bf16[80,1536]{1,0:T(8,128)(2,1)S(1)} collective-permute-done((bf16[80,1536]{1,0:T(8,128)(2,1)}, bf16[80,1536]{1,0:T(8,128)(2,1)S(1)}, u32[]{:S(2)}, u32[]{:S(2)}) %collective-permute-start.5) | collective-permute-done | bytes 245792 | tf_op jit(solution)/shard_map/ppermute | solution.py:73
  98.3 3.9 %collective-permute-done.7 = bf16[80,1536]{1,0:T(8,128)(2,1)} collective-permute-done((bf16[80,1536]{1,0:T(8,128)(2,1)}, bf16[80,1536]{1,0:T(8,128)(2,1)}, u32[]{:S(2)}, u32[]{:S(2)}) %collective-permute-start.7) | collective-permute-done | bytes 245792 | tf_op jit(solution)/shard_map/ppermute | solution.py:73
  104.4 5.3 %collective-permute-start.11 = (bf16[80,1664]{1,0:T(8,128)(2,1)}, bf16[80,1664]{1,0:T(8,128)(2,1)S(1)}, u32[]{:S(2)}, u32[]{:S(2)}) collective-permute-start(bf16[80,1664]{1,0:T(8,128)(2,1)} %fusion.22), channel_id=1, source_target_pairs={{0,2},{1,3},{2,4},{3,5},{4,6},{5,7},{6,0},{7,1},{8,10},{9,11},{10,... | collective-permute-start | bytes 798728 | tf_op jit(solution)/shard_map/ppermute | solution.py:73
  109.7 2.6 %collective-permute-start.9 = (bf16[80,1664]{1,0:T(8,128)(2,1)}, bf16[80,1664]{1,0:T(8,128)(2,1)S(1)}, u32[]{:S(2)}, u32[]{:S(2)}) collective-permute-start(bf16[80,1664]{1,0:T(8,128)(2,1)} %fusion.22), channel_id=1, source_target_pairs={{0,6},{1,7},{2,0},{3,1},{4,2},{5,3},{6,4},{7,5},{8,14},{9,15},{10,... | collective-permute-start | bytes 798728 | tf_op jit(solution)/shard_map/ppermute | solution.py:73
  114.4 3.9 %collective-permute-start.14 = (bf16[80,1664]{1,0:T(8,128)(2,1)}, bf16[80,1664]{1,0:T(8,128)(2,1)S(1)}, u32[]{:S(2)}, u32[]{:S(2)}) collective-permute-start(bf16[80,1664]{1,0:T(8,128)(2,1)} %fusion.22), channel_id=1, source_target_pairs={{0,1},{1,2},{2,3},{3,4},{4,5},{5,6},{6,7},{7,0},{8,9},{9,10},{10,1... | collective-permute-start | bytes 798728 | tf_op jit(solution)/shard_map/ppermute | solution.py:73
  119.2 2.0 %collective-permute-done.11 = bf16[80,1664]{1,0:T(8,128)(2,1)S(1)} collective-permute-done((bf16[80,1664]{1,0:T(8,128)(2,1)}, bf16[80,1664]{1,0:T(8,128)(2,1)S(1)}, u32[]{:S(2)}, u32[]{:S(2)}) %collective-permute-start.11) | collective-permute-done | bytes 266272 | tf_op jit(solution)/shard_map/ppermute | solution.py:73
  121.2 2.9 %collective-permute-done.9 = bf16[80,1664]{1,0:T(8,128)(2,1)S(1)} collective-permute-done((bf16[80,1664]{1,0:T(8,128)(2,1)}, bf16[80,1664]{1,0:T(8,128)(2,1)S(1)}, u32[]{:S(2)}, u32[]{:S(2)}) %collective-permute-start.9) | collective-permute-done | bytes 266272 | tf_op jit(solution)/shard_map/ppermute | solution.py:73
  124.1 5.3 %collective-permute-start.12 = (bf16[80,1664]{1,0:T(8,128)(2,1)S(1)}, bf16[80,1664]{1,0:T(8,128)(2,1)S(1)}, u32[]{:S(2)}, u32[]{:S(2)}) collective-permute-start(bf16[80,1664]{1,0:T(8,128)(2,1)S(1)} %broadcast_select_fusion), channel_id=1, source_target_pairs={{0,6},{1,7},{2,0},{3,1},{4,2},{5,3},{6,4},{7,5},{8,10},{9,11},{10,... | collective-permute-start | bytes 798728 | tf_op jit(solution)/shard_map/ppermute | solution.py:81
  131.3 3.9 %collective-permute-start.13 = (bf16[80,1664]{1,0:T(8,128)(2,1)S(1)}, bf16[80,1664]{1,0:T(8,128)(2,1)S(1)}, u32[]{:S(2)}, u32[]{:S(2)}) collective-permute-start(bf16[80,1664]{1,0:T(8,128)(2,1)S(1)} %collective-permute-done.11), channel_id=1, source_target_pairs={{0,1},{1,2},{2,3},{3,4},{4,5},{5,6},{6,7},{7,0},{8,9},{9,10},{10,1... | collective-permute-start | bytes 798728 | tf_op jit(solution)/shard_map/ppermute | solution.py:73
  135.3 6.0 %collective-permute-done.10 = bf16[80,1664]{1,0:T(8,128)(2,1)S(1)} collective-permute-done((bf16[80,1664]{1,0:T(8,128)(2,1)S(1)}, bf16[80,1664]{1,0:T(8,128)(2,1)S(1)}, u32[]{:S(2)}, u32[]{:S(2)}) %collective-permute-start.10) | collective-permute-done | bytes 266272 | tf_op jit(solution)/shard_map/ppermute | solution.py:73
  147.2 2.6 %collective-permute-done.15 = bf16[320,1664]{1,0:T(8,128)(2,1)S(1)} collective-permute-done((bf16[320,1664]{1,0:T(8,128)(2,1)S(1)}, bf16[320,1664]{1,0:T(8,128)(2,1)S(1)}, u32[]{:S(2)}, u32[]{:S(2)}) %collective-permute-start.15) | collective-permute-done | bytes 1064992 | tf_op jit(solution)/shard_map/ppermute | solution.py:42
  151.1 3.1 %reshape.108 = bf16[8,520,128]{2,1,0:T(8,128)(2,1)} reshape(bf16[320,1664]{1,0:T(8,128)(2,1)} %add_convert_fusion) | data formatting | bytes 2129920 | tf_op jit(solution)/shard_map/reshape | solution.py:169
  154.2 5.6 %all-to-all-start.2 = ((bf16[8,520,128]{2,1,0:T(8,128)(2,1)}), bf16[8,520,128]{2,1,0:T(8,128)(2,1)}, u32[]{:S(2)}, u32[]{:S(2)}) async-start(bf16[8,520,128]{2,1,0:T(8,128)(2,1)} %reshape.108), calls=%async_computation.2 | async-start | bytes 2129920 | tf_op jit(solution)/shard_map/all_to_all | solution.py:37
  160.1 3.0 %convolution_convert_fusion.1 = bf16[512,768]{1,0:T(8,128)(2,1)} fusion(bf16[640,1536]{1,0:T(8,128)(2,1)} %constant_dynamic-update-slice_fusion, bf16[640,1664]{1,0:T(8,128)(2,1)S(1)} %bitcast.65), kind=kOutput, calls=%fused_computation.7 | convolution fusion | flops 503709696 | bytes 2424832 | tf_op jit(solution)/shard_map/dot_general | solution.py:13
  164.8 10.1 %all-to-all-done.2 = bf16[8,520,128]{2,1,0:T(8,128)(2,1)} async-done(((bf16[8,520,128]{2,1,0:T(8,128)(2,1)}), bf16[8,520,128]{2,1,0:T(8,128)(2,1)}, u32[]{:S(2)}, u32[]{:S(2)}) %all-to-all-start.2) | async-done | bytes 1064992 | tf_op jit(solution)/shard_map/all_to_all | solution.py:37
  177.0 3.3 %all-to-all-start.3 = ((bf16[4,130,128]{2,1,0:T(8,128)(2,1)}), bf16[4,130,128]{2,1,0:T(8,128)(2,1)S(1)}, u32[]{:S(2)}, u32[]{:S(2)}) async-start(bf16[4,130,128]{2,1,0:T(8,128)(2,1)} %reshape.109), calls=%async_computation.3 | async-start | bytes 278528 | tf_op jit(solution)/shard_map/all_to_all | solution.py:37
  180.3 2.9 %convolution_convert_fusion.3 = bf16[768,512]{1,0:T(8,128)(2,1)} fusion(bf16[640,1536]{1,0:T(8,128)(2,1)} %constant_dynamic-update-slice_fusion, bf16[640,1664]{1,0:T(8,128)(2,1)S(1)} %bitcast.67), kind=kOutput, calls=%fused_computation.9 | convolution fusion | flops 503709696 | bytes 2424832 | tf_op jit(solution)/shard_map/dot_general | solution.py:13
  183.2 5.7 %all-to-all-done.3 = bf16[4,130,128]{2,1,0:T(8,128)(2,1)S(1)} async-done(((bf16[4,130,128]{2,1,0:T(8,128)(2,1)}), bf16[4,130,128]{2,1,0:T(8,128)(2,1)S(1)}, u32[]{:S(2)}, u32[]{:S(2)}) %all-to-all-start.3) | async-done | bytes 133152 | tf_op jit(solution)/shard_map/all_to_all | solution.py:37
  (122 shorter events, 37.6 us)
Async XLA Ops:
  0.6 47.7 %copy-start = (bf16[768,512]{1,0:T(8,128)(2,1)S(1)}, bf16[768,512]{1,0:T(8,128)(2,1)}, u32[]{:S(2)}) copy-start(bf16[768,512]{1,0:T(8,128)(2,1)} %param.13) | copy-start | bytes 2359300
  1.4 1.4 copy-start.12
  38.3 4.6 %collective-permute-start = (bf16[8,480,128]{2,1,0:T(8,128)(2,1)S(1)}, bf16[8,480,128]{2,1,0:T(8,128)(2,1)}, u32[]{:S(2)}, u32[]{:S(2)}) collective-permute-start(bf16[8,480,128]{2,1,0:T(8,128)(2,1)S(1)} %all_to_all.21), channel_id=1, source_target_pairs={{0,8},{8,0},{16,24},{24,16},{32,40},{40,32},{48,56},{56,48},{64,72... | collective-permute-start | bytes 2949128 | tf_op jit(solution)/shard_map/ppermute | solution.py:42
  42.4 3.8 %copy-start.14 = (bf16[512,768]{1,0:T(8,128)(2,1)S(1)}, bf16[512,768]{1,0:T(8,128)(2,1)}, u32[]{:S(2)}) copy-start(bf16[512,768]{1,0:T(8,128)(2,1)} %param.14) | copy-start | bytes 2359300
  46.1 2.2 %copy-start.7 = (bf16[640,1536]{1,0:T(8,128)(2,1)S(1)}, bf16[640,1536]{1,0:T(8,128)(2,1)}, u32[]{:S(2)}) copy-start(bf16[640,1536]{1,0:T(8,128)(2,1)} %constant_dynamic-update-slice_fusion) | copy-start | bytes 5898244
  48.3 1.1 copy-start.1
  55.4 21.9 %collective-permute-start.3 = (bf16[80,1536]{1,0:T(8,128)(2,1)}, bf16[80,1536]{1,0:T(8,128)(2,1)}, u32[]{:S(2)}, u32[]{:S(2)}) collective-permute-start(bf16[80,1536]{1,0:T(8,128)(2,1)} %get-tuple-element.18), channel_id=1, source_target_pairs={{0,1},{1,2},{2,3},{3,4},{4,5},{5,6},{6,7},{7,0},{8,9},{9,10},{10,1... | collective-permute-start | bytes 737288 | tf_op jit(solution)/shard_map/ppermute | solution.py:73
  59.7 20.1 %collective-permute-start.4 = (bf16[80,1536]{1,0:T(8,128)(2,1)}, bf16[80,1536]{1,0:T(8,128)(2,1)}, u32[]{:S(2)}, u32[]{:S(2)}) collective-permute-start(bf16[80,1536]{1,0:T(8,128)(2,1)} %get-tuple-element.17), channel_id=1, source_target_pairs={{0,2},{1,3},{2,4},{3,5},{4,6},{5,7},{6,0},{7,1},{8,14},{9,15},{10,... | collective-permute-start | bytes 737288 | tf_op jit(solution)/shard_map/ppermute | solution.py:81
  65.8 14.0 %collective-permute-start.6 = (bf16[80,1536]{1,0:T(8,128)(2,1)S(1)}, bf16[80,1536]{1,0:T(8,128)(2,1)}, u32[]{:S(2)}, u32[]{:S(2)}) collective-permute-start(bf16[80,1536]{1,0:T(8,128)(2,1)S(1)} %get-tuple-element.16), channel_id=1, source_target_pairs={{0,7},{1,0},{2,1},{3,2},{4,3},{5,4},{6,5},{7,6},{8,15},{9,8},{10,9... | collective-permute-start | bytes 737288 | tf_op jit(solution)/shard_map/ppermute | solution.py:73
  70.2 19.7 %collective-permute-start.1 = (bf16[80,1536]{1,0:T(8,128)(2,1)}, bf16[80,1536]{1,0:T(8,128)(2,1)S(1)}, u32[]{:S(2)}, u32[]{:S(2)}) collective-permute-start(bf16[80,1536]{1,0:T(8,128)(2,1)} %get-tuple-element.15), channel_id=1, source_target_pairs={{0,1},{1,2},{2,3},{3,4},{4,5},{5,6},{6,7},{7,0},{8,9},{9,10},{10,1... | collective-permute-start | bytes 737288 | tf_op jit(solution)/shard_map/ppermute | solution.py:73
  73.2 16.7 %collective-permute-start.2 = (bf16[80,1536]{1,0:T(8,128)(2,1)}, bf16[80,1536]{1,0:T(8,128)(2,1)S(1)}, u32[]{:S(2)}, u32[]{:S(2)}) collective-permute-start(bf16[80,1536]{1,0:T(8,128)(2,1)} %get-tuple-element.19), channel_id=1, source_target_pairs={{0,7},{1,0},{2,1},{3,2},{4,3},{5,4},{6,5},{7,6},{8,15},{9,8},{10,9... | collective-permute-start | bytes 737288 | tf_op jit(solution)/shard_map/ppermute | solution.py:73
  81.9 16.3 %collective-permute-start.5 = (bf16[80,1536]{1,0:T(8,128)(2,1)}, bf16[80,1536]{1,0:T(8,128)(2,1)S(1)}, u32[]{:S(2)}, u32[]{:S(2)}) collective-permute-start(bf16[80,1536]{1,0:T(8,128)(2,1)} %get-tuple-element.13), channel_id=1, source_target_pairs={{0,2},{1,3},{2,4},{3,5},{4,6},{5,7},{6,0},{7,1},{8,10},{9,11},{10,... | collective-permute-start | bytes 737288 | tf_op jit(solution)/shard_map/ppermute | solution.py:73
  85.2 17.0 %collective-permute-start.7 = (bf16[80,1536]{1,0:T(8,128)(2,1)}, bf16[80,1536]{1,0:T(8,128)(2,1)}, u32[]{:S(2)}, u32[]{:S(2)}) collective-permute-start(bf16[80,1536]{1,0:T(8,128)(2,1)} %get-tuple-element.14), channel_id=1, source_target_pairs={{0,6},{1,7},{2,0},{3,1},{4,2},{5,3},{6,4},{7,5},{8,14},{9,15},{10,... | collective-permute-start | bytes 737288 | tf_op jit(solution)/shard_map/ppermute | solution.py:73
  103.5 10.8 %copy-start.3 = (bf16[80,512]{1,0:T(8,128)(2,1)}, bf16[80,512]{1,0:T(8,128)(2,1)S(1)}, u32[]{:S(2)}) copy-start(bf16[80,512]{1,0:T(8,128)(2,1)S(1)} %get-tuple-element.21) | copy-start | bytes 245764
  103.5 10.9 %copy-start.5 = (bf16[80,512]{1,0:T(8,128)(2,1)}, bf16[80,512]{1,0:T(8,128)(2,1)S(1)}, u32[]{:S(2)}) copy-start(bf16[80,512]{1,0:T(8,128)(2,1)S(1)} %get-tuple-element.23) | copy-start | bytes 245764
  104.4 16.8 %collective-permute-start.11 = (bf16[80,1664]{1,0:T(8,128)(2,1)}, bf16[80,1664]{1,0:T(8,128)(2,1)S(1)}, u32[]{:S(2)}, u32[]{:S(2)}) collective-permute-start(bf16[80,1664]{1,0:T(8,128)(2,1)} %fusion.22), channel_id=1, source_target_pairs={{0,2},{1,3},{2,4},{3,5},{4,6},{5,7},{6,0},{7,1},{8,10},{9,11},{10,... | collective-permute-start | bytes 798728 | tf_op jit(solution)/shard_map/ppermute | solution.py:73
  109.7 14.4 %collective-permute-start.9 = (bf16[80,1664]{1,0:T(8,128)(2,1)}, bf16[80,1664]{1,0:T(8,128)(2,1)S(1)}, u32[]{:S(2)}, u32[]{:S(2)}) collective-permute-start(bf16[80,1664]{1,0:T(8,128)(2,1)} %fusion.22), channel_id=1, source_target_pairs={{0,6},{1,7},{2,0},{3,1},{4,2},{5,3},{6,4},{7,5},{8,14},{9,15},{10,... | collective-permute-start | bytes 798728 | tf_op jit(solution)/shard_map/ppermute | solution.py:73
  112.4 22.8 %collective-permute-start.8 = (bf16[80,1664]{1,0:T(8,128)(2,1)}, bf16[80,1664]{1,0:T(8,128)(2,1)S(1)}, u32[]{:S(2)}, u32[]{:S(2)}) collective-permute-start(bf16[80,1664]{1,0:T(8,128)(2,1)} %fusion.22), channel_id=1, source_target_pairs={{0,7},{1,0},{2,1},{3,2},{4,3},{5,4},{6,5},{7,6},{8,15},{9,8},{10,9... | collective-permute-start | bytes 798728 | tf_op jit(solution)/shard_map/ppermute | solution.py:73
  114.4 27.7 %collective-permute-start.14 = (bf16[80,1664]{1,0:T(8,128)(2,1)}, bf16[80,1664]{1,0:T(8,128)(2,1)S(1)}, u32[]{:S(2)}, u32[]{:S(2)}) collective-permute-start(bf16[80,1664]{1,0:T(8,128)(2,1)} %fusion.22), channel_id=1, source_target_pairs={{0,1},{1,2},{2,3},{3,4},{4,5},{5,6},{6,7},{7,0},{8,9},{9,10},{10,1... | collective-permute-start | bytes 798728 | tf_op jit(solution)/shard_map/ppermute | solution.py:73
  118.3 0.9 copy-start.6
  124.1 17.3 %collective-permute-start.12 = (bf16[80,1664]{1,0:T(8,128)(2,1)S(1)}, bf16[80,1664]{1,0:T(8,128)(2,1)S(1)}, u32[]{:S(2)}, u32[]{:S(2)}) collective-permute-start(bf16[80,1664]{1,0:T(8,128)(2,1)S(1)} %broadcast_select_fusion), channel_id=1, source_target_pairs={{0,6},{1,7},{2,0},{3,1},{4,2},{5,3},{6,4},{7,5},{8,10},{9,11},{10,... | collective-permute-start | bytes 798728 | tf_op jit(solution)/shard_map/ppermute | solution.py:81
  129.4 12.0 %collective-permute-start.10 = (bf16[80,1664]{1,0:T(8,128)(2,1)S(1)}, bf16[80,1664]{1,0:T(8,128)(2,1)S(1)}, u32[]{:S(2)}, u32[]{:S(2)}) collective-permute-start(bf16[80,1664]{1,0:T(8,128)(2,1)S(1)} %collective-permute-done.9), channel_id=1, source_target_pairs={{0,7},{1,0},{2,1},{3,2},{4,3},{5,4},{6,5},{7,6},{8,15},{9,8},{10,9... | collective-permute-start | bytes 798728 | tf_op jit(solution)/shard_map/ppermute | solution.py:73
  131.3 10.7 %collective-permute-start.13 = (bf16[80,1664]{1,0:T(8,128)(2,1)S(1)}, bf16[80,1664]{1,0:T(8,128)(2,1)S(1)}, u32[]{:S(2)}, u32[]{:S(2)}) collective-permute-start(bf16[80,1664]{1,0:T(8,128)(2,1)S(1)} %collective-permute-done.11), channel_id=1, source_target_pairs={{0,1},{1,2},{2,3},{3,4},{4,5},{5,6},{6,7},{7,0},{8,9},{9,10},{10,1... | collective-permute-start | bytes 798728 | tf_op jit(solution)/shard_map/ppermute | solution.py:73
  142.0 1.1 copy-start.15
  143.1 1.1 copy-start.2
  145.3 4.6 %collective-permute-start.15 = (bf16[320,1664]{1,0:T(8,128)(2,1)S(1)}, bf16[320,1664]{1,0:T(8,128)(2,1)S(1)}, u32[]{:S(2)}, u32[]{:S(2)}) collective-permute-start(bf16[320,1664]{1,0:T(8,128)(2,1)S(1)} %slice.90), channel_id=1, source_target_pairs={{0,8},{8,0},{16,24},{24,16},{32,40},{40,32},{48,56},{56,48},{64,72... | collective-permute-start | bytes 3194888 | tf_op jit(solution)/shard_map/ppermute | solution.py:42
  151.1 8.7 %copy-start.10 = (f32[16,2]{0,1:T(2,128)S(1)}, f32[16,2]{0,1:T(2,128)}, u32[]{:S(2)}) copy-start(f32[16,2]{0,1:T(2,128)} %copy-done.9) | copy-start | bytes 388
  151.1 8.7 %copy-start.11 = (s32[16,2]{0,1:T(2,128)S(1)}, s32[16,2]{0,1:T(2,128)}, u32[]{:S(2)}) copy-start(s32[16,2]{0,1:T(2,128)} %param.10) | copy-start | bytes 388
  154.2 20.7 %all-to-all-start.2 = ((bf16[8,520,128]{2,1,0:T(8,128)(2,1)}), bf16[8,520,128]{2,1,0:T(8,128)(2,1)}, u32[]{:S(2)}, u32[]{:S(2)}) async-start(bf16[8,520,128]{2,1,0:T(8,128)(2,1)} %reshape.108), calls=%async_computation.2 | async-start | bytes 2129920 | tf_op jit(solution)/shard_map/all_to_all | solution.py:37
  160.1 3.1 %copy-start.8 = (bf16[640,1536]{1,0:T(8,128)(2,1)S(1)}, bf16[640,1536]{1,0:T(8,128)(2,1)}, u32[]{:S(2)}) copy-start(bf16[640,1536]{1,0:T(8,128)(2,1)} %constant_dynamic-update-slice_fusion) | copy-start | bytes 5898244
  177.0 12.0 %all-to-all-start.3 = ((bf16[4,130,128]{2,1,0:T(8,128)(2,1)}), bf16[4,130,128]{2,1,0:T(8,128)(2,1)S(1)}, u32[]{:S(2)}, u32[]{:S(2)}) async-start(bf16[4,130,128]{2,1,0:T(8,128)(2,1)} %reshape.109), calls=%async_computation.3 | async-start | bytes 278528 | tf_op jit(solution)/shard_map/all_to_all | solution.py:37
  180.3 9.2 %copy-start.13 = (f32[16,1]{0,1:T(1,128)S(1)}, f32[16,1]{0,1:T(1,128)}, u32[]{:S(2)}) copy-start(f32[16,1]{0,1:T(1,128)} %copy-done.12) | copy-start | bytes 196
  (2 other events, 1.6 us)

commit v4 on v0

v4 whole, which is shorter than its diff:
```python
import jax
import jax.numpy as jnp
from jax import lax
from jax.experimental import pallas as pl
from jax.experimental.pallas import tpu as pltpu
from jax.sharding import PartitionSpec as P

EXPERTS = 4
MOST = 10
CORES = 2
LANES = 128


def contract(left, right, left_dim, right_dim):
    return lax.dot_general(
        left, right, (((left_dim,), (right_dim,)), ((), ())), preferred_element_type=jnp.float32
    )


VMEM = pl.BlockSpec(memory_space=pltpu.VMEM)
SMEM = pl.BlockSpec(memory_space=pltpu.SMEM)
PARAMS = pltpu.CompilerParams(vmem_limit_bytes=40 * 1024 * 1024)


def route_masks(ids_ref, logits_ref):
    count = ids_ref.shape[0]
    slots = EXPERTS * MOST
    slot = lax.broadcasted_iota(jnp.int32, (count, slots), 1)
    expert = jnp.zeros((count, slots), jnp.int32)
    for e in range(1, EXPERTS):
        expert = expert + (slot >= e * MOST).astype(jnp.int32)
    named = [ids_ref[:, k : k + 1] == expert for k in range(2)]
    chosen = (named[0] | named[1]).astype(jnp.float32)
    row = lax.broadcasted_iota(jnp.int32, (count, count), 0)
    column = lax.broadcasted_iota(jnp.int32, (count, count), 1)
    before = (column < row).astype(jnp.float32)
    rank = jnp.dot(before, chosen, preferred_element_type=jnp.float32)
    placed = rank == (slot - expert * MOST).astype(jnp.float32)
    masks = [(n & placed).astype(jnp.bfloat16) for n in named]
    first = jax.nn.sigmoid(logits_ref[:, 0:1] - logits_ref[:, 1:2])
    return masks, (first, 1.0 - first)


def pack_kernel(ids_ref, logits_ref, tokens_ref, grad_ref, slots_ref):
    width = tokens_ref.shape[1]
    masks, weights = route_masks(ids_ref, logits_ref)
    grad = grad_ref[...].astype(jnp.float32)
    cots = [(w * grad).astype(jnp.bfloat16) for w in weights]
    slots_ref[:, :width] = contract(masks[0] + masks[1], tokens_ref[...], 0, 0).astype(
        jnp.bfloat16
    )
    slots_ref[:, width:] = (
        contract(masks[0], cots[0], 0, 0) + contract(masks[1], cots[1], 0, 0)
    ).astype(jnp.bfloat16)


def parts_kernel(plane_ref, near_ref, far_ref, gate_ref, up_ref, down_ref, *rest):
    chunks, parts_ref = rest[:-1], rest[-1]
    half = near_ref.shape[0]
    depth, units = gate_ref.shape
    own = chunks[0].shape[0]
    for start, rows_ref in ((0, near_ref), (half, far_ref)):
        rows = rows_ref[:, :depth]
        cots = rows_ref[:, depth:]
        at = slice(start, start + half)
        gate = jnp.dot(rows, gate_ref[...], preferred_element_type=jnp.float32)
        parts_ref[at, :units] = gate.astype(jnp.bfloat16)
        upper = jnp.dot(rows, up_ref[...], preferred_element_type=jnp.float32)
        parts_ref[at, units : 2 * units] = upper.astype(jnp.bfloat16)
        hidden_cot = contract(cots, down_ref[...], 1, 1)
        parts_ref[at, 2 * units :] = hidden_cot.astype(jnp.bfloat16)
    for ahead, chunk_ref in enumerate(chunks):
        at = lax.rem(plane_ref[0] + ahead, len(chunks)) * own
        chunk_ref[...] = parts_ref[pl.ds(pl.multiple_of(at, 16), own), :]


def product_block(product):
    near = product.astype(jnp.bfloat16).astype(jnp.float32)
    lane = lax.broadcasted_iota(jnp.int32, (product.shape[0], LANES), 1)
    block = jnp.where(lane == 0, near, jnp.where(lane == 1, product - near, 0.0))
    return block.astype(jnp.bfloat16)


def store_narrow(ref, summed):
    ref[:, :-LANES] = summed[:, :-LANES].astype(jnp.bfloat16)
    tail = summed[:, -LANES:]
    ref[:, -LANES:] = product_block(tail[:, 0:1] + tail[:, 1:2])


def relay_kernel(core_ref, up_ref, up_three_ref, down_ref, down_three_ref, four_ref, *outs):
    even = core_ref[0] == 0
    four = four_ref[...].astype(jnp.float32)
    up = up_ref[...].astype(jnp.float32) + up_three_ref[...].astype(jnp.float32)
    outs[0][...] = (up + jnp.where(even, four, 0.0)).astype(jnp.bfloat16)
    down = down_ref[...].astype(jnp.float32) + down_three_ref[...].astype(jnp.float32)
    outs[1][...] = (down + jnp.where(even, 0.0, four)).astype(jnp.bfloat16)


def hidden_kernel(a_ref, b_ref, c_ref, d_ref, e_ref, value_ref):
    units = a_ref.shape[1] // 3

    def summed(columns):
        total = a_ref[:, columns].astype(jnp.float32)
        for ref in (b_ref, c_ref, d_ref, e_ref):
            total = total + ref[:, columns].astype(jnp.float32)
        return total

    gate = summed(slice(0, units))
    upper = summed(slice(units, 2 * units))
    hidden_cot = summed(slice(2 * units, 3 * units))
    sig = jax.nn.sigmoid(gate)
    hidden = (gate * sig * upper).astype(jnp.bfloat16)
    value_ref[:, :units] = hidden
    gate_cot = hidden_cot * upper * sig * (1.0 + gate * (1.0 - sig))
    value_ref[:, units : 2 * units] = gate_cot.astype(jnp.bfloat16)
    value_ref[:, 2 * units : 3 * units] = (hidden_cot * gate * sig).astype(jnp.bfloat16)
    product = jnp.sum(hidden.astype(jnp.float32) * hidden_cot, axis=1, keepdims=True)
    value_ref[:, 3 * units :] = product_block(product)


def back_kernel(plane_ref, gate_ref, up_ref, down_ref, *rest):
    pieces, (near_ref, far_ref, hidden_ref, gate_cot_ref, up_cot_ref, tail_ref) = rest[:8], rest[8:]
    own = pieces[0].shape[0]
    half = near_ref.shape[0]
    depth, units = gate_ref.shape
    for ahead, piece in enumerate(pieces):
        at = pl.multiple_of(lax.rem(plane_ref[0] + ahead, len(pieces)) * own, 16)
        at = pl.ds(at, own)
        hidden_ref[at, :] = piece[:, :units]
        gate_cot_ref[at, :] = piece[:, units : 2 * units]
        up_cot_ref[at, :] = piece[:, 2 * units : 3 * units]
        tail_ref[at, :] = piece[:, 3 * units :]
    for start, ref in ((half, far_ref), (0, near_ref)):
        at = slice(start, start + half)
        out = jnp.dot(hidden_ref[at, :], down_ref[...], preferred_element_type=jnp.float32)
        ref[:, :depth] = out.astype(jnp.bfloat16)
        grad = contract(gate_cot_ref[at, :], gate_ref[...], 1, 1)
        grad = grad + contract(up_cot_ref[at, :], up_ref[...], 1, 1)
        ref[:, depth : 2 * depth] = grad.astype(jnp.bfloat16)
        ref[:, 2 * depth :] = tail_ref[at, :]


def add_kernel(near_ref, far_ref, sum_ref):
    store_narrow(sum_ref, near_ref[...].astype(jnp.float32) + far_ref[...].astype(jnp.float32))


def fold_kernel(blocks_ref, sum_ref):
    total = blocks_ref[0].astype(jnp.float32)
    for i in range(1, blocks_ref.shape[0]):
        total = total + blocks_ref[i].astype(jnp.float32)
    store_narrow(sum_ref, total)


def call(kernel, outs, scalars, arrays, scratch=(), flops=0):
    return pl.pallas_call(
        kernel,
        out_shape=[pltpu.VMEM(shape, jnp.bfloat16) for shape in outs],
        in_specs=[SMEM] * len(scalars) + [VMEM] * len(arrays),
        out_specs=[VMEM] * len(outs),
        scratch_shapes=scratch,
        compiler_params=PARAMS,
        cost_estimate=pl.CostEstimate(flops=flops, bytes_accessed=4 << 20, transcendentals=0),
    )(*[value.reshape(1) for value in scalars], *arrays)


def combine_kernel(ids_ref, logits_ref, back_ref, out_ref, tokens_ref, logits_grad_ref):
    width = out_ref.shape[1]
    masks, weights = route_masks(ids_ref, logits_ref)

    def pick(mask, columns):
        return jnp.dot(mask, back_ref[:, columns], preferred_element_type=jnp.float32)

    outs = [pick(m, slice(0, width)) for m in masks]
    out_ref[...] = (weights[0] * outs[0] + weights[1] * outs[1]).astype(jnp.bfloat16)
    tokens_ref[...] = pick(masks[0] + masks[1], slice(width, 2 * width)).astype(jnp.bfloat16)
    products = [pick(m, slice(2 * width, 2 * width + LANES)) for m in masks]
    products = [p[:, 0:1] + p[:, 1:2] for p in products]
    change = products[0] * weights[1] - products[1] * weights[0]
    which = lax.broadcasted_iota(jnp.int32, logits_grad_ref.shape, 1)
    logits_grad_ref[...] = jnp.where(which == 0, change, -change)


def on_device(tokens, expert_ids, route_logits, w_gate, w_up, w_down, out_grad):
    count, width = tokens.shape
    hidden_width = w_gate.shape[1]
    peers = lax.axis_size("expert")
    planes = lax.axis_size("fsdp")
    group = peers // EXPERTS
    chips = group // CORES
    half = peers // CORES * MOST
    rows = CORES * half
    own = rows // planes
    matching = [[group * e + i for e in range(EXPERTS)] for i in range(group)]
    same_core = [
        [group * e + CORES * p + c for p in range(chips)]
        for e in range(EXPERTS)
        for c in range(CORES)
    ]
    other_core = [(i, i ^ 1) for i in range(peers)]

    def across(blocks, groups):
        return lax.all_to_all(
            blocks, "expert", split_axis=0, concat_axis=0, axis_index_groups=groups, tiled=True
        )

    def swap(value):
        return lax.ppermute(value, "expert", other_core)

    def shift(value, by):
        pairs = [(i, (i + by) % planes) for i in range(planes)]
        return lax.ppermute(value, "fsdp", pairs)

    def shift_by_core(value, by):
        pairs = []
        for e in range(peers):
            for z in range(planes):
                there = (z + by) % planes if e % CORES == 0 else (z - by) % planes
                pairs.append((e * planes + z, e * planes + there))
        return lax.ppermute(value, ("expert", "fsdp"), pairs)

    me = lax.axis_index("expert")
    plane = lax.axis_index("fsdp")
    core = me % CORES

    def relay(chunk):
        up_three = shift(chunk[3], 1)
        down_three = shift(chunk[-3], -1)
        four = shift_by_core(chunk[4], 2)
        up_one = shift(chunk[1], 1)
        down_one = shift(chunk[-1], -1)
        arrays = (chunk[2], up_three, chunk[-2], down_three, four)
        up_two, down_two = call(relay_kernel, [four.shape] * 2, [core], arrays)
        return chunk[0], up_one, down_one, shift(up_two, 2), shift(down_two, -2)

    def to_all_planes(value):
        next_two, last_two = shift(value, -2), shift(value, 2)
        next_one, last_one = shift(value, -1), shift(value, 1)
        four = shift_by_core(jnp.where(core == 0, next_two, last_two), -2)
        next_three, last_three = shift(next_two, -1), shift(last_two, 1)
        return value, next_one, next_two, next_three, four, last_three, last_two, last_one

    def gather_rows(slot_rows):
        mine = across(slot_rows.reshape(EXPERTS, -1, LANES), matching)
        mine = mine.reshape(1, EXPERTS * MOST, -1)
        near = across(jnp.broadcast_to(mine, (chips,) + mine.shape[1:]), same_core)
        near = near.reshape(half, -1)
        return near, swap(near)

    def give_back(near, far):
        [mine] = call(add_kernel, [near.shape], [], [near, swap(far)])
        arrived = across(mine.reshape(chips, EXPERTS * MOST, -1), same_core)
        [summed] = call(fold_kernel, [arrived.shape[1:]], [], [arrived])
        back = across(summed.reshape(EXPERTS, -1, LANES), matching)
        return back.reshape(EXPERTS * MOST, -1)

    bf16 = jnp.bfloat16
    [slots] = call(
        pack_kernel,
        [(EXPERTS * MOST, 2 * width)],
        [],
        [expert_ids, route_logits, tokens, out_grad],
    )
    near, far = gather_rows(slots)
    chunks = call(
        parts_kernel,
        [(own, 3 * hidden_width)] * planes,
        [plane],
        [near, far, w_gate, w_up, w_down],
        scratch=[pltpu.VMEM((rows, 3 * hidden_width), bf16)],
        flops=6 * rows * width * hidden_width,
    )
    arrived = jnp.concatenate([near[:, :width], far[:, :width]], axis=0)
    arrived_cot = jnp.concatenate([near[:, width:], far[:, width:]], axis=0)
    [value] = call(hidden_kernel, [(own, 3 * hidden_width + LANES)], [], relay(chunks))
    near_part, far_part, hidden, gate_cot, up_cot = call(
        back_kernel,
        [(half, 2 * width + LANES)] * 2 + [(rows, hidden_width)] * 3,
        [plane],
        [w_gate, w_up, w_down, *to_all_planes(value)],
        scratch=[pltpu.VMEM((rows, LANES), bf16)],
        flops=6 * rows * width * hidden_width,
    )
    back = give_back(near_part, far_part)
    down_grad = contract(hidden, arrived_cot, 0, 0).astype(jnp.bfloat16)
    gate_grad = contract(arrived, gate_cot, 0, 0).astype(jnp.bfloat16)
    up_grad = contract(arrived, up_cot, 0, 0).astype(jnp.bfloat16)

    layer_out, tokens_grad, logits_grad = pl.pallas_call(
        combine_kernel,
        out_shape=[
            jax.ShapeDtypeStruct((count, width), bf16),
            jax.ShapeDtypeStruct((count, width), bf16),
            jax.ShapeDtypeStruct(route_logits.shape, jnp.float32),
        ],
        in_specs=[VMEM] * 3,
        out_specs=[VMEM] * 3,
        compiler_params=PARAMS,
    )(expert_ids, route_logits, back)
    return (layer_out, tokens_grad, gate_grad, up_grad, down_grad, logits_grad)


def solution(mesh):
    return jax.shard_map(
        on_device,
        mesh=mesh,
        in_specs=(
            P("expert", "fsdp"),
            P("expert", None),
            P("expert", None),
            P("fsdp", "expert"),
            P("fsdp", "expert"),
            P("expert", "fsdp"),
            P("expert", "fsdp"),
        ),
        out_specs=(
            P("expert", "fsdp"),
            P("expert", "fsdp"),
            P("fsdp", "expert"),
            P("fsdp", "expert"),
            P("expert", "fsdp"),
            P("expert", None),
        ),
        check_vma=False,
    )
```

time: 330 us -> 175 us (0.53)
  the two profiles are of different devices: /device:TPU:2 before, /device:TPU:64 now
where the time goes in v4:
time: 175 us; the launch traced here: 174 us
  starting transfers between devices  64.7 us (37%)
  waiting for transfers between devices  46.9 us (27%)
  blocking collectives  33.1 us (19%)
  local copies, waits for them, and re-layouts  14.6 us (8%)
  Pallas kernels  8.22 us (5%)
  matrix products  5.06 us (3%)
    ppermute x12, starting transfers between devices, shift(): return lax.ppermute(value, 'fsdp', pairs)  42.9 us
    all_to_all x2, blocking collectives, across(): lax.all_to_all(blocks, 'expert', split_axis=0, concat_axis=0, axis_index_...  33.1 us
    ppermute x12, waiting for transfers between devices, shift(): return lax.ppermute(value, 'fsdp', pairs)  18.8 us
    all_to_all x2, waiting for transfers between devices, across(): lax.all_to_all(blocks, 'expert', split_axis=0, concat_axis=0, axis_index_...  18.6 us
    unnamed x37, local copies, waits for them, and re-layouts  12.2 us
    ppermute x2, starting transfers between devices, shift_by_core(): return lax.ppermute(value, ('expert', 'fsdp'), pairs)  11.1 us
    pallas_call x7, Pallas kernels, call(): pl.pallas_call(kernel, out_shape=[pltpu.VMEM(shape, jnp.bfloat16) for sha...  7.19 us
    all_to_all x2, starting transfers between devices, across(): lax.all_to_all(blocks, 'expert', split_axis=0, concat_axis=0, axis_index_...  6.89 us
  transfers between devices with their start and end apart: 18, of which 12 were waited for; matrix products, arithmetic and copies ran while one was open for 3% of the time, Pallas kernels for 0%

profile of v4, /device:TPU:64, one launch (start us, length us, event | category | flops | bytes accessed | tf_op | source)
XLA Modules:
  0.0 173.6 jit_solution(4275339978379148223)
XLA Ops:
  4.2 15.7 %all_to_all.20 = bf16[4,120,128]{2,1,0:T(8,128)(2,1)S(1)} all-to-all(bf16[4,120,128]{2,1,0:T(8,128)(2,1)S(1)} %reshape.37), channel_id=1, replica_groups={{0,128,256,384},{8,136,264,392},{16,144,272,400},{24,152,280,408},{32,1..., dimensions={0} | all-to-all | bytes 245760 | tf_op jit(solution)/shard_map/all_to_all | solution.py:202
  20.2 17.4 %all_to_all.21 = bf16[8,40,1536]{2,1,0:T(8,128)(2,1)S(1)} all-to-all(bf16[8,40,1536]{2,1,0:T(8,128)(2,1)S(1)} %broadcast_in_dim.8), channel_id=1, replica_groups={{0,16,32,48,64,80,96,112},{8,24,40,56,72,88,104,120},{128,144,160,176,1..., dimensions={0} | all-to-all | bytes 1966080 | tf_op jit(solution)/shard_map/all_to_all | solution.py:202
  37.6 1.9 %collective-permute-start = (bf16[320,1536]{1,0:T(8,128)(2,1)S(1)}, bf16[320,1536]{1,0:T(8,128)(2,1)S(1)}, u32[]{:S(2)}, u32[]{:S(2)}) collective-permute-start(bf16[320,1536]{1,0:T(8,128)(2,1)S(1)} %bitcast.7), channel_id=1, source_target_pairs={{0,8},{8,0},{16,24},{24,16},{32,40},{40,32},{48,56},{56,48},{64,72... | collective-permute-start | bytes 2949128 | tf_op jit(solution)/shard_map/ppermute | solution.py:207
  39.5 2.5 %collective-permute-done.far_ref = bf16[320,1536]{1,0:T(8,128)(2,1)S(1)} collective-permute-done((bf16[320,1536]{1,0:T(8,128)(2,1)S(1)}, bf16[320,1536]{1,0:T(8,128)(2,1)S(1)}, u32[]{:S(2)}, u32[]{:S(2)}) %collective-permute-start) | collective-permute-done | bytes 983072 | tf_op jit(solution)/shard_map/ppermute | solution.py:207
  45.4 2.6 %shard_map.119 = (bf16[80,1536]{1,0:T(8,128)(2,1)S(1)}, bf16[80,1536]{1,0:T(8,128)(2,1)S(1)}, bf16[80,1536]{1,0:T(8,128)(2,1)S(1)}, bf16[80,1536]{1,0:T(8,128)(2...) custom-call(s32[1]{0:T(128)} %bitcast.plane_ref, ...), custom_call_target="tpu_custom_call" | custom-call | flops 1509949440 | bytes 4194304 | tf_op jit(solution)/shard_map/pallas_call | solution.py:155
  49.4 4.3 %collective-permute-start.3 = (bf16[80,1536]{1,0:T(8,128)(2,1)}, bf16[80,1536]{1,0:T(8,128)(2,1)S(1)}, u32[]{:S(2)}, u32[]{:S(2)}) collective-permute-start(bf16[80,1536]{1,0:T(8,128)(2,1)} %get-tuple-element.28), channel_id=1, source_target_pairs={{0,1},{1,2},{2,3},{3,4},{4,5},{5,6},{6,7},{7,0},{8,9},{9,10},{10,1... | collective-permute-start | bytes 737288 | tf_op jit(solution)/shard_map/ppermute | solution.py:211
  53.7 1.9 %collective-permute-start.4 = (bf16[80,1536]{1,0:T(8,128)(2,1)}, bf16[80,1536]{1,0:T(8,128)(2,1)S(1)}, u32[]{:S(2)}, u32[]{:S(2)}) collective-permute-start(bf16[80,1536]{1,0:T(8,128)(2,1)} %get-tuple-element.30), channel_id=1, source_target_pairs={{0,7},{1,0},{2,1},{3,2},{4,3},{5,4},{6,5},{7,6},{8,15},{9,8},{10,9... | collective-permute-start | bytes 737288 | tf_op jit(solution)/shard_map/ppermute | solution.py:211
  55.6 7.3 %collective-permute-start.5 = (bf16[80,1536]{1,0:T(8,128)(2,1)}, bf16[80,1536]{1,0:T(8,128)(2,1)S(1)}, u32[]{:S(2)}, u32[]{:S(2)}) collective-permute-start(bf16[80,1536]{1,0:T(8,128)(2,1)} %get-tuple-element.31), channel_id=1, source_target_pairs={{0,2},{1,3},{2,4},{3,5},{4,6},{5,7},{6,0},{7,1},{8,14},{9,15},{10,... | collective-permute-start | bytes 737288 | tf_op jit(solution)/shard_map/ppermute | solution.py:219
  62.9 5.1 %collective-permute-start.1 = (bf16[80,1536]{1,0:T(8,128)(2,1)}, bf16[80,1536]{1,0:T(8,128)(2,1)S(1)}, u32[]{:S(2)}, u32[]{:S(2)}) collective-permute-start(bf16[80,1536]{1,0:T(8,128)(2,1)} %copy-done.9), channel_id=1, source_target_pairs={{0,1},{1,2},{2,3},{3,4},{4,5},{5,6},{6,7},{7,0},{8,9},{9,10},{10,1... | collective-permute-start | bytes 737288 | tf_op jit(solution)/shard_map/ppermute | solution.py:211
  68.1 1.9 %collective-permute-start.2 = (bf16[80,1536]{1,0:T(8,128)(2,1)}, bf16[80,1536]{1,0:T(8,128)(2,1)S(1)}, u32[]{:S(2)}, u32[]{:S(2)}) collective-permute-start(bf16[80,1536]{1,0:T(8,128)(2,1)} %copy-done.8), channel_id=1, source_target_pairs={{0,7},{1,0},{2,1},{3,2},{4,3},{5,4},{6,5},{7,6},{8,15},{9,8},{10,9... | collective-permute-start | bytes 737288 | tf_op jit(solution)/shard_map/ppermute | solution.py:211
  70.5 5.5 %collective-permute-start.6 = (bf16[80,1536]{1,0:T(8,128)(2,1)S(1)}, bf16[80,1536]{1,0:T(8,128)(2,1)S(1)}, u32[]{:S(2)}, u32[]{:S(2)}) collective-permute-start(bf16[80,1536]{1,0:T(8,128)(2,1)S(1)} %get-tuple-element.32), channel_id=1, source_target_pairs={{0,2},{1,3},{2,4},{3,5},{4,6},{5,7},{6,0},{7,1},{8,10},{9,11},{10,... | collective-permute-start | bytes 737288 | tf_op jit(solution)/shard_map/ppermute | solution.py:211
  76.0 5.7 %collective-permute-start.7 = (bf16[80,1536]{1,0:T(8,128)(2,1)S(1)}, bf16[80,1536]{1,0:T(8,128)(2,1)S(1)}, u32[]{:S(2)}, u32[]{:S(2)}) collective-permute-start(bf16[80,1536]{1,0:T(8,128)(2,1)S(1)} %get-tuple-element.33), channel_id=1, source_target_pairs={{0,6},{1,7},{2,0},{3,1},{4,2},{5,3},{6,4},{7,5},{8,14},{9,15},{10,... | collective-permute-start | bytes 737288 | tf_op jit(solution)/shard_map/ppermute | solution.py:211
  81.8 3.4 %collective-permute-done.6.d_ref = bf16[80,1536]{1,0:T(8,128)(2,1)S(1)} collective-permute-done((bf16[80,1536]{1,0:T(8,128)(2,1)S(1)}, bf16[80,1536]{1,0:T(8,128)(2,1)S(1)}, u32[]{:S(2)}, u32[]{:S(2)}) %collective-permute-start.6) | collective-permute-done | bytes 245792 | tf_op jit(solution)/shard_map/ppermute | solution.py:211
  85.2 5.5 %collective-permute-done.7.e_ref = bf16[80,1536]{1,0:T(8,128)(2,1)S(1)} collective-permute-done((bf16[80,1536]{1,0:T(8,128)(2,1)S(1)}, bf16[80,1536]{1,0:T(8,128)(2,1)S(1)}, u32[]{:S(2)}, u32[]{:S(2)}) %collective-permute-start.7) | collective-permute-done | bytes 245792 | tf_op jit(solution)/shard_map/ppermute | solution.py:211
  91.0 5.7 %collective-permute-start.11 = (bf16[80,1664]{1,0:T(8,128)(2,1)S(1)}, bf16[80,1664]{1,0:T(8,128)(2,1)S(1)}, u32[]{:S(2)}, u32[]{:S(2)}) collective-permute-start(bf16[80,1664]{1,0:T(8,128)(2,1)S(1)} %shard_map.121.rest_0_), channel_id=1, source_target_pairs={{0,2},{1,3},{2,4},{3,5},{4,6},{5,7},{6,0},{7,1},{8,10},{9,11},{10,... | collective-permute-start | bytes 798728 | tf_op jit(solution)/shard_map/ppermute | solution.py:211
  96.7 2.7 %collective-permute-start.9 = (bf16[80,1664]{1,0:T(8,128)(2,1)S(1)}, bf16[80,1664]{1,0:T(8,128)(2,1)S(1)}, u32[]{:S(2)}, u32[]{:S(2)}) collective-permute-start(bf16[80,1664]{1,0:T(8,128)(2,1)S(1)} %shard_map.121.rest_0_), channel_id=1, source_target_pairs={{0,6},{1,7},{2,0},{3,1},{4,2},{5,3},{6,4},{7,5},{8,14},{9,15},{10,... | collective-permute-start | bytes 798728 | tf_op jit(solution)/shard_map/ppermute | solution.py:211
  99.4 4.3 %collective-permute-start.14 = (bf16[80,1664]{1,0:T(8,128)(2,1)S(1)}, bf16[80,1664]{1,0:T(8,128)(2,1)S(1)}, u32[]{:S(2)}, u32[]{:S(2)}) collective-permute-start(bf16[80,1664]{1,0:T(8,128)(2,1)S(1)} %shard_map.121.rest_0_), channel_id=1, source_target_pairs={{0,1},{1,2},{2,3},{3,4},{4,5},{5,6},{6,7},{7,0},{8,9},{9,10},{10,1... | collective-permute-start | bytes 798728 | tf_op jit(solution)/shard_map/ppermute | solution.py:211
  103.7 1.9 %collective-permute-start.8 = (bf16[80,1664]{1,0:T(8,128)(2,1)S(1)}, bf16[80,1664]{1,0:T(8,128)(2,1)S(1)}, u32[]{:S(2)}, u32[]{:S(2)}) collective-permute-start(bf16[80,1664]{1,0:T(8,128)(2,1)S(1)} %shard_map.121.rest_0_), channel_id=1, source_target_pairs={{0,7},{1,0},{2,1},{3,2},{4,3},{5,4},{6,5},{7,6},{8,15},{9,8},{10,9... | collective-permute-start | bytes 798728 | tf_op jit(solution)/shard_map/ppermute | solution.py:211
  105.6 3.1 %collective-permute-done.11.rest_6_ = bf16[80,1664]{1,0:T(8,128)(2,1)S(1)} collective-permute-done((bf16[80,1664]{1,0:T(8,128)(2,1)S(1)}, bf16[80,1664]{1,0:T(8,128)(2,1)S(1)}, u32[]{:S(2)}, u32[]{:S(2)}) %collective-permute-start.11) | collective-permute-done | bytes 266272 | tf_op jit(solution)/shard_map/ppermute | solution.py:211
  108.7 1.9 %collective-permute-start.13 = (bf16[80,1664]{1,0:T(8,128)(2,1)S(1)}, bf16[80,1664]{1,0:T(8,128)(2,1)S(1)}, u32[]{:S(2)}, u32[]{:S(2)}) collective-permute-start(bf16[80,1664]{1,0:T(8,128)(2,1)S(1)} %collective-permute-done.11.rest_6_), channel_id=1, source_target_pairs={{0,1},{1,2},{2,3},{3,4},{4,5},{5,6},{6,7},{7,0},{8,9},{9,10},{10,1... | collective-permute-start | bytes 798728 | tf_op jit(solution)/shard_map/ppermute | solution.py:211
  110.6 2.0 %collective-permute-done.9.rest_2_ = bf16[80,1664]{1,0:T(8,128)(2,1)S(1)} collective-permute-done((bf16[80,1664]{1,0:T(8,128)(2,1)S(1)}, bf16[80,1664]{1,0:T(8,128)(2,1)S(1)}, u32[]{:S(2)}, u32[]{:S(2)}) %collective-permute-start.9) | collective-permute-done | bytes 266272 | tf_op jit(solution)/shard_map/ppermute | solution.py:211
  112.6 3.8 %collective-permute-start.12 = (bf16[80,1664]{1,0:T(8,128)(2,1)S(1)}, bf16[80,1664]{1,0:T(8,128)(2,1)S(1)}, u32[]{:S(2)}, u32[]{:S(2)}) collective-permute-start(bf16[80,1664]{1,0:T(8,128)(2,1)S(1)} %broadcast_select_fusion), channel_id=1, source_target_pairs={{0,6},{1,7},{2,0},{3,1},{4,2},{5,3},{6,4},{7,5},{8,10},{9,11},{10,... | collective-permute-start | bytes 798728 | tf_op jit(solution)/shard_map/ppermute | solution.py:219
  116.4 1.9 %collective-permute-start.10 = (bf16[80,1664]{1,0:T(8,128)(2,1)S(1)}, bf16[80,1664]{1,0:T(8,128)(2,1)S(1)}, u32[]{:S(2)}, u32[]{:S(2)}) collective-permute-start(bf16[80,1664]{1,0:T(8,128)(2,1)S(1)} %collective-permute-done.9.rest_2_), channel_id=1, source_target_pairs={{0,7},{1,0},{2,1},{3,2},{4,3},{5,4},{6,5},{7,6},{8,15},{9,8},{10,9... | collective-permute-start | bytes 798728 | tf_op jit(solution)/shard_map/ppermute | solution.py:211
  118.4 2.3 %collective-permute-done.13.rest_5_ = bf16[80,1664]{1,0:T(8,128)(2,1)S(1)} collective-permute-done((bf16[80,1664]{1,0:T(8,128)(2,1)S(1)}, bf16[80,1664]{1,0:T(8,128)(2,1)S(1)}, u32[]{:S(2)}, u32[]{:S(2)}) %collective-permute-start.13) | collective-permute-done | bytes 266272 | tf_op jit(solution)/shard_map/ppermute | solution.py:211
  120.7 4.1 %collective-permute-done.12.rest_4_ = bf16[80,1664]{1,0:T(8,128)(2,1)S(1)} collective-permute-done((bf16[80,1664]{1,0:T(8,128)(2,1)S(1)}, bf16[80,1664]{1,0:T(8,128)(2,1)S(1)}, u32[]{:S(2)}, u32[]{:S(2)}) %collective-permute-start.12) | collective-permute-done | bytes 266272 | tf_op jit(solution)/shard_map/ppermute | solution.py:219
  124.8 2.4 %collective-permute-done.10.rest_3_ = bf16[80,1664]{1,0:T(8,128)(2,1)S(1)} collective-permute-done((bf16[80,1664]{1,0:T(8,128)(2,1)S(1)}, bf16[80,1664]{1,0:T(8,128)(2,1)S(1)}, u32[]{:S(2)}, u32[]{:S(2)}) %collective-permute-start.10) | collective-permute-done | bytes 266272 | tf_op jit(solution)/shard_map/ppermute | solution.py:211
  132.5 1.9 %collective-permute-start.15 = (bf16[320,1664]{1,0:T(8,128)(2,1)S(1)}, bf16[320,1664]{1,0:T(8,128)(2,1)S(1)}, u32[]{:S(2)}, u32[]{:S(2)}) collective-permute-start(bf16[320,1664]{1,0:T(8,128)(2,1)S(1)} %get-tuple-element.35), channel_id=1, source_target_pairs={{0,8},{8,0},{16,24},{24,16},{32,40},{40,32},{48,56},{56,48},{64,72... | collective-permute-start | bytes 3194888 | tf_op jit(solution)/shard_map/ppermute | solution.py:207
  134.4 2.6 %collective-permute-done.15.far_ref = bf16[320,1664]{1,0:T(8,128)(2,1)S(1)} collective-permute-done((bf16[320,1664]{1,0:T(8,128)(2,1)S(1)}, bf16[320,1664]{1,0:T(8,128)(2,1)S(1)}, u32[]{:S(2)}, u32[]{:S(2)}) %collective-permute-start.15) | collective-permute-done | bytes 1064992 | tf_op jit(solution)/shard_map/ppermute | solution.py:207
  138.7 3.6 %all-to-all-start.2 = ((bf16[8,40,1664]{2,1,0:T(8,128)(2,1)}), bf16[8,40,1664]{2,1,0:T(8,128)(2,1)S(1)}, u32[]{:S(2)}, u32[]{:S(2)}) async-start(bf16[8,40,1664]{2,1,0:T(8,128)(2,1)} %bitcast.3), calls=%async_computation.2 | async-start | bytes 2129920 | tf_op jit(solution)/shard_map/all_to_all | solution.py:202
  147.0 10.8 %all-to-all-done.2.blocks_ref = bf16[8,40,1664]{2,1,0:T(8,128)(2,1)S(1)} async-done(((bf16[8,40,1664]{2,1,0:T(8,128)(2,1)}), bf16[8,40,1664]{2,1,0:T(8,128)(2,1)S(1)}, u32[]{:S(2)}, u32[]{:S(2)}) %all-to-all-start.2) | async-done | bytes 1064992 | tf_op jit(solution)/shard_map/all_to_all | solution.py:202
  158.8 3.3 %all-to-all-start.3 = ((bf16[4,130,128]{2,1,0:T(8,128)(2,1)}), bf16[4,130,128]{2,1,0:T(8,128)(2,1)S(1)}, u32[]{:S(2)}, u32[]{:S(2)}) async-start(bf16[4,130,128]{2,1,0:T(8,128)(2,1)} %reshape.41), calls=%async_computation.3 | async-start | bytes 278528 | tf_op jit(solution)/shard_map/all_to_all | solution.py:202
  163.9 7.9 %all-to-all-done.3 = bf16[4,130,128]{2,1,0:T(8,128)(2,1)S(1)} async-done(((bf16[4,130,128]{2,1,0:T(8,128)(2,1)}), bf16[4,130,128]{2,1,0:T(8,128)(2,1)S(1)}, u32[]{:S(2)}, u32[]{:S(2)}) %all-to-all-start.3) | async-done | bytes 133152 | tf_op jit(solution)/shard_map/all_to_all | solution.py:202
  (62 shorter events, 25.6 us)
Async XLA Ops:
  2.1 0.7 copy-start
  37.6 4.4 %collective-permute-start = (bf16[320,1536]{1,0:T(8,128)(2,1)S(1)}, bf16[320,1536]{1,0:T(8,128)(2,1)S(1)}, u32[]{:S(2)}, u32[]{:S(2)}) collective-permute-start(bf16[320,1536]{1,0:T(8,128)(2,1)S(1)} %bitcast.7), channel_id=1, source_target_pairs={{0,8},{8,0},{16,24},{24,16},{32,40},{40,32},{48,56},{56,48},{64,72... | collective-permute-start | bytes 2949128 | tf_op jit(solution)/shard_map/ppermute | solution.py:207
  42.0 1.1 copy-start.2
  43.2 1.1 copy-start.4
  44.3 1.1 copy-start.6
  49.4 20.6 %collective-permute-start.3 = (bf16[80,1536]{1,0:T(8,128)(2,1)}, bf16[80,1536]{1,0:T(8,128)(2,1)S(1)}, u32[]{:S(2)}, u32[]{:S(2)}) collective-permute-start(bf16[80,1536]{1,0:T(8,128)(2,1)} %get-tuple-element.28), channel_id=1, source_target_pairs={{0,1},{1,2},{2,3},{3,4},{4,5},{5,6},{6,7},{7,0},{8,9},{9,10},{10,1... | collective-permute-start | bytes 737288 | tf_op jit(solution)/shard_map/ppermute | solution.py:211
  53.7 16.3 %collective-permute-start.4 = (bf16[80,1536]{1,0:T(8,128)(2,1)}, bf16[80,1536]{1,0:T(8,128)(2,1)S(1)}, u32[]{:S(2)}, u32[]{:S(2)}) collective-permute-start(bf16[80,1536]{1,0:T(8,128)(2,1)} %get-tuple-element.30), channel_id=1, source_target_pairs={{0,7},{1,0},{2,1},{3,2},{4,3},{5,4},{6,5},{7,6},{8,15},{9,8},{10,9... | collective-permute-start | bytes 737288 | tf_op jit(solution)/shard_map/ppermute | solution.py:211
  55.6 14.7 %collective-permute-start.5 = (bf16[80,1536]{1,0:T(8,128)(2,1)}, bf16[80,1536]{1,0:T(8,128)(2,1)S(1)}, u32[]{:S(2)}, u32[]{:S(2)}) collective-permute-start(bf16[80,1536]{1,0:T(8,128)(2,1)} %get-tuple-element.31), channel_id=1, source_target_pairs={{0,2},{1,3},{2,4},{3,5},{4,6},{5,7},{6,0},{7,1},{8,14},{9,15},{10,... | collective-permute-start | bytes 737288 | tf_op jit(solution)/shard_map/ppermute | solution.py:219
  62.9 18.8 %collective-permute-start.1 = (bf16[80,1536]{1,0:T(8,128)(2,1)}, bf16[80,1536]{1,0:T(8,128)(2,1)S(1)}, u32[]{:S(2)}, u32[]{:S(2)}) collective-permute-start(bf16[80,1536]{1,0:T(8,128)(2,1)} %copy-done.9), channel_id=1, source_target_pairs={{0,1},{1,2},{2,3},{3,4},{4,5},{5,6},{6,7},{7,0},{8,9},{9,10},{10,1... | collective-permute-start | bytes 737288 | tf_op jit(solution)/shard_map/ppermute | solution.py:211
  68.1 13.7 %collective-permute-start.2 = (bf16[80,1536]{1,0:T(8,128)(2,1)}, bf16[80,1536]{1,0:T(8,128)(2,1)S(1)}, u32[]{:S(2)}, u32[]{:S(2)}) collective-permute-start(bf16[80,1536]{1,0:T(8,128)(2,1)} %copy-done.8), channel_id=1, source_target_pairs={{0,7},{1,0},{2,1},{3,2},{4,3},{5,4},{6,5},{7,6},{8,15},{9,8},{10,9... | collective-permute-start | bytes 737288 | tf_op jit(solution)/shard_map/ppermute | solution.py:211
  70.5 14.7 %collective-permute-start.6 = (bf16[80,1536]{1,0:T(8,128)(2,1)S(1)}, bf16[80,1536]{1,0:T(8,128)(2,1)S(1)}, u32[]{:S(2)}, u32[]{:S(2)}) collective-permute-start(bf16[80,1536]{1,0:T(8,128)(2,1)S(1)} %get-tuple-element.32), channel_id=1, source_target_pairs={{0,2},{1,3},{2,4},{3,5},{4,6},{5,7},{6,0},{7,1},{8,10},{9,11},{10,... | collective-permute-start | bytes 737288 | tf_op jit(solution)/shard_map/ppermute | solution.py:211
  76.0 14.7 %collective-permute-start.7 = (bf16[80,1536]{1,0:T(8,128)(2,1)S(1)}, bf16[80,1536]{1,0:T(8,128)(2,1)S(1)}, u32[]{:S(2)}, u32[]{:S(2)}) collective-permute-start(bf16[80,1536]{1,0:T(8,128)(2,1)S(1)} %get-tuple-element.33), channel_id=1, source_target_pairs={{0,6},{1,7},{2,0},{3,1},{4,2},{5,3},{6,4},{7,5},{8,14},{9,15},{10,... | collective-permute-start | bytes 737288 | tf_op jit(solution)/shard_map/ppermute | solution.py:211
  91.0 17.7 %collective-permute-start.11 = (bf16[80,1664]{1,0:T(8,128)(2,1)S(1)}, bf16[80,1664]{1,0:T(8,128)(2,1)S(1)}, u32[]{:S(2)}, u32[]{:S(2)}) collective-permute-start(bf16[80,1664]{1,0:T(8,128)(2,1)S(1)} %shard_map.121.rest_0_), channel_id=1, source_target_pairs={{0,2},{1,3},{2,4},{3,5},{4,6},{5,7},{6,0},{7,1},{8,10},{9,11},{10,... | collective-permute-start | bytes 798728 | tf_op jit(solution)/shard_map/ppermute | solution.py:211
  96.7 15.9 %collective-permute-start.9 = (bf16[80,1664]{1,0:T(8,128)(2,1)S(1)}, bf16[80,1664]{1,0:T(8,128)(2,1)S(1)}, u32[]{:S(2)}, u32[]{:S(2)}) collective-permute-start(bf16[80,1664]{1,0:T(8,128)(2,1)S(1)} %shard_map.121.rest_0_), channel_id=1, source_target_pairs={{0,6},{1,7},{2,0},{3,1},{4,2},{5,3},{6,4},{7,5},{8,14},{9,15},{10,... | collective-permute-start | bytes 798728 | tf_op jit(solution)/shard_map/ppermute | solution.py:211
  99.4 19.0 %collective-permute-start.14 = (bf16[80,1664]{1,0:T(8,128)(2,1)S(1)}, bf16[80,1664]{1,0:T(8,128)(2,1)S(1)}, u32[]{:S(2)}, u32[]{:S(2)}) collective-permute-start(bf16[80,1664]{1,0:T(8,128)(2,1)S(1)} %shard_map.121.rest_0_), channel_id=1, source_target_pairs={{0,1},{1,2},{2,3},{3,4},{4,5},{5,6},{6,7},{7,0},{8,9},{9,10},{10,1... | collective-permute-start | bytes 798728 | tf_op jit(solution)/shard_map/ppermute | solution.py:211
  103.7 14.7 %collective-permute-start.8 = (bf16[80,1664]{1,0:T(8,128)(2,1)S(1)}, bf16[80,1664]{1,0:T(8,128)(2,1)S(1)}, u32[]{:S(2)}, u32[]{:S(2)}) collective-permute-start(bf16[80,1664]{1,0:T(8,128)(2,1)S(1)} %shard_map.121.rest_0_), channel_id=1, source_target_pairs={{0,7},{1,0},{2,1},{3,2},{4,3},{5,4},{6,5},{7,6},{8,15},{9,8},{10,9... | collective-permute-start | bytes 798728 | tf_op jit(solution)/shard_map/ppermute | solution.py:211
  108.7 12.0 %collective-permute-start.13 = (bf16[80,1664]{1,0:T(8,128)(2,1)S(1)}, bf16[80,1664]{1,0:T(8,128)(2,1)S(1)}, u32[]{:S(2)}, u32[]{:S(2)}) collective-permute-start(bf16[80,1664]{1,0:T(8,128)(2,1)S(1)} %collective-permute-done.11.rest_6_), channel_id=1, source_target_pairs={{0,1},{1,2},{2,3},{3,4},{4,5},{5,6},{6,7},{7,0},{8,9},{9,10},{10,1... | collective-permute-start | bytes 798728 | tf_op jit(solution)/shard_map/ppermute | solution.py:211
  112.6 12.2 %collective-permute-start.12 = (bf16[80,1664]{1,0:T(8,128)(2,1)S(1)}, bf16[80,1664]{1,0:T(8,128)(2,1)S(1)}, u32[]{:S(2)}, u32[]{:S(2)}) collective-permute-start(bf16[80,1664]{1,0:T(8,128)(2,1)S(1)} %broadcast_select_fusion), channel_id=1, source_target_pairs={{0,6},{1,7},{2,0},{3,1},{4,2},{5,3},{6,4},{7,5},{8,10},{9,11},{10,... | collective-permute-start | bytes 798728 | tf_op jit(solution)/shard_map/ppermute | solution.py:219
  116.4 10.8 %collective-permute-start.10 = (bf16[80,1664]{1,0:T(8,128)(2,1)S(1)}, bf16[80,1664]{1,0:T(8,128)(2,1)S(1)}, u32[]{:S(2)}, u32[]{:S(2)}) collective-permute-start(bf16[80,1664]{1,0:T(8,128)(2,1)S(1)} %collective-permute-done.9.rest_2_), channel_id=1, source_target_pairs={{0,7},{1,0},{2,1},{3,2},{4,3},{5,4},{6,5},{7,6},{8,15},{9,8},{10,9... | collective-permute-start | bytes 798728 | tf_op jit(solution)/shard_map/ppermute | solution.py:211
  127.2 1.1 copy-start.3
  128.4 1.1 copy-start.5
  129.5 1.1 copy-start.7
  132.5 6.2 %copy-start.10 = (bf16[640,512]{1,0:T(8,128)(2,1)}, bf16[640,512]{1,0:T(8,128)(2,1)S(1)}, u32[]{:S(2)}) copy-start(bf16[640,512]{1,0:T(8,128)(2,1)S(1)} %get-tuple-element.40) | copy-start | bytes 1966084
  132.5 6.2 %copy-start.12 = (bf16[640,512]{1,0:T(8,128)(2,1)}, bf16[640,512]{1,0:T(8,128)(2,1)S(1)}, u32[]{:S(2)}) copy-start(bf16[640,512]{1,0:T(8,128)(2,1)S(1)} %get-tuple-element.39) | copy-start | bytes 1966084
  132.5 6.2 %copy-start.14 = (bf16[640,512]{1,0:T(8,128)(2,1)}, bf16[640,512]{1,0:T(8,128)(2,1)S(1)}, u32[]{:S(2)}) copy-start(bf16[640,512]{1,0:T(8,128)(2,1)S(1)} %get-tuple-element.38) | copy-start | bytes 1966084
  132.5 4.6 %collective-permute-start.15 = (bf16[320,1664]{1,0:T(8,128)(2,1)S(1)}, bf16[320,1664]{1,0:T(8,128)(2,1)S(1)}, u32[]{:S(2)}, u32[]{:S(2)}) collective-permute-start(bf16[320,1664]{1,0:T(8,128)(2,1)S(1)} %get-tuple-element.35), channel_id=1, source_target_pairs={{0,8},{8,0},{16,24},{24,16},{32,40},{40,32},{48,56},{56,48},{64,72... | collective-permute-start | bytes 3194888 | tf_op jit(solution)/shard_map/ppermute | solution.py:207
  138.7 19.0 %all-to-all-start.2 = ((bf16[8,40,1664]{2,1,0:T(8,128)(2,1)}), bf16[8,40,1664]{2,1,0:T(8,128)(2,1)S(1)}, u32[]{:S(2)}, u32[]{:S(2)}) async-start(bf16[8,40,1664]{2,1,0:T(8,128)(2,1)} %bitcast.3), calls=%async_computation.2 | async-start | bytes 2129920 | tf_op jit(solution)/shard_map/all_to_all | solution.py:202
  142.4 1.3 copy-start.15
  143.6 1.7 copy-start.13
  147.0 15.2 %copy-start.11 = (bf16[640,512]{1,0:T(8,128)(2,1)S(1)}, bf16[640,512]{1,0:T(8,128)(2,1)}, u32[]{:S(2)}) copy-start(bf16[640,512]{1,0:T(8,128)(2,1)} %copy-done.10) | copy-start | bytes 1966084
  147.0 15.2 %copy-start.16 = (bf16[320,768]{1,0:T(8,128)(2,1)S(1)}, bf16[320,768]{1,0:T(8,128)(2,1)}, u32[]{:S(2)}) copy-start(bf16[320,768]{1,0:T(8,128)(2,1)} %get-tuple-element.56) | copy-start | bytes 1474564
  158.8 12.9 %all-to-all-start.3 = ((bf16[4,130,128]{2,1,0:T(8,128)(2,1)}), bf16[4,130,128]{2,1,0:T(8,128)(2,1)S(1)}, u32[]{:S(2)}, u32[]{:S(2)}) async-start(bf16[4,130,128]{2,1,0:T(8,128)(2,1)} %reshape.41), calls=%async_computation.3 | async-start | bytes 278528 | tf_op jit(solution)/shard_map/all_to_all | solution.py:202
  (3 other events, 2.1 us)

commit v5 on v4

--- a/solution.py
+++ b/solution.py
@@ -52,6 +52,17 @@
     slots_ref[:, width:] = (
         contract(masks[0], cots[0], 0, 0) + contract(masks[1], cots[1], 0, 0)
     ).astype(jnp.bfloat16)
+
+
+def load_kernel(*refs):
+    count = len(refs) // 2
+    copies = [
+        pltpu.make_async_copy(refs[i], refs[count + i], refs[2 * count].at[i]) for i in range(count)
+    ]
+    for copy in copies:
+        copy.start()
+    for copy in copies:
+        copy.wait()
 
 
 def parts_kernel(plane_ref, near_ref, far_ref, gate_ref, up_ref, down_ref, *rest):
@@ -254,6 +265,18 @@
         return back.reshape(EXPERTS * MOST, -1)
 
     bf16 = jnp.bfloat16
+    def load(weights, earlier):
+        return pl.pallas_call(
+            load_kernel,
+            out_shape=[pltpu.VMEM(w.shape, w.dtype) for w in weights],
+            in_specs=[pl.BlockSpec(memory_space=pl.ANY)] * len(weights),
+            out_specs=[VMEM] * len(weights),
+            scratch_shapes=[pltpu.SemaphoreType.DMA((len(weights),))],
+            compiler_params=PARAMS,
+            cost_estimate=pl.CostEstimate(flops=0, bytes_accessed=4 << 20, transcendentals=0),
+        )(*lax.optimization_barrier((*weights, earlier))[:-1])
+
+    weights = [w_gate, w_up, w_down]
     [slots] = call(
         pack_kernel,
         [(EXPERTS * MOST, 2 * width)],
@@ -265,18 +288,19 @@
         parts_kernel,
         [(own, 3 * hidden_width)] * planes,
         [plane],
-        [near, far, w_gate, w_up, w_down],
+        [near, far, *load(weights, near)],
         scratch=[pltpu.VMEM((rows, 3 * hidden_width), bf16)],
         flops=6 * rows * width * hidden_width,
     )
     arrived = jnp.concatenate([near[:, :width], far[:, :width]], axis=0)
     arrived_cot = jnp.concatenate([near[:, width:], far[:, width:]], axis=0)
     [value] = call(hidden_kernel, [(own, 3 * hidden_width + LANES)], [], relay(chunks))
+    pieces = to_all_planes(value)
     near_part, far_part, hidden, gate_cot, up_cot = call(
         back_kernel,
         [(half, 2 * width + LANES)] * 2 + [(rows, hidden_width)] * 3,
         [plane],
-        [w_gate, w_up, w_down, *to_all_planes(value)],
+        [*load(weights, pieces[2]), *pieces],
         scratch=[pltpu.VMEM((rows, LANES), bf16)],
         flops=6 * rows * width * hidden_width,
     )

time: 175 us -> 172 us (0.983)
  waiting for transfers between devices: 46.9 us -> 42.8 us
  Pallas kernels: 8.22 us -> 11.1 us
  local copies, waits for them, and re-layouts: 14.6 us -> 12.5 us
    unnamed x37 -> x31, local copies, waits for them, and re-layouts: 12.2 us -> 8.14 us
    pallas_call x7, Pallas kernels: 7.19 us -> 9.66 us  [call(): pl.pallas_call(kernel, out_shape=[pltpu.VMEM(shape, jnp.bfloat16) for sha...]
    slice x2, local copies, waits for them, and re-layouts: 0.93 us -> 2.95 us  [on_device(): arrived_cot = jnp.concatenate([near[:, width:], far[:, width:]], axis=0)]
  transfers between devices with their start and end apart: 18 -> 18, of which waited for: 12 -> 12; matrix products, arithmetic and copies ran while one was open for 3% -> 5% of each run, Pallas kernels for 0% -> 1%
where the time goes in v5:
time: 172 us; the launch traced here: 170 us
  starting transfers between devices  64.7 us (38%)
  waiting for transfers between devices  42.8 us (25%)
  blocking collectives  33.3 us (19%)
  local copies, waits for them, and re-layouts  12.5 us (7%)
  Pallas kernels  11.1 us (6%)
  matrix products  5.06 us (3%)
    ppermute x12, starting transfers between devices, shift(): return lax.ppermute(value, 'fsdp', pairs)  42.9 us
    all_to_all x2, blocking collectives, across(): lax.all_to_all(blocks, 'expert', split_axis=0, concat_axis=0, axis_index_...  33.3 us
    ppermute x12, waiting for transfers between devices, shift(): return lax.ppermute(value, 'fsdp', pairs)  17.5 us
    all_to_all x2, waiting for transfers between devices, across(): lax.all_to_all(blocks, 'expert', split_axis=0, concat_axis=0, axis_index_...  17 us
    ppermute x2, starting transfers between devices, shift_by_core(): return lax.ppermute(value, ('expert', 'fsdp'), pairs)  11.1 us
    pallas_call x7, Pallas kernels, call(): pl.pallas_call(kernel, out_shape=[pltpu.VMEM(shape, jnp.bfloat16) for sha...  9.66 us
    unnamed x31, local copies, waits for them, and re-layouts  8.14 us
    all_to_all x2, starting transfers between devices, across(): lax.all_to_all(blocks, 'expert', split_axis=0, concat_axis=0, axis_index_...  6.89 us
  transfers between devices with their start and end apart: 18, of which 12 were waited for; matrix products, arithmetic and copies ran while one was open for 5% of the time, Pallas kernels for 1%

profile of v5, /device:TPU:64, one launch (start us, length us, event | category | flops | bytes accessed | tf_op | source)
XLA Modules:
  0.0 170.5 jit_solution(17484144457440836948)
XLA Ops:
  4.2 15.7 %all_to_all.20 = bf16[4,120,128]{2,1,0:T(8,128)(2,1)S(1)} all-to-all(bf16[4,120,128]{2,1,0:T(8,128)(2,1)S(1)} %reshape.37), channel_id=1, replica_groups={{0,128,256,384},{8,136,264,392},{16,144,272,400},{24,152,280,408},{32,1..., dimensions={0} | all-to-all | bytes 245760 | tf_op jit(solution)/shard_map/all_to_all | solution.py:213
  20.2 17.5 %all_to_all.21 = bf16[8,40,1536]{2,1,0:T(8,128)(2,1)S(1)} all-to-all(bf16[8,40,1536]{2,1,0:T(8,128)(2,1)S(1)} %broadcast_in_dim.8), channel_id=1, replica_groups={{0,16,32,48,64,80,96,112},{8,24,40,56,72,88,104,120},{128,144,160,176,1..., dimensions={0} | all-to-all | bytes 1966080 | tf_op jit(solution)/shard_map/all_to_all | solution.py:213
  37.8 1.9 %collective-permute-start = (bf16[320,1536]{1,0:T(8,128)(2,1)S(1)}, bf16[320,1536]{1,0:T(8,128)(2,1)}, u32[]{:S(2)}, u32[]{:S(2)}) collective-permute-start(bf16[320,1536]{1,0:T(8,128)(2,1)S(1)} %bitcast.7), channel_id=1, source_target_pairs={{0,8},{8,0},{16,24},{24,16},{32,40},{40,32},{48,56},{56,48},{64,72... | collective-permute-start | bytes 2949128 | tf_op jit(solution)/shard_map/ppermute | solution.py:218
  42.3 3.8 %shard_map.120 = (bf16[80,1536]{1,0:T(8,128)(2,1)S(1)}, bf16[80,1536]{1,0:T(8,128)(2,1)S(1)}, bf16[80,1536]{1,0:T(8,128)(2,1)S(1)}, bf16[80,1536]{1,0:T(8,128)(2...) custom-call(s32[1]{0:T(128)} %bitcast.plane_ref, ...), custom_call_target="tpu_custom_call" | custom-call | flops 1509949440 | bytes 4194304 | tf_op jit(solution)/shard_map/pallas_call | solution.py:166
  47.6 4.3 %collective-permute-start.3 = (bf16[80,1536]{1,0:T(8,128)(2,1)}, bf16[80,1536]{1,0:T(8,128)(2,1)}, u32[]{:S(2)}, u32[]{:S(2)}) collective-permute-start(bf16[80,1536]{1,0:T(8,128)(2,1)} %get-tuple-element.46), channel_id=1, source_target_pairs={{0,1},{1,2},{2,3},{3,4},{4,5},{5,6},{6,7},{7,0},{8,9},{9,10},{10,1... | collective-permute-start | bytes 737288 | tf_op jit(solution)/shard_map/ppermute | solution.py:222
  51.9 1.9 %collective-permute-start.4 = (bf16[80,1536]{1,0:T(8,128)(2,1)}, bf16[80,1536]{1,0:T(8,128)(2,1)}, u32[]{:S(2)}, u32[]{:S(2)}) collective-permute-start(bf16[80,1536]{1,0:T(8,128)(2,1)} %get-tuple-element.48), channel_id=1, source_target_pairs={{0,7},{1,0},{2,1},{3,2},{4,3},{5,4},{6,5},{7,6},{8,15},{9,8},{10,9... | collective-permute-start | bytes 737288 | tf_op jit(solution)/shard_map/ppermute | solution.py:222
  53.8 7.3 %collective-permute-start.5 = (bf16[80,1536]{1,0:T(8,128)(2,1)}, bf16[80,1536]{1,0:T(8,128)(2,1)}, u32[]{:S(2)}, u32[]{:S(2)}) collective-permute-start(bf16[80,1536]{1,0:T(8,128)(2,1)} %get-tuple-element.49), channel_id=1, source_target_pairs={{0,2},{1,3},{2,4},{3,5},{4,6},{5,7},{6,0},{7,1},{8,14},{9,15},{10,... | collective-permute-start | bytes 737288 | tf_op jit(solution)/shard_map/ppermute | solution.py:230
  61.1 5.1 %collective-permute-start.1 = (bf16[80,1536]{1,0:T(8,128)(2,1)}, bf16[80,1536]{1,0:T(8,128)(2,1)S(1)}, u32[]{:S(2)}, u32[]{:S(2)}) collective-permute-start(bf16[80,1536]{1,0:T(8,128)(2,1)} %copy-done.7), channel_id=1, source_target_pairs={{0,1},{1,2},{2,3},{3,4},{4,5},{5,6},{6,7},{7,0},{8,9},{9,10},{10,1... | collective-permute-start | bytes 737288 | tf_op jit(solution)/shard_map/ppermute | solution.py:222
  66.2 1.9 %collective-permute-start.2 = (bf16[80,1536]{1,0:T(8,128)(2,1)}, bf16[80,1536]{1,0:T(8,128)(2,1)S(1)}, u32[]{:S(2)}, u32[]{:S(2)}) collective-permute-start(bf16[80,1536]{1,0:T(8,128)(2,1)} %copy-done.6), channel_id=1, source_target_pairs={{0,7},{1,0},{2,1},{3,2},{4,3},{5,4},{6,5},{7,6},{8,15},{9,8},{10,9... | collective-permute-start | bytes 737288 | tf_op jit(solution)/shard_map/ppermute | solution.py:222
  69.9 5.5 %collective-permute-start.6 = (bf16[80,1536]{1,0:T(8,128)(2,1)S(1)}, bf16[80,1536]{1,0:T(8,128)(2,1)S(1)}, u32[]{:S(2)}, u32[]{:S(2)}) collective-permute-start(bf16[80,1536]{1,0:T(8,128)(2,1)S(1)} %get-tuple-element.50), channel_id=1, source_target_pairs={{0,2},{1,3},{2,4},{3,5},{4,6},{5,7},{6,0},{7,1},{8,10},{9,11},{10,... | collective-permute-start | bytes 737288 | tf_op jit(solution)/shard_map/ppermute | solution.py:222
  75.5 5.7 %collective-permute-start.7 = (bf16[80,1536]{1,0:T(8,128)(2,1)S(1)}, bf16[80,1536]{1,0:T(8,128)(2,1)S(1)}, u32[]{:S(2)}, u32[]{:S(2)}) collective-permute-start(bf16[80,1536]{1,0:T(8,128)(2,1)S(1)} %get-tuple-element.51), channel_id=1, source_target_pairs={{0,6},{1,7},{2,0},{3,1},{4,2},{5,3},{6,4},{7,5},{8,14},{9,15},{10,... | collective-permute-start | bytes 737288 | tf_op jit(solution)/shard_map/ppermute | solution.py:222
  81.2 7.4 %collective-permute-done.6.d_ref = bf16[80,1536]{1,0:T(8,128)(2,1)S(1)} collective-permute-done((bf16[80,1536]{1,0:T(8,128)(2,1)S(1)}, bf16[80,1536]{1,0:T(8,128)(2,1)S(1)}, u32[]{:S(2)}, u32[]{:S(2)}) %collective-permute-start.6) | collective-permute-done | bytes 245792 | tf_op jit(solution)/shard_map/ppermute | solution.py:222
  90.4 5.7 %collective-permute-start.11 = (bf16[80,1664]{1,0:T(8,128)(2,1)S(1)}, bf16[80,1664]{1,0:T(8,128)(2,1)S(1)}, u32[]{:S(2)}, u32[]{:S(2)}) collective-permute-start(bf16[80,1664]{1,0:T(8,128)(2,1)S(1)} %shard_map.122.rest_0_), channel_id=1, source_target_pairs={{0,2},{1,3},{2,4},{3,5},{4,6},{5,7},{6,0},{7,1},{8,10},{9,11},{10,... | collective-permute-start | bytes 798728 | tf_op jit(solution)/shard_map/ppermute | solution.py:222
  96.2 2.7 %collective-permute-start.8 = (bf16[80,1664]{1,0:T(8,128)(2,1)S(1)}, bf16[80,1664]{1,0:T(8,128)(2,1)S(1)}, u32[]{:S(2)}, u32[]{:S(2)}) collective-permute-start(bf16[80,1664]{1,0:T(8,128)(2,1)S(1)} %shard_map.122.rest_0_), channel_id=1, source_target_pairs={{0,6},{1,7},{2,0},{3,1},{4,2},{5,3},{6,4},{7,5},{8,14},{9,15},{10,... | collective-permute-start | bytes 798728 | tf_op jit(solution)/shard_map/ppermute | solution.py:222
  98.8 4.3 %collective-permute-start.14 = (bf16[80,1664]{1,0:T(8,128)(2,1)S(1)}, bf16[80,1664]{1,0:T(8,128)(2,1)S(1)}, u32[]{:S(2)}, u32[]{:S(2)}) collective-permute-start(bf16[80,1664]{1,0:T(8,128)(2,1)S(1)} %shard_map.122.rest_0_), channel_id=1, source_target_pairs={{0,1},{1,2},{2,3},{3,4},{4,5},{5,6},{6,7},{7,0},{8,9},{9,10},{10,1... | collective-permute-start | bytes 798728 | tf_op jit(solution)/shard_map/ppermute | solution.py:222
  103.1 1.9 %collective-permute-start.9 = (bf16[80,1664]{1,0:T(8,128)(2,1)S(1)}, bf16[80,1664]{1,0:T(8,128)(2,1)S(1)}, u32[]{:S(2)}, u32[]{:S(2)}) collective-permute-start(bf16[80,1664]{1,0:T(8,128)(2,1)S(1)} %shard_map.122.rest_0_), channel_id=1, source_target_pairs={{0,7},{1,0},{2,1},{3,2},{4,3},{5,4},{6,5},{7,6},{8,15},{9,8},{10,9... | collective-permute-start | bytes 798728 | tf_op jit(solution)/shard_map/ppermute | solution.py:222
  105.1 3.1 %collective-permute-done.11.rest_6_ = bf16[80,1664]{1,0:T(8,128)(2,1)S(1)} collective-permute-done((bf16[80,1664]{1,0:T(8,128)(2,1)S(1)}, bf16[80,1664]{1,0:T(8,128)(2,1)S(1)}, u32[]{:S(2)}, u32[]{:S(2)}) %collective-permute-start.11) | collective-permute-done | bytes 266272 | tf_op jit(solution)/shard_map/ppermute | solution.py:222
  108.2 1.9 %collective-permute-start.13 = (bf16[80,1664]{1,0:T(8,128)(2,1)S(1)}, bf16[80,1664]{1,0:T(8,128)(2,1)S(1)}, u32[]{:S(2)}, u32[]{:S(2)}) collective-permute-start(bf16[80,1664]{1,0:T(8,128)(2,1)S(1)} %collective-permute-done.11.rest_6_), channel_id=1, source_target_pairs={{0,1},{1,2},{2,3},{3,4},{4,5},{5,6},{6,7},{7,0},{8,9},{9,10},{10,1... | collective-permute-start | bytes 798728 | tf_op jit(solution)/shard_map/ppermute | solution.py:222
  110.1 2.0 %collective-permute-done.8.rest_2_ = bf16[80,1664]{1,0:T(8,128)(2,1)S(1)} collective-permute-done((bf16[80,1664]{1,0:T(8,128)(2,1)S(1)}, bf16[80,1664]{1,0:T(8,128)(2,1)S(1)}, u32[]{:S(2)}, u32[]{:S(2)}) %collective-permute-start.8) | collective-permute-done | bytes 266272 | tf_op jit(solution)/shard_map/ppermute | solution.py:222
  112.1 3.8 %collective-permute-start.12 = (bf16[80,1664]{1,0:T(8,128)(2,1)S(1)}, bf16[80,1664]{1,0:T(8,128)(2,1)S(1)}, u32[]{:S(2)}, u32[]{:S(2)}) collective-permute-start(bf16[80,1664]{1,0:T(8,128)(2,1)S(1)} %broadcast_select_fusion), channel_id=1, source_target_pairs={{0,6},{1,7},{2,0},{3,1},{4,2},{5,3},{6,4},{7,5},{8,10},{9,11},{10,... | collective-permute-start | bytes 798728 | tf_op jit(solution)/shard_map/ppermute | solution.py:230
  115.9 1.9 %collective-permute-start.10 = (bf16[80,1664]{1,0:T(8,128)(2,1)S(1)}, bf16[80,1664]{1,0:T(8,128)(2,1)S(1)}, u32[]{:S(2)}, u32[]{:S(2)}) collective-permute-start(bf16[80,1664]{1,0:T(8,128)(2,1)S(1)} %collective-permute-done.8.rest_2_), channel_id=1, source_target_pairs={{0,7},{1,0},{2,1},{3,2},{4,3},{5,4},{6,5},{7,6},{8,15},{9,8},{10,9... | collective-permute-start | bytes 798728 | tf_op jit(solution)/shard_map/ppermute | solution.py:222
  120.2 4.1 %collective-permute-done.12.rest_4_ = bf16[80,1664]{1,0:T(8,128)(2,1)S(1)} collective-permute-done((bf16[80,1664]{1,0:T(8,128)(2,1)S(1)}, bf16[80,1664]{1,0:T(8,128)(2,1)S(1)}, u32[]{:S(2)}, u32[]{:S(2)}) %collective-permute-start.12) | collective-permute-done | bytes 266272 | tf_op jit(solution)/shard_map/ppermute | solution.py:230
  124.3 2.4 %collective-permute-done.10.rest_3_ = bf16[80,1664]{1,0:T(8,128)(2,1)S(1)} collective-permute-done((bf16[80,1664]{1,0:T(8,128)(2,1)S(1)}, bf16[80,1664]{1,0:T(8,128)(2,1)S(1)}, u32[]{:S(2)}, u32[]{:S(2)}) %collective-permute-start.10) | collective-permute-done | bytes 266272 | tf_op jit(solution)/shard_map/ppermute | solution.py:222
  126.7 1.8 %shard_map.124 = (bf16[320,1664]{1,0:T(8,128)(2,1)S(1)}, bf16[320,1664]{1,0:T(8,128)(2,1)S(1)}, bf16[640,512]{1,0:T(8,128)(2,1)S(1)}, bf16[640,512]{1,0:T(8,128)(2,1)S(1)}, bf16[640,512]{1,0:T(8,128)(2,1)S(1)}) custom-call(s32[1]{0:T(128)} %bitcast.plane_ref, bf16[768,512]{1,0:T(8,128)(2,1)S(1)} %get-tuple-element.55.gate_ref, ...), custom_call_target="tpu_custom_call" | custom-call | flops 1509949440 | bytes 4194304 | tf_op jit(solution)/shard_map/pallas_call | solution.py:166
  129.4 1.9 %collective-permute-start.15 = (bf16[320,1664]{1,0:T(8,128)(2,1)S(1)}, bf16[320,1664]{1,0:T(8,128)(2,1)S(1)}, u32[]{:S(2)}, u32[]{:S(2)}) collective-permute-start(bf16[320,1664]{1,0:T(8,128)(2,1)S(1)} %get-tuple-element.59), channel_id=1, source_target_pairs={{0,8},{8,0},{16,24},{24,16},{32,40},{40,32},{48,56},{56,48},{64,72... | collective-permute-start | bytes 3194888 | tf_op jit(solution)/shard_map/ppermute | solution.py:218
  131.3 2.6 %collective-permute-done.15.far_ref = bf16[320,1664]{1,0:T(8,128)(2,1)S(1)} collective-permute-done((bf16[320,1664]{1,0:T(8,128)(2,1)S(1)}, bf16[320,1664]{1,0:T(8,128)(2,1)S(1)}, u32[]{:S(2)}, u32[]{:S(2)}) %collective-permute-start.15) | collective-permute-done | bytes 1064992 | tf_op jit(solution)/shard_map/ppermute | solution.py:218
  135.6 3.6 %all-to-all-start.2 = ((bf16[8,40,1664]{2,1,0:T(8,128)(2,1)}), bf16[8,40,1664]{2,1,0:T(8,128)(2,1)S(1)}, u32[]{:S(2)}, u32[]{:S(2)}) async-start(bf16[8,40,1664]{2,1,0:T(8,128)(2,1)} %bitcast.3), calls=%async_computation.2 | async-start | bytes 2129920 | tf_op jit(solution)/shard_map/all_to_all | solution.py:213
  140.0 2.1 %fusion.7 = (bf16[320,768]{1,0:T(8,128)(2,1)}, bf16[320,768]{1,0:T(8,128)(2,1)S(1)}) fusion(bf16[320,1536]{1,0:T(8,128)(2,1)} %collective-permute-done.far_ref), kind=kLoop, calls=%fused_computation.12 | loop fusion | bytes 1966080 | tf_op jit(solution)/shard_map/slice | solution.py:296
  145.5 9.1 %all-to-all-done.2.blocks_ref = bf16[8,40,1664]{2,1,0:T(8,128)(2,1)S(1)} async-done(((bf16[8,40,1664]{2,1,0:T(8,128)(2,1)}), bf16[8,40,1664]{2,1,0:T(8,128)(2,1)S(1)}, u32[]{:S(2)}, u32[]{:S(2)}) %all-to-all-start.2) | async-done | bytes 1064992 | tf_op jit(solution)/shard_map/all_to_all | solution.py:213
  155.7 3.3 %all-to-all-start.3 = ((bf16[4,130,128]{2,1,0:T(8,128)(2,1)}), bf16[4,130,128]{2,1,0:T(8,128)(2,1)S(1)}, u32[]{:S(2)}, u32[]{:S(2)}) async-start(bf16[4,130,128]{2,1,0:T(8,128)(2,1)} %reshape.41), calls=%async_computation.3 | async-start | bytes 278528 | tf_op jit(solution)/shard_map/all_to_all | solution.py:213
  159.1 1.7 convolution_convert_fusion
  160.8 7.9 %all-to-all-done.3 = bf16[4,130,128]{2,1,0:T(8,128)(2,1)S(1)} async-done(((bf16[4,130,128]{2,1,0:T(8,128)(2,1)}), bf16[4,130,128]{2,1,0:T(8,128)(2,1)S(1)}, u32[]{:S(2)}, u32[]{:S(2)}) %all-to-all-start.3) | async-done | bytes 133152 | tf_op jit(solution)/shard_map/all_to_all | solution.py:213
  (58 shorter events, 23.4 us)
Async XLA Ops:
  2.1 0.7 copy-start.4
  2.9 0.7 copy-start.5
  20.2 19.5 %copy-start = (bf16[768,512]{1,0:T(8,128)(2,1)S(1)}, bf16[768,512]{1,0:T(8,128)(2,1)}, u32[]{:S(2)}) copy-start(bf16[768,512]{1,0:T(8,128)(2,1)} %refs_0_.1) | copy-start | bytes 2359300
  20.2 19.5 %copy-start.1 = (bf16[768,512]{1,0:T(8,128)(2,1)S(1)}, bf16[768,512]{1,0:T(8,128)(2,1)}, u32[]{:S(2)}) copy-start(bf16[768,512]{1,0:T(8,128)(2,1)} %refs_1_.1) | copy-start | bytes 2359300
  37.8 4.6 %collective-permute-start = (bf16[320,1536]{1,0:T(8,128)(2,1)S(1)}, bf16[320,1536]{1,0:T(8,128)(2,1)}, u32[]{:S(2)}, u32[]{:S(2)}) collective-permute-start(bf16[320,1536]{1,0:T(8,128)(2,1)S(1)} %bitcast.7), channel_id=1, source_target_pairs={{0,8},{8,0},{16,24},{24,16},{32,40},{40,32},{48,56},{56,48},{64,72... | collective-permute-start | bytes 2949128 | tf_op jit(solution)/shard_map/ppermute | solution.py:218
  39.7 1.1 copy-start.2
  46.2 0.7 copy-start.6
  46.9 0.7 copy-start.7
  47.6 20.6 %collective-permute-start.3 = (bf16[80,1536]{1,0:T(8,128)(2,1)}, bf16[80,1536]{1,0:T(8,128)(2,1)}, u32[]{:S(2)}, u32[]{:S(2)}) collective-permute-start(bf16[80,1536]{1,0:T(8,128)(2,1)} %get-tuple-element.46), channel_id=1, source_target_pairs={{0,1},{1,2},{2,3},{3,4},{4,5},{5,6},{6,7},{7,0},{8,9},{9,10},{10,1... | collective-permute-start | bytes 737288 | tf_op jit(solution)/shard_map/ppermute | solution.py:222
  51.9 16.3 %collective-permute-start.4 = (bf16[80,1536]{1,0:T(8,128)(2,1)}, bf16[80,1536]{1,0:T(8,128)(2,1)}, u32[]{:S(2)}, u32[]{:S(2)}) collective-permute-start(bf16[80,1536]{1,0:T(8,128)(2,1)} %get-tuple-element.48), channel_id=1, source_target_pairs={{0,7},{1,0},{2,1},{3,2},{4,3},{5,4},{6,5},{7,6},{8,15},{9,8},{10,9... | collective-permute-start | bytes 737288 | tf_op jit(solution)/shard_map/ppermute | solution.py:222
  53.8 14.8 %collective-permute-start.5 = (bf16[80,1536]{1,0:T(8,128)(2,1)}, bf16[80,1536]{1,0:T(8,128)(2,1)}, u32[]{:S(2)}, u32[]{:S(2)}) collective-permute-start(bf16[80,1536]{1,0:T(8,128)(2,1)} %get-tuple-element.49), channel_id=1, source_target_pairs={{0,2},{1,3},{2,4},{3,5},{4,6},{5,7},{6,0},{7,1},{8,14},{9,15},{10,... | collective-permute-start | bytes 737288 | tf_op jit(solution)/shard_map/ppermute | solution.py:230
  61.1 20.1 %collective-permute-start.1 = (bf16[80,1536]{1,0:T(8,128)(2,1)}, bf16[80,1536]{1,0:T(8,128)(2,1)S(1)}, u32[]{:S(2)}, u32[]{:S(2)}) collective-permute-start(bf16[80,1536]{1,0:T(8,128)(2,1)} %copy-done.7), channel_id=1, source_target_pairs={{0,1},{1,2},{2,3},{3,4},{4,5},{5,6},{6,7},{7,0},{8,9},{9,10},{10,1... | collective-permute-start | bytes 737288 | tf_op jit(solution)/shard_map/ppermute | solution.py:222
  66.2 15.0 %collective-permute-start.2 = (bf16[80,1536]{1,0:T(8,128)(2,1)}, bf16[80,1536]{1,0:T(8,128)(2,1)S(1)}, u32[]{:S(2)}, u32[]{:S(2)}) collective-permute-start(bf16[80,1536]{1,0:T(8,128)(2,1)} %copy-done.6), channel_id=1, source_target_pairs={{0,7},{1,0},{2,1},{3,2},{4,3},{5,4},{6,5},{7,6},{8,15},{9,8},{10,9... | collective-permute-start | bytes 737288 | tf_op jit(solution)/shard_map/ppermute | solution.py:222
  69.9 18.7 %collective-permute-start.6 = (bf16[80,1536]{1,0:T(8,128)(2,1)S(1)}, bf16[80,1536]{1,0:T(8,128)(2,1)S(1)}, u32[]{:S(2)}, u32[]{:S(2)}) collective-permute-start(bf16[80,1536]{1,0:T(8,128)(2,1)S(1)} %get-tuple-element.50), channel_id=1, source_target_pairs={{0,2},{1,3},{2,4},{3,5},{4,6},{5,7},{6,0},{7,1},{8,10},{9,11},{10,... | collective-permute-start | bytes 737288 | tf_op jit(solution)/shard_map/ppermute | solution.py:222
  75.5 14.7 %collective-permute-start.7 = (bf16[80,1536]{1,0:T(8,128)(2,1)S(1)}, bf16[80,1536]{1,0:T(8,128)(2,1)S(1)}, u32[]{:S(2)}, u32[]{:S(2)}) collective-permute-start(bf16[80,1536]{1,0:T(8,128)(2,1)S(1)} %get-tuple-element.51), channel_id=1, source_target_pairs={{0,6},{1,7},{2,0},{3,1},{4,2},{5,3},{6,4},{7,5},{8,14},{9,15},{10,... | collective-permute-start | bytes 737288 | tf_op jit(solution)/shard_map/ppermute | solution.py:222
  90.4 17.7 %collective-permute-start.11 = (bf16[80,1664]{1,0:T(8,128)(2,1)S(1)}, bf16[80,1664]{1,0:T(8,128)(2,1)S(1)}, u32[]{:S(2)}, u32[]{:S(2)}) collective-permute-start(bf16[80,1664]{1,0:T(8,128)(2,1)S(1)} %shard_map.122.rest_0_), channel_id=1, source_target_pairs={{0,2},{1,3},{2,4},{3,5},{4,6},{5,7},{6,0},{7,1},{8,10},{9,11},{10,... | collective-permute-start | bytes 798728 | tf_op jit(solution)/shard_map/ppermute | solution.py:222
  96.2 15.9 %collective-permute-start.8 = (bf16[80,1664]{1,0:T(8,128)(2,1)S(1)}, bf16[80,1664]{1,0:T(8,128)(2,1)S(1)}, u32[]{:S(2)}, u32[]{:S(2)}) collective-permute-start(bf16[80,1664]{1,0:T(8,128)(2,1)S(1)} %shard_map.122.rest_0_), channel_id=1, source_target_pairs={{0,6},{1,7},{2,0},{3,1},{4,2},{5,3},{6,4},{7,5},{8,14},{9,15},{10,... | collective-permute-start | bytes 798728 | tf_op jit(solution)/shard_map/ppermute | solution.py:222
  98.8 20.3 %collective-permute-start.14 = (bf16[80,1664]{1,0:T(8,128)(2,1)S(1)}, bf16[80,1664]{1,0:T(8,128)(2,1)S(1)}, u32[]{:S(2)}, u32[]{:S(2)}) collective-permute-start(bf16[80,1664]{1,0:T(8,128)(2,1)S(1)} %shard_map.122.rest_0_), channel_id=1, source_target_pairs={{0,1},{1,2},{2,3},{3,4},{4,5},{5,6},{6,7},{7,0},{8,9},{9,10},{10,1... | collective-permute-start | bytes 798728 | tf_op jit(solution)/shard_map/ppermute | solution.py:222
  103.1 16.0 %collective-permute-start.9 = (bf16[80,1664]{1,0:T(8,128)(2,1)S(1)}, bf16[80,1664]{1,0:T(8,128)(2,1)S(1)}, u32[]{:S(2)}, u32[]{:S(2)}) collective-permute-start(bf16[80,1664]{1,0:T(8,128)(2,1)S(1)} %shard_map.122.rest_0_), channel_id=1, source_target_pairs={{0,7},{1,0},{2,1},{3,2},{4,3},{5,4},{6,5},{7,6},{8,15},{9,8},{10,9... | collective-permute-start | bytes 798728 | tf_op jit(solution)/shard_map/ppermute | solution.py:222
  108.2 12.0 %collective-permute-start.13 = (bf16[80,1664]{1,0:T(8,128)(2,1)S(1)}, bf16[80,1664]{1,0:T(8,128)(2,1)S(1)}, u32[]{:S(2)}, u32[]{:S(2)}) collective-permute-start(bf16[80,1664]{1,0:T(8,128)(2,1)S(1)} %collective-permute-done.11.rest_6_), channel_id=1, source_target_pairs={{0,1},{1,2},{2,3},{3,4},{4,5},{5,6},{6,7},{7,0},{8,9},{9,10},{10,1... | collective-permute-start | bytes 798728 | tf_op jit(solution)/shard_map/ppermute | solution.py:222
  112.1 12.2 %collective-permute-start.12 = (bf16[80,1664]{1,0:T(8,128)(2,1)S(1)}, bf16[80,1664]{1,0:T(8,128)(2,1)S(1)}, u32[]{:S(2)}, u32[]{:S(2)}) collective-permute-start(bf16[80,1664]{1,0:T(8,128)(2,1)S(1)} %broadcast_select_fusion), channel_id=1, source_target_pairs={{0,6},{1,7},{2,0},{3,1},{4,2},{5,3},{6,4},{7,5},{8,10},{9,11},{10,... | collective-permute-start | bytes 798728 | tf_op jit(solution)/shard_map/ppermute | solution.py:230
  115.9 10.8 %collective-permute-start.10 = (bf16[80,1664]{1,0:T(8,128)(2,1)S(1)}, bf16[80,1664]{1,0:T(8,128)(2,1)S(1)}, u32[]{:S(2)}, u32[]{:S(2)}) collective-permute-start(bf16[80,1664]{1,0:T(8,128)(2,1)S(1)} %collective-permute-done.8.rest_2_), channel_id=1, source_target_pairs={{0,7},{1,0},{2,1},{3,2},{4,3},{5,4},{6,5},{7,6},{8,15},{9,8},{10,9... | collective-permute-start | bytes 798728 | tf_op jit(solution)/shard_map/ppermute | solution.py:222
  117.8 1.1 copy-start.3
  128.6 0.8 copy-start.10
  129.4 6.2 %copy-start.8 = (bf16[640,512]{1,0:T(8,128)(2,1)}, bf16[640,512]{1,0:T(8,128)(2,1)S(1)}, u32[]{:S(2)}) copy-start(bf16[640,512]{1,0:T(8,128)(2,1)S(1)} %get-tuple-element.63) | copy-start | bytes 1966084
  129.4 4.6 %collective-permute-start.15 = (bf16[320,1664]{1,0:T(8,128)(2,1)S(1)}, bf16[320,1664]{1,0:T(8,128)(2,1)S(1)}, u32[]{:S(2)}, u32[]{:S(2)}) collective-permute-start(bf16[320,1664]{1,0:T(8,128)(2,1)S(1)} %get-tuple-element.59), channel_id=1, source_target_pairs={{0,8},{8,0},{16,24},{24,16},{32,40},{40,32},{48,56},{56,48},{64,72... | collective-permute-start | bytes 3194888 | tf_op jit(solution)/shard_map/ppermute | solution.py:218
  135.6 19.0 %all-to-all-start.2 = ((bf16[8,40,1664]{2,1,0:T(8,128)(2,1)}), bf16[8,40,1664]{2,1,0:T(8,128)(2,1)S(1)}, u32[]{:S(2)}, u32[]{:S(2)}) async-start(bf16[8,40,1664]{2,1,0:T(8,128)(2,1)} %bitcast.3), calls=%async_computation.2 | async-start | bytes 2129920 | tf_op jit(solution)/shard_map/all_to_all | solution.py:213
  140.0 2.1 %copy-start.11 = (bf16[640,512]{1,0:T(8,128)(2,1)S(1)}, bf16[640,512]{1,0:T(8,128)(2,1)}, u32[]{:S(2)}) copy-start(bf16[640,512]{1,0:T(8,128)(2,1)} %copy-done.10) | copy-start | bytes 1966084
  142.1 1.7 copy-start.9
  145.5 13.6 %copy-start.12 = (bf16[320,768]{1,0:T(8,128)(2,1)S(1)}, bf16[320,768]{1,0:T(8,128)(2,1)}, u32[]{:S(2)}) copy-start(bf16[320,768]{1,0:T(8,128)(2,1)} %get-tuple-element.78) | copy-start | bytes 1474564
  145.5 13.6 %copy-start.13 = (bf16[320,768]{1,0:T(8,128)(2,1)S(1)}, bf16[320,768]{1,0:T(8,128)(2,1)}, u32[]{:S(2)}) copy-start(bf16[320,768]{1,0:T(8,128)(2,1)} %get-tuple-element.80) | copy-start | bytes 1474564
  155.7 12.9 %all-to-all-start.3 = ((bf16[4,130,128]{2,1,0:T(8,128)(2,1)}), bf16[4,130,128]{2,1,0:T(8,128)(2,1)S(1)}, u32[]{:S(2)}, u32[]{:S(2)}) async-start(bf16[4,130,128]{2,1,0:T(8,128)(2,1)} %reshape.41), calls=%async_computation.3 | async-start | bytes 278528 | tf_op jit(solution)/shard_map/all_to_all | solution.py:213

commit v6 on v5

--- a/solution.py
+++ b/solution.py
@@ -22,22 +22,30 @@
 PARAMS = pltpu.CompilerParams(vmem_limit_bytes=40 * 1024 * 1024)
 
 
+def column(row):
+    count = row.shape[1]
+    down = lax.broadcasted_iota(jnp.int32, (count, count), 0)
+    across = lax.broadcasted_iota(jnp.int32, (count, count), 1)
+    return jnp.sum(jnp.where(down == across, row, 0.0), axis=1, keepdims=True)
+
+
 def route_masks(ids_ref, logits_ref):
-    count = ids_ref.shape[0]
+    count = ids_ref.shape[1]
     slots = EXPERTS * MOST
     slot = lax.broadcasted_iota(jnp.int32, (count, slots), 1)
     expert = jnp.zeros((count, slots), jnp.int32)
     for e in range(1, EXPERTS):
         expert = expert + (slot >= e * MOST).astype(jnp.int32)
-    named = [ids_ref[:, k : k + 1] == expert for k in range(2)]
+    ids = [column(ids_ref[k : k + 1, :].astype(jnp.float32)) for k in range(2)]
+    named = [i == expert.astype(jnp.float32) for i in ids]
     chosen = (named[0] | named[1]).astype(jnp.float32)
     row = lax.broadcasted_iota(jnp.int32, (count, count), 0)
-    column = lax.broadcasted_iota(jnp.int32, (count, count), 1)
-    before = (column < row).astype(jnp.float32)
+    place = lax.broadcasted_iota(jnp.int32, (count, count), 1)
+    before = (place < row).astype(jnp.float32)
     rank = jnp.dot(before, chosen, preferred_element_type=jnp.float32)
     placed = rank == (slot - expert * MOST).astype(jnp.float32)
     masks = [(n & placed).astype(jnp.bfloat16) for n in named]
-    first = jax.nn.sigmoid(logits_ref[:, 0:1] - logits_ref[:, 1:2])
+    first = column(jax.nn.sigmoid(logits_ref[0:1, :] - logits_ref[1:2, :]))
     return masks, (first, 1.0 - first)
 
 
@@ -187,8 +195,12 @@
     products = [pick(m, slice(2 * width, 2 * width + LANES)) for m in masks]
     products = [p[:, 0:1] + p[:, 1:2] for p in products]
     change = products[0] * weights[1] - products[1] * weights[0]
-    which = lax.broadcasted_iota(jnp.int32, logits_grad_ref.shape, 1)
-    logits_grad_ref[...] = jnp.where(which == 0, change, -change)
+    count = change.shape[0]
+    down = lax.broadcasted_iota(jnp.int32, (count, count), 0)
+    across = lax.broadcasted_iota(jnp.int32, (count, count), 1)
+    change = jnp.sum(jnp.where(down == across, change, 0.0), axis=0, keepdims=True)
+    logits_grad_ref[0:1, :] = change
+    logits_grad_ref[1:2, :] = -change
 
 
 def on_device(tokens, expert_ids, route_logits, w_gate, w_up, w_down, out_grad):
@@ -277,11 +289,12 @@
         )(*lax.optimization_barrier((*weights, earlier))[:-1])
 
     weights = [w_gate, w_up, w_down]
+    small = [expert_ids.T, route_logits.T]
     [slots] = call(
         pack_kernel,
         [(EXPERTS * MOST, 2 * width)],
         [],
-        [expert_ids, route_logits, tokens, out_grad],
+        [*small, tokens, out_grad],
     )
     near, far = gather_rows(slots)
     chunks = call(
@@ -314,13 +327,13 @@
         out_shape=[
             jax.ShapeDtypeStruct((count, width), bf16),
             jax.ShapeDtypeStruct((count, width), bf16),
-            jax.ShapeDtypeStruct(route_logits.shape, jnp.float32),
+            jax.ShapeDtypeStruct(small[1].shape, jnp.float32),
         ],
         in_specs=[VMEM] * 3,
         out_specs=[VMEM] * 3,
         compiler_params=PARAMS,
-    )(expert_ids, route_logits, back)
-    return (layer_out, tokens_grad, gate_grad, up_grad, down_grad, logits_grad)
+    )(*small, back)
+    return (layer_out, tokens_grad, gate_grad, up_grad, down_grad, logits_grad.T)
 
 
 def solution(mesh):

time: 172 us -> 171 us (level)
  the two profiles are of different devices: /device:TPU:64 before, /device:TPU:8 now
where the time goes in v6:
time: 171 us; the launch traced here: 169 us
  starting transfers between devices  70.4 us (41%)
  waiting for transfers between devices  38.6 us (23%)
  blocking collectives  32.3 us (19%)
  Pallas kernels  11.1 us (6%)
  local copies, waits for them, and re-layouts  10.9 us (6%)
  matrix products  5.06 us (3%)
    ppermute x12, starting transfers between devices, shift(): return lax.ppermute(value, 'fsdp', pairs)  52.6 us
    all_to_all x2, blocking collectives, across(): lax.all_to_all(blocks, 'expert', split_axis=0, concat_axis=0, axis_index_...  32.3 us
    all_to_all x2, waiting for transfers between devices, across(): lax.all_to_all(blocks, 'expert', split_axis=0, concat_axis=0, axis_index_...  16.4 us
    ppermute x12, waiting for transfers between devices, shift(): return lax.ppermute(value, 'fsdp', pairs)  10.6 us
    pallas_call x7, Pallas kernels, call(): pl.pallas_call(kernel, out_shape=[pltpu.VMEM(shape, jnp.bfloat16) for sha...  9.66 us
    all_to_all x2, starting transfers between devices, across(): lax.all_to_all(blocks, 'expert', split_axis=0, concat_axis=0, axis_index_...  8.24 us
    ppermute x2, waiting for transfers between devices, shift_by_core(): return lax.ppermute(value, ('expert', 'fsdp'), pairs)  7.71 us
    unnamed x34, local copies, waits for them, and re-layouts  7.33 us
  transfers between devices with their start and end apart: 18, of which 9 were waited for; matrix products, arithmetic and copies ran while one was open for 4% of the time, Pallas kernels for 1%

profile of v6, /device:TPU:8, one launch (start us, length us, event | category | flops | bytes accessed | tf_op | source)
XLA Modules:
  0.0 169.5 jit_solution(11973887079076642606)
XLA Ops:
  4.1 14.4 %all_to_all.20 = bf16[4,120,128]{2,1,0:T(8,128)(2,1)S(1)} all-to-all(bf16[4,120,128]{2,1,0:T(8,128)(2,1)S(1)} %reshape.37), channel_id=1, replica_groups={{0,128,256,384},{8,136,264,392},{16,144,272,400},{24,152,280,408},{32,1..., dimensions={0} | all-to-all | bytes 245760 | tf_op jit(solution)/shard_map/all_to_all | solution.py:225
  18.7 17.9 %all_to_all.21 = bf16[8,40,1536]{2,1,0:T(8,128)(2,1)S(1)} all-to-all(bf16[8,40,1536]{2,1,0:T(8,128)(2,1)S(1)} %broadcast_in_dim.8), channel_id=1, replica_groups={{0,16,32,48,64,80,96,112},{8,24,40,56,72,88,104,120},{128,144,160,176,1..., dimensions={0} | all-to-all | bytes 1966080 | tf_op jit(solution)/shard_map/all_to_all | solution.py:225
  36.6 1.9 %collective-permute-start = (bf16[320,1536]{1,0:T(8,128)(2,1)S(1)}, bf16[320,1536]{1,0:T(8,128)(2,1)}, u32[]{:S(2)}, u32[]{:S(2)}) collective-permute-start(bf16[320,1536]{1,0:T(8,128)(2,1)S(1)} %bitcast.10), channel_id=1, source_target_pairs={{0,8},{8,0},{16,24},{24,16},{32,40},{40,32},{48,56},{56,48},{64,72... | collective-permute-start | bytes 2949128 | tf_op jit(solution)/shard_map/ppermute | solution.py:230
  41.2 3.8 %shard_map.120 = (bf16[80,1536]{1,0:T(8,128)(2,1)S(1)}, bf16[80,1536]{1,0:T(8,128)(2,1)S(1)}, bf16[80,1536]{1,0:T(8,128)(2,1)S(1)}, bf16[80,1536]{1,0:T(8,128)(2...) custom-call(s32[1]{0:T(128)} %bitcast.2.plane_ref, ...), custom_call_target="tpu_custom_call" | custom-call | flops 1509949440 | bytes 4194304 | tf_op jit(solution)/shard_map/pallas_call | solution.py:174
  46.4 4.3 %collective-permute-start.3 = (bf16[80,1536]{1,0:T(8,128)(2,1)}, bf16[80,1536]{1,0:T(8,128)(2,1)}, u32[]{:S(2)}, u32[]{:S(2)}) collective-permute-start(bf16[80,1536]{1,0:T(8,128)(2,1)} %get-tuple-element.46), channel_id=1, source_target_pairs={{0,1},{1,2},{2,3},{3,4},{4,5},{5,6},{6,7},{7,0},{8,9},{9,10},{10,1... | collective-permute-start | bytes 737288 | tf_op jit(solution)/shard_map/ppermute | solution.py:234
  50.7 8.6 %collective-permute-start.4 = (bf16[80,1536]{1,0:T(8,128)(2,1)}, bf16[80,1536]{1,0:T(8,128)(2,1)}, u32[]{:S(2)}, u32[]{:S(2)}) collective-permute-start(bf16[80,1536]{1,0:T(8,128)(2,1)} %get-tuple-element.48), channel_id=1, source_target_pairs={{0,7},{1,0},{2,1},{3,2},{4,3},{5,4},{6,5},{7,6},{8,15},{9,8},{10,9... | collective-permute-start | bytes 737288 | tf_op jit(solution)/shard_map/ppermute | solution.py:234
  59.3 1.9 %collective-permute-start.5 = (bf16[80,1536]{1,0:T(8,128)(2,1)}, bf16[80,1536]{1,0:T(8,128)(2,1)}, u32[]{:S(2)}, u32[]{:S(2)}) collective-permute-start(bf16[80,1536]{1,0:T(8,128)(2,1)} %get-tuple-element.49), channel_id=1, source_target_pairs={{0,2},{1,3},{2,4},{3,5},{4,6},{5,7},{6,0},{7,1},{8,14},{9,15},{10,... | collective-permute-start | bytes 737288 | tf_op jit(solution)/shard_map/ppermute | solution.py:242
  61.2 3.0 %collective-permute-start.1 = (bf16[80,1536]{1,0:T(8,128)(2,1)}, bf16[80,1536]{1,0:T(8,128)(2,1)S(1)}, u32[]{:S(2)}, u32[]{:S(2)}) collective-permute-start(bf16[80,1536]{1,0:T(8,128)(2,1)} %copy-done.11), channel_id=1, source_target_pairs={{0,1},{1,2},{2,3},{3,4},{4,5},{5,6},{6,7},{7,0},{8,9},{9,10},{10,1... | collective-permute-start | bytes 737288 | tf_op jit(solution)/shard_map/ppermute | solution.py:234
  64.3 4.1 %collective-permute-start.2 = (bf16[80,1536]{1,0:T(8,128)(2,1)}, bf16[80,1536]{1,0:T(8,128)(2,1)S(1)}, u32[]{:S(2)}, u32[]{:S(2)}) collective-permute-start(bf16[80,1536]{1,0:T(8,128)(2,1)} %copy-done.10), channel_id=1, source_target_pairs={{0,7},{1,0},{2,1},{3,2},{4,3},{5,4},{6,5},{7,6},{8,15},{9,8},{10,9... | collective-permute-start | bytes 737288 | tf_op jit(solution)/shard_map/ppermute | solution.py:234
  68.3 6.3 %collective-permute-done.5.four_ref = bf16[80,1536]{1,0:T(8,128)(2,1)} collective-permute-done((bf16[80,1536]{1,0:T(8,128)(2,1)}, bf16[80,1536]{1,0:T(8,128)(2,1)}, u32[]{:S(2)}, u32[]{:S(2)}) %collective-permute-start.5) | collective-permute-done | bytes 245792 | tf_op jit(solution)/shard_map/ppermute | solution.py:242
  76.0 1.9 %collective-permute-start.6 = (bf16[80,1536]{1,0:T(8,128)(2,1)S(1)}, bf16[80,1536]{1,0:T(8,128)(2,1)S(1)}, u32[]{:S(2)}, u32[]{:S(2)}) collective-permute-start(bf16[80,1536]{1,0:T(8,128)(2,1)S(1)} %get-tuple-element.50), channel_id=1, source_target_pairs={{0,2},{1,3},{2,4},{3,5},{4,6},{5,7},{6,0},{7,1},{8,10},{9,11},{10,... | collective-permute-start | bytes 737288 | tf_op jit(solution)/shard_map/ppermute | solution.py:234
  78.0 6.0 %collective-permute-start.7 = (bf16[80,1536]{1,0:T(8,128)(2,1)S(1)}, bf16[80,1536]{1,0:T(8,128)(2,1)S(1)}, u32[]{:S(2)}, u32[]{:S(2)}) collective-permute-start(bf16[80,1536]{1,0:T(8,128)(2,1)S(1)} %get-tuple-element.51), channel_id=1, source_target_pairs={{0,6},{1,7},{2,0},{3,1},{4,2},{5,3},{6,4},{7,5},{8,14},{9,15},{10,... | collective-permute-start | bytes 737288 | tf_op jit(solution)/shard_map/ppermute | solution.py:234
  84.0 3.3 %collective-permute-done.6.d_ref = bf16[80,1536]{1,0:T(8,128)(2,1)S(1)} collective-permute-done((bf16[80,1536]{1,0:T(8,128)(2,1)S(1)}, bf16[80,1536]{1,0:T(8,128)(2,1)S(1)}, u32[]{:S(2)}, u32[]{:S(2)}) %collective-permute-start.6) | collective-permute-done | bytes 245792 | tf_op jit(solution)/shard_map/ppermute | solution.py:234
  87.3 4.2 %collective-permute-done.7.e_ref = bf16[80,1536]{1,0:T(8,128)(2,1)S(1)} collective-permute-done((bf16[80,1536]{1,0:T(8,128)(2,1)S(1)}, bf16[80,1536]{1,0:T(8,128)(2,1)S(1)}, u32[]{:S(2)}, u32[]{:S(2)}) %collective-permute-start.7) | collective-permute-done | bytes 245792 | tf_op jit(solution)/shard_map/ppermute | solution.py:234
  91.8 5.3 %collective-permute-start.11 = (bf16[80,1664]{1,0:T(8,128)(2,1)S(1)}, bf16[80,1664]{1,0:T(8,128)(2,1)S(1)}, u32[]{:S(2)}, u32[]{:S(2)}) collective-permute-start(bf16[80,1664]{1,0:T(8,128)(2,1)S(1)} %shard_map.122.rest_0_), channel_id=1, source_target_pairs={{0,2},{1,3},{2,4},{3,5},{4,6},{5,7},{6,0},{7,1},{8,10},{9,11},{10,... | collective-permute-start | bytes 798728 | tf_op jit(solution)/shard_map/ppermute | solution.py:234
  97.1 2.6 %collective-permute-start.8 = (bf16[80,1664]{1,0:T(8,128)(2,1)S(1)}, bf16[80,1664]{1,0:T(8,128)(2,1)S(1)}, u32[]{:S(2)}, u32[]{:S(2)}) collective-permute-start(bf16[80,1664]{1,0:T(8,128)(2,1)S(1)} %shard_map.122.rest_0_), channel_id=1, source_target_pairs={{0,6},{1,7},{2,0},{3,1},{4,2},{5,3},{6,4},{7,5},{8,14},{9,15},{10,... | collective-permute-start | bytes 798728 | tf_op jit(solution)/shard_map/ppermute | solution.py:234
  99.8 2.2 %collective-permute-start.14 = (bf16[80,1664]{1,0:T(8,128)(2,1)S(1)}, bf16[80,1664]{1,0:T(8,128)(2,1)S(1)}, u32[]{:S(2)}, u32[]{:S(2)}) collective-permute-start(bf16[80,1664]{1,0:T(8,128)(2,1)S(1)} %shard_map.122.rest_0_), channel_id=1, source_target_pairs={{0,1},{1,2},{2,3},{3,4},{4,5},{5,6},{6,7},{7,0},{8,9},{9,10},{10,1... | collective-permute-start | bytes 798728 | tf_op jit(solution)/shard_map/ppermute | solution.py:234
  102.0 4.8 %collective-permute-start.9 = (bf16[80,1664]{1,0:T(8,128)(2,1)S(1)}, bf16[80,1664]{1,0:T(8,128)(2,1)S(1)}, u32[]{:S(2)}, u32[]{:S(2)}) collective-permute-start(bf16[80,1664]{1,0:T(8,128)(2,1)S(1)} %shard_map.122.rest_0_), channel_id=1, source_target_pairs={{0,7},{1,0},{2,1},{3,2},{4,3},{5,4},{6,5},{7,6},{8,15},{9,8},{10,9... | collective-permute-start | bytes 798728 | tf_op jit(solution)/shard_map/ppermute | solution.py:234
  106.8 4.4 %collective-permute-start.13 = (bf16[80,1664]{1,0:T(8,128)(2,1)S(1)}, bf16[80,1664]{1,0:T(8,128)(2,1)S(1)}, u32[]{:S(2)}, u32[]{:S(2)}) collective-permute-start(bf16[80,1664]{1,0:T(8,128)(2,1)S(1)} %collective-permute-done.11.rest_6_), channel_id=1, source_target_pairs={{0,1},{1,2},{2,3},{3,4},{4,5},{5,6},{6,7},{7,0},{8,9},{9,10},{10,1... | collective-permute-start | bytes 798728 | tf_op jit(solution)/shard_map/ppermute | solution.py:234
  111.3 3.7 %collective-permute-start.12 = (bf16[80,1664]{1,0:T(8,128)(2,1)S(1)}, bf16[80,1664]{1,0:T(8,128)(2,1)S(1)}, u32[]{:S(2)}, u32[]{:S(2)}) collective-permute-start(bf16[80,1664]{1,0:T(8,128)(2,1)S(1)} %broadcast_select_fusion), channel_id=1, source_target_pairs={{0,6},{1,7},{2,0},{3,1},{4,2},{5,3},{6,4},{7,5},{8,10},{9,11},{10,... | collective-permute-start | bytes 798728 | tf_op jit(solution)/shard_map/ppermute | solution.py:242
  115.0 5.4 %collective-permute-start.10 = (bf16[80,1664]{1,0:T(8,128)(2,1)S(1)}, bf16[80,1664]{1,0:T(8,128)(2,1)S(1)}, u32[]{:S(2)}, u32[]{:S(2)}) collective-permute-start(bf16[80,1664]{1,0:T(8,128)(2,1)S(1)} %collective-permute-done.8.rest_2_), channel_id=1, source_target_pairs={{0,7},{1,0},{2,1},{3,2},{4,3},{5,4},{6,5},{7,6},{8,15},{9,8},{10,9... | collective-permute-start | bytes 798728 | tf_op jit(solution)/shard_map/ppermute | solution.py:234
  123.2 3.1 %collective-permute-done.10.rest_3_ = bf16[80,1664]{1,0:T(8,128)(2,1)S(1)} collective-permute-done((bf16[80,1664]{1,0:T(8,128)(2,1)S(1)}, bf16[80,1664]{1,0:T(8,128)(2,1)S(1)}, u32[]{:S(2)}, u32[]{:S(2)}) %collective-permute-start.10) | collective-permute-done | bytes 266272 | tf_op jit(solution)/shard_map/ppermute | solution.py:234
  126.3 1.8 %shard_map.124 = (bf16[320,1664]{1,0:T(8,128)(2,1)S(1)}, bf16[320,1664]{1,0:T(8,128)(2,1)S(1)}, bf16[640,512]{1,0:T(8,128)(2,1)S(1)}, bf16[640,512]{1,0:T(8,128)(2,1)S(1)}, bf16[640,512]{1,0:T(8,128)(2,1)S(1)}) custom-call(s32[1]{0:T(128)} %bitcast.2.plane_ref, bf16[768,512]{1,0:T(8,128)(2,1)S(1)} %get-tuple-element.55.gate_ref, ...), custom_call_target="tpu_custom_call" | custom-call | flops 1509949440 | bytes 4194304 | tf_op jit(solution)/shard_map/pallas_call | solution.py:174
  129.0 1.9 %collective-permute-start.15 = (bf16[320,1664]{1,0:T(8,128)(2,1)S(1)}, bf16[320,1664]{1,0:T(8,128)(2,1)S(1)}, u32[]{:S(2)}, u32[]{:S(2)}) collective-permute-start(bf16[320,1664]{1,0:T(8,128)(2,1)S(1)} %get-tuple-element.59), channel_id=1, source_target_pairs={{0,8},{8,0},{16,24},{24,16},{32,40},{40,32},{48,56},{56,48},{64,72... | collective-permute-start | bytes 3194888 | tf_op jit(solution)/shard_map/ppermute | solution.py:230
  130.9 2.6 %collective-permute-done.15.far_ref = bf16[320,1664]{1,0:T(8,128)(2,1)S(1)} collective-permute-done((bf16[320,1664]{1,0:T(8,128)(2,1)S(1)}, bf16[320,1664]{1,0:T(8,128)(2,1)S(1)}, u32[]{:S(2)}, u32[]{:S(2)}) %collective-permute-start.15) | collective-permute-done | bytes 1064992 | tf_op jit(solution)/shard_map/ppermute | solution.py:230
  135.2 4.9 %all-to-all-start.2 = ((bf16[8,40,1664]{2,1,0:T(8,128)(2,1)}), bf16[8,40,1664]{2,1,0:T(8,128)(2,1)S(1)}, u32[]{:S(2)}, u32[]{:S(2)}) async-start(bf16[8,40,1664]{2,1,0:T(8,128)(2,1)} %bitcast.5), calls=%async_computation.2 | async-start | bytes 2129920 | tf_op jit(solution)/shard_map/all_to_all | solution.py:225
  140.2 2.1 %fusion.7 = (bf16[320,768]{1,0:T(8,128)(2,1)}, bf16[320,768]{1,0:T(8,128)(2,1)S(1)}) fusion(bf16[320,1536]{1,0:T(8,128)(2,1)} %collective-permute-done.far_ref), kind=kLoop, calls=%fused_computation.12 | loop fusion | bytes 1966080 | tf_op jit(solution)/shard_map/slice | solution.py:309
  142.3 1.7 convolution_convert_fusion.2
  145.7 9.5 %all-to-all-done.2.blocks_ref = bf16[8,40,1664]{2,1,0:T(8,128)(2,1)S(1)} async-done(((bf16[8,40,1664]{2,1,0:T(8,128)(2,1)}), bf16[8,40,1664]{2,1,0:T(8,128)(2,1)S(1)}, u32[]{:S(2)}, u32[]{:S(2)}) %all-to-all-start.2) | async-done | bytes 1064992 | tf_op jit(solution)/shard_map/all_to_all | solution.py:225
  156.2 3.3 %all-to-all-start.3 = ((bf16[4,130,128]{2,1,0:T(8,128)(2,1)}), bf16[4,130,128]{2,1,0:T(8,128)(2,1)S(1)}, u32[]{:S(2)}, u32[]{:S(2)}) async-start(bf16[4,130,128]{2,1,0:T(8,128)(2,1)} %reshape.41), calls=%async_computation.3 | async-start | bytes 278528 | tf_op jit(solution)/shard_map/all_to_all | solution.py:225
  159.6 1.7 convolution_convert_fusion
  161.3 6.9 %all-to-all-done.3 = bf16[4,130,128]{2,1,0:T(8,128)(2,1)S(1)} async-done(((bf16[4,130,128]{2,1,0:T(8,128)(2,1)}), bf16[4,130,128]{2,1,0:T(8,128)(2,1)S(1)}, u32[]{:S(2)}, u32[]{:S(2)}) %all-to-all-start.3) | async-done | bytes 133152 | tf_op jit(solution)/shard_map/all_to_all | solution.py:225
  (61 shorter events, 18.7 us)
Async XLA Ops:
  0.6 0.7 copy-start.4
  1.4 0.7 copy-start.5
  18.7 19.9 %copy-start = (bf16[768,512]{1,0:T(8,128)(2,1)S(1)}, bf16[768,512]{1,0:T(8,128)(2,1)}, u32[]{:S(2)}) copy-start(bf16[768,512]{1,0:T(8,128)(2,1)} %refs_0_.1) | copy-start | bytes 2359300
  18.7 19.9 %copy-start.1 = (bf16[768,512]{1,0:T(8,128)(2,1)S(1)}, bf16[768,512]{1,0:T(8,128)(2,1)}, u32[]{:S(2)}) copy-start(bf16[768,512]{1,0:T(8,128)(2,1)} %refs_1_.1) | copy-start | bytes 2359300
  36.6 4.6 %collective-permute-start = (bf16[320,1536]{1,0:T(8,128)(2,1)S(1)}, bf16[320,1536]{1,0:T(8,128)(2,1)}, u32[]{:S(2)}, u32[]{:S(2)}) collective-permute-start(bf16[320,1536]{1,0:T(8,128)(2,1)S(1)} %bitcast.10), channel_id=1, source_target_pairs={{0,8},{8,0},{16,24},{24,16},{32,40},{40,32},{48,56},{56,48},{64,72... | collective-permute-start | bytes 2949128 | tf_op jit(solution)/shard_map/ppermute | solution.py:230
  38.6 1.1 copy-start.2
  45.7 0.7 copy-start.11
  46.4 21.9 %collective-permute-start.3 = (bf16[80,1536]{1,0:T(8,128)(2,1)}, bf16[80,1536]{1,0:T(8,128)(2,1)}, u32[]{:S(2)}, u32[]{:S(2)}) collective-permute-start(bf16[80,1536]{1,0:T(8,128)(2,1)} %get-tuple-element.46), channel_id=1, source_target_pairs={{0,1},{1,2},{2,3},{3,4},{4,5},{5,6},{6,7},{7,0},{8,9},{9,10},{10,1... | collective-permute-start | bytes 737288 | tf_op jit(solution)/shard_map/ppermute | solution.py:234
  50.7 17.6 %collective-permute-start.4 = (bf16[80,1536]{1,0:T(8,128)(2,1)}, bf16[80,1536]{1,0:T(8,128)(2,1)}, u32[]{:S(2)}, u32[]{:S(2)}) collective-permute-start(bf16[80,1536]{1,0:T(8,128)(2,1)} %get-tuple-element.48), channel_id=1, source_target_pairs={{0,7},{1,0},{2,1},{3,2},{4,3},{5,4},{6,5},{7,6},{8,15},{9,8},{10,9... | collective-permute-start | bytes 737288 | tf_op jit(solution)/shard_map/ppermute | solution.py:234
  59.3 15.3 %collective-permute-start.5 = (bf16[80,1536]{1,0:T(8,128)(2,1)}, bf16[80,1536]{1,0:T(8,128)(2,1)}, u32[]{:S(2)}, u32[]{:S(2)}) collective-permute-start(bf16[80,1536]{1,0:T(8,128)(2,1)} %get-tuple-element.49), channel_id=1, source_target_pairs={{0,2},{1,3},{2,4},{3,5},{4,6},{5,7},{6,0},{7,1},{8,14},{9,15},{10,... | collective-permute-start | bytes 737288 | tf_op jit(solution)/shard_map/ppermute | solution.py:242
  61.2 22.8 %collective-permute-start.1 = (bf16[80,1536]{1,0:T(8,128)(2,1)}, bf16[80,1536]{1,0:T(8,128)(2,1)S(1)}, u32[]{:S(2)}, u32[]{:S(2)}) collective-permute-start(bf16[80,1536]{1,0:T(8,128)(2,1)} %copy-done.11), channel_id=1, source_target_pairs={{0,1},{1,2},{2,3},{3,4},{4,5},{5,6},{6,7},{7,0},{8,9},{9,10},{10,1... | collective-permute-start | bytes 737288 | tf_op jit(solution)/shard_map/ppermute | solution.py:234
  64.3 19.8 %collective-permute-start.2 = (bf16[80,1536]{1,0:T(8,128)(2,1)}, bf16[80,1536]{1,0:T(8,128)(2,1)S(1)}, u32[]{:S(2)}, u32[]{:S(2)}) collective-permute-start(bf16[80,1536]{1,0:T(8,128)(2,1)} %copy-done.10), channel_id=1, source_target_pairs={{0,7},{1,0},{2,1},{3,2},{4,3},{5,4},{6,5},{7,6},{8,15},{9,8},{10,9... | collective-permute-start | bytes 737288 | tf_op jit(solution)/shard_map/ppermute | solution.py:234
  76.0 11.3 %collective-permute-start.6 = (bf16[80,1536]{1,0:T(8,128)(2,1)S(1)}, bf16[80,1536]{1,0:T(8,128)(2,1)S(1)}, u32[]{:S(2)}, u32[]{:S(2)}) collective-permute-start(bf16[80,1536]{1,0:T(8,128)(2,1)S(1)} %get-tuple-element.50), channel_id=1, source_target_pairs={{0,2},{1,3},{2,4},{3,5},{4,6},{5,7},{6,0},{7,1},{8,10},{9,11},{10,... | collective-permute-start | bytes 737288 | tf_op jit(solution)/shard_map/ppermute | solution.py:234
  78.0 13.5 %collective-permute-start.7 = (bf16[80,1536]{1,0:T(8,128)(2,1)S(1)}, bf16[80,1536]{1,0:T(8,128)(2,1)S(1)}, u32[]{:S(2)}, u32[]{:S(2)}) collective-permute-start(bf16[80,1536]{1,0:T(8,128)(2,1)S(1)} %get-tuple-element.51), channel_id=1, source_target_pairs={{0,6},{1,7},{2,0},{3,1},{4,2},{5,3},{6,4},{7,5},{8,14},{9,15},{10,... | collective-permute-start | bytes 737288 | tf_op jit(solution)/shard_map/ppermute | solution.py:234
  91.8 15.0 %collective-permute-start.11 = (bf16[80,1664]{1,0:T(8,128)(2,1)S(1)}, bf16[80,1664]{1,0:T(8,128)(2,1)S(1)}, u32[]{:S(2)}, u32[]{:S(2)}) collective-permute-start(bf16[80,1664]{1,0:T(8,128)(2,1)S(1)} %shard_map.122.rest_0_), channel_id=1, source_target_pairs={{0,2},{1,3},{2,4},{3,5},{4,6},{5,7},{6,0},{7,1},{8,10},{9,11},{10,... | collective-permute-start | bytes 798728 | tf_op jit(solution)/shard_map/ppermute | solution.py:234
  97.1 14.1 %collective-permute-start.8 = (bf16[80,1664]{1,0:T(8,128)(2,1)S(1)}, bf16[80,1664]{1,0:T(8,128)(2,1)S(1)}, u32[]{:S(2)}, u32[]{:S(2)}) collective-permute-start(bf16[80,1664]{1,0:T(8,128)(2,1)S(1)} %shard_map.122.rest_0_), channel_id=1, source_target_pairs={{0,6},{1,7},{2,0},{3,1},{4,2},{5,3},{6,4},{7,5},{8,14},{9,15},{10,... | collective-permute-start | bytes 798728 | tf_op jit(solution)/shard_map/ppermute | solution.py:234
  99.8 22.0 %collective-permute-start.14 = (bf16[80,1664]{1,0:T(8,128)(2,1)S(1)}, bf16[80,1664]{1,0:T(8,128)(2,1)S(1)}, u32[]{:S(2)}, u32[]{:S(2)}) collective-permute-start(bf16[80,1664]{1,0:T(8,128)(2,1)S(1)} %shard_map.122.rest_0_), channel_id=1, source_target_pairs={{0,1},{1,2},{2,3},{3,4},{4,5},{5,6},{6,7},{7,0},{8,9},{9,10},{10,1... | collective-permute-start | bytes 798728 | tf_op jit(solution)/shard_map/ppermute | solution.py:234
  102.0 19.8 %collective-permute-start.9 = (bf16[80,1664]{1,0:T(8,128)(2,1)S(1)}, bf16[80,1664]{1,0:T(8,128)(2,1)S(1)}, u32[]{:S(2)}, u32[]{:S(2)}) collective-permute-start(bf16[80,1664]{1,0:T(8,128)(2,1)S(1)} %shard_map.122.rest_0_), channel_id=1, source_target_pairs={{0,7},{1,0},{2,1},{3,2},{4,3},{5,4},{6,5},{7,6},{8,15},{9,8},{10,9... | collective-permute-start | bytes 798728 | tf_op jit(solution)/shard_map/ppermute | solution.py:234
  106.8 14.9 %collective-permute-start.13 = (bf16[80,1664]{1,0:T(8,128)(2,1)S(1)}, bf16[80,1664]{1,0:T(8,128)(2,1)S(1)}, u32[]{:S(2)}, u32[]{:S(2)}) collective-permute-start(bf16[80,1664]{1,0:T(8,128)(2,1)S(1)} %collective-permute-done.11.rest_6_), channel_id=1, source_target_pairs={{0,1},{1,2},{2,3},{3,4},{4,5},{5,6},{6,7},{7,0},{8,9},{9,10},{10,1... | collective-permute-start | bytes 798728 | tf_op jit(solution)/shard_map/ppermute | solution.py:234
  111.3 11.9 %collective-permute-start.12 = (bf16[80,1664]{1,0:T(8,128)(2,1)S(1)}, bf16[80,1664]{1,0:T(8,128)(2,1)S(1)}, u32[]{:S(2)}, u32[]{:S(2)}) collective-permute-start(bf16[80,1664]{1,0:T(8,128)(2,1)S(1)} %broadcast_select_fusion), channel_id=1, source_target_pairs={{0,6},{1,7},{2,0},{3,1},{4,2},{5,3},{6,4},{7,5},{8,10},{9,11},{10,... | collective-permute-start | bytes 798728 | tf_op jit(solution)/shard_map/ppermute | solution.py:242
  115.0 11.2 %collective-permute-start.10 = (bf16[80,1664]{1,0:T(8,128)(2,1)S(1)}, bf16[80,1664]{1,0:T(8,128)(2,1)S(1)}, u32[]{:S(2)}, u32[]{:S(2)}) collective-permute-start(bf16[80,1664]{1,0:T(8,128)(2,1)S(1)} %collective-permute-done.8.rest_2_), channel_id=1, source_target_pairs={{0,7},{1,0},{2,1},{3,2},{4,3},{5,4},{6,5},{7,6},{8,15},{9,8},{10,9... | collective-permute-start | bytes 798728 | tf_op jit(solution)/shard_map/ppermute | solution.py:234
  120.4 1.1 copy-start.3
  128.1 0.8 copy-start.14
  129.0 6.2 %copy-start.12 = (bf16[640,512]{1,0:T(8,128)(2,1)}, bf16[640,512]{1,0:T(8,128)(2,1)S(1)}, u32[]{:S(2)}) copy-start(bf16[640,512]{1,0:T(8,128)(2,1)S(1)} %get-tuple-element.63) | copy-start | bytes 1966084
  129.0 4.6 %collective-permute-start.15 = (bf16[320,1664]{1,0:T(8,128)(2,1)S(1)}, bf16[320,1664]{1,0:T(8,128)(2,1)S(1)}, u32[]{:S(2)}, u32[]{:S(2)}) collective-permute-start(bf16[320,1664]{1,0:T(8,128)(2,1)S(1)} %get-tuple-element.59), channel_id=1, source_target_pairs={{0,8},{8,0},{16,24},{24,16},{32,40},{40,32},{48,56},{56,48},{64,72... | collective-permute-start | bytes 3194888 | tf_op jit(solution)/shard_map/ppermute | solution.py:230
  135.2 19.9 %all-to-all-start.2 = ((bf16[8,40,1664]{2,1,0:T(8,128)(2,1)}), bf16[8,40,1664]{2,1,0:T(8,128)(2,1)S(1)}, u32[]{:S(2)}, u32[]{:S(2)}) async-start(bf16[8,40,1664]{2,1,0:T(8,128)(2,1)} %bitcast.5), calls=%async_computation.2 | async-start | bytes 2129920 | tf_op jit(solution)/shard_map/all_to_all | solution.py:225
  140.2 2.1 %copy-start.15 = (bf16[640,512]{1,0:T(8,128)(2,1)S(1)}, bf16[640,512]{1,0:T(8,128)(2,1)}, u32[]{:S(2)}) copy-start(bf16[640,512]{1,0:T(8,128)(2,1)} %copy-done.14) | copy-start | bytes 1966084
  142.3 1.7 copy-start.13
  145.7 13.9 %copy-start.16 = (bf16[320,768]{1,0:T(8,128)(2,1)S(1)}, bf16[320,768]{1,0:T(8,128)(2,1)}, u32[]{:S(2)}) copy-start(bf16[320,768]{1,0:T(8,128)(2,1)} %get-tuple-element.68) | copy-start | bytes 1474564
  156.2 12.0 %all-to-all-start.3 = ((bf16[4,130,128]{2,1,0:T(8,128)(2,1)}), bf16[4,130,128]{2,1,0:T(8,128)(2,1)S(1)}, u32[]{:S(2)}, u32[]{:S(2)}) async-start(bf16[4,130,128]{2,1,0:T(8,128)(2,1)} %reshape.41), calls=%async_computation.3 | async-start | bytes 278528 | tf_op jit(solution)/shard_map/all_to_all | solution.py:225
  159.5 8.8 %copy-start.7 = (s32[16,2]{0,1:T(2,128)S(1)}, s32[16,2]{0,1:T(2,128)}, u32[]{:S(2)}) copy-start(s32[16,2]{0,1:T(2,128)} %param.8) | copy-start | bytes 388
  159.6 8.8 %copy-start.9 = (f32[16,2]{0,1:T(2,128)S(1)}, f32[16,2]{0,1:T(2,128)}, u32[]{:S(2)}) copy-start(f32[16,2]{0,1:T(2,128)} %param.9) | copy-start | bytes 388
  (3 other events, 2.0 us)

commit v7 on v6

--- a/solution.py
+++ b/solution.py
@@ -137,26 +137,31 @@
     value_ref[:, 3 * units :] = product_block(product)
 
 
-def back_kernel(plane_ref, gate_ref, up_ref, down_ref, *rest):
-    pieces, (near_ref, far_ref, hidden_ref, gate_cot_ref, up_cot_ref, tail_ref) = rest[:8], rest[8:]
+def back_half(start, gate_ref, up_ref, down_ref, hidden_ref, gate_cot_ref, up_cot_ref, tail_ref, ref):
+    half = ref.shape[0]
+    depth = gate_ref.shape[0]
+    at = slice(start, start + half)
+    out = jnp.dot(hidden_ref[at, :], down_ref[...], preferred_element_type=jnp.float32)
+    ref[:, :depth] = out.astype(jnp.bfloat16)
+    grad = contract(gate_cot_ref[at, :], gate_ref[...], 1, 1)
+    grad = grad + contract(up_cot_ref[at, :], up_ref[...], 1, 1)
+    ref[:, depth : 2 * depth] = grad.astype(jnp.bfloat16)
+    ref[:, 2 * depth :] = tail_ref[at, :]
+
+
+def far_kernel(plane_ref, gate_ref, up_ref, down_ref, *rest):
+    pieces, (far_ref, *whole) = rest[:8], rest[8:]
     own = pieces[0].shape[0]
-    half = near_ref.shape[0]
-    depth, units = gate_ref.shape
+    units = whole[0].shape[1]
     for ahead, piece in enumerate(pieces):
         at = pl.multiple_of(lax.rem(plane_ref[0] + ahead, len(pieces)) * own, 16)
-        at = pl.ds(at, own)
-        hidden_ref[at, :] = piece[:, :units]
-        gate_cot_ref[at, :] = piece[:, units : 2 * units]
-        up_cot_ref[at, :] = piece[:, 2 * units : 3 * units]
-        tail_ref[at, :] = piece[:, 3 * units :]
-    for start, ref in ((half, far_ref), (0, near_ref)):
-        at = slice(start, start + half)
-        out = jnp.dot(hidden_ref[at, :], down_ref[...], preferred_element_type=jnp.float32)
-        ref[:, :depth] = out.astype(jnp.bfloat16)
-        grad = contract(gate_cot_ref[at, :], gate_ref[...], 1, 1)
-        grad = grad + contract(up_cot_ref[at, :], up_ref[...], 1, 1)
-        ref[:, depth : 2 * depth] = grad.astype(jnp.bfloat16)
-        ref[:, 2 * depth :] = tail_ref[at, :]
+        for i, ref in enumerate(whole):
+            ref[pl.ds(at, own), :] = piece[:, i * units : i * units + ref.shape[1]]
+    back_half(far_ref.shape[0], gate_ref, up_ref, down_ref, *whole, far_ref)
+
+
+def near_kernel(*refs):
+    back_half(0, *refs)
 
 
 def add_kernel(near_ref, far_ref, sum_ref):
@@ -269,8 +274,8 @@
         near = near.reshape(half, -1)
         return near, swap(near)
 
-    def give_back(near, far):
-        [mine] = call(add_kernel, [near.shape], [], [near, swap(far)])
+    def give_back(near, swapped):
+        [mine] = call(add_kernel, [near.shape], [], [near, swapped])
         arrived = across(mine.reshape(chips, EXPERTS * MOST, -1), same_core)
         [summed] = call(fold_kernel, [arrived.shape[1:]], [], [arrived])
         back = across(summed.reshape(EXPERTS, -1, LANES), matching)
@@ -309,15 +314,21 @@
     arrived_cot = jnp.concatenate([near[:, width:], far[:, width:]], axis=0)
     [value] = call(hidden_kernel, [(own, 3 * hidden_width + LANES)], [], relay(chunks))
     pieces = to_all_planes(value)
-    near_part, far_part, hidden, gate_cot, up_cot = call(
-        back_kernel,
-        [(half, 2 * width + LANES)] * 2 + [(rows, hidden_width)] * 3,
+    held = load(weights, pieces[2])
+    back_shape = (half, 2 * width + LANES)
+    flops = 3 * rows * width * hidden_width
+    far_part, hidden, gate_cot, up_cot, tail = call(
+        far_kernel,
+        [back_shape] + [(rows, hidden_width)] * 3 + [(rows, LANES)],
         [plane],
-        [*load(weights, pieces[2]), *pieces],
-        scratch=[pltpu.VMEM((rows, LANES), bf16)],
-        flops=6 * rows * width * hidden_width,
-    )
-    back = give_back(near_part, far_part)
+        [*held, *pieces],
+        flops=flops,
+    )
+    swapped = swap(far_part)
+    [near_part] = call(
+        near_kernel, [back_shape], [], [*held, hidden, gate_cot, up_cot, tail], flops=flops
+    )
+    back = give_back(near_part, swapped)
     down_grad = contract(hidden, arrived_cot, 0, 0).astype(jnp.bfloat16)
     gate_grad = contract(arrived, gate_cot, 0, 0).astype(jnp.bfloat16)
     up_grad = contract(arrived, up_cot, 0, 0).astype(jnp.bfloat16)

time: 171 us -> 169 us (0.988)
    pallas_call x7 -> x8, Pallas kernels: 9.66 us -> 9.85 us  [call(): pl.pallas_call(kernel, out_shape=[pltpu.VMEM(shape, jnp.bfloat16) for sha...]
  transfers between devices with their start and end apart: 18 -> 18, of which waited for: 9 -> 9; matrix products, arithmetic and copies ran while one was open for 4% -> 4% of each run, Pallas kernels for 1% -> 2%
where the time goes in v7:
time: 169 us; the launch traced here: 168 us
  starting transfers between devices  70.4 us (42%)
  waiting for transfers between devices  37.6 us (22%)
  blocking collectives  32.3 us (19%)
  Pallas kernels  11.3 us (7%)
  local copies, waits for them, and re-layouts  10.1 us (6%)
  matrix products  5.06 us (3%)
    ppermute x12, starting transfers between devices, shift(): return lax.ppermute(value, 'fsdp', pairs)  52.6 us
    all_to_all x2, blocking collectives, across(): lax.all_to_all(blocks, 'expert', split_axis=0, concat_axis=0, axis_index_...  32.3 us
    all_to_all x2, waiting for transfers between devices, across(): lax.all_to_all(blocks, 'expert', split_axis=0, concat_axis=0, axis_index_...  16.4 us
    ppermute x12, waiting for transfers between devices, shift(): return lax.ppermute(value, 'fsdp', pairs)  10.6 us
    pallas_call x8, Pallas kernels, call(): pl.pallas_call(kernel, out_shape=[pltpu.VMEM(shape, jnp.bfloat16) for sha...  9.85 us
    all_to_all x2, starting transfers between devices, across(): lax.all_to_all(blocks, 'expert', split_axis=0, concat_axis=0, axis_index_...  8.24 us
    ppermute x2, waiting for transfers between devices, shift_by_core(): return lax.ppermute(value, ('expert', 'fsdp'), pairs)  7.71 us
    unnamed x34, local copies, waits for them, and re-layouts  6.51 us
  transfers between devices with their start and end apart: 18, of which 9 were waited for; matrix products, arithmetic and copies ran while one was open for 4% of the time, Pallas kernels for 2%

profile of v7, /device:TPU:8, one launch (start us, length us, event | category | flops | bytes accessed | tf_op | source)
XLA Modules:
  0.0 167.9 jit_solution(10669431445110616504)
XLA Ops:
  4.1 14.4 %all_to_all.20 = bf16[4,120,128]{2,1,0:T(8,128)(2,1)S(1)} all-to-all(bf16[4,120,128]{2,1,0:T(8,128)(2,1)S(1)} %reshape.37), channel_id=1, replica_groups={{0,128,256,384},{8,136,264,392},{16,144,272,400},{24,152,280,408},{32,1..., dimensions={0} | all-to-all | bytes 245760 | tf_op jit(solution)/shard_map/all_to_all | solution.py:230
  18.7 17.9 %all_to_all.21 = bf16[8,40,1536]{2,1,0:T(8,128)(2,1)S(1)} all-to-all(bf16[8,40,1536]{2,1,0:T(8,128)(2,1)S(1)} %broadcast_in_dim.8), channel_id=1, replica_groups={{0,16,32,48,64,80,96,112},{8,24,40,56,72,88,104,120},{128,144,160,176,1..., dimensions={0} | all-to-all | bytes 1966080 | tf_op jit(solution)/shard_map/all_to_all | solution.py:230
  36.6 1.9 %collective-permute-start = (bf16[320,1536]{1,0:T(8,128)(2,1)S(1)}, bf16[320,1536]{1,0:T(8,128)(2,1)}, u32[]{:S(2)}, u32[]{:S(2)}) collective-permute-start(bf16[320,1536]{1,0:T(8,128)(2,1)S(1)} %bitcast.10), channel_id=1, source_target_pairs={{0,8},{8,0},{16,24},{24,16},{32,40},{40,32},{48,56},{56,48},{64,72... | collective-permute-start | bytes 2949128 | tf_op jit(solution)/shard_map/ppermute | solution.py:235
  41.2 3.8 %shard_map.120 = (bf16[80,1536]{1,0:T(8,128)(2,1)S(1)}, bf16[80,1536]{1,0:T(8,128)(2,1)S(1)}, bf16[80,1536]{1,0:T(8,128)(2,1)S(1)}, bf16[80,1536]{1,0:T(8,128)(2...) custom-call(s32[1]{0:T(128)} %bitcast.2.plane_ref, ...), custom_call_target="tpu_custom_call" | custom-call | flops 1509949440 | bytes 4194304 | tf_op jit(solution)/shard_map/pallas_call | solution.py:179
  46.4 4.3 %collective-permute-start.3 = (bf16[80,1536]{1,0:T(8,128)(2,1)}, bf16[80,1536]{1,0:T(8,128)(2,1)}, u32[]{:S(2)}, u32[]{:S(2)}) collective-permute-start(bf16[80,1536]{1,0:T(8,128)(2,1)} %get-tuple-element.46), channel_id=1, source_target_pairs={{0,1},{1,2},{2,3},{3,4},{4,5},{5,6},{6,7},{7,0},{8,9},{9,10},{10,1... | collective-permute-start | bytes 737288 | tf_op jit(solution)/shard_map/ppermute | solution.py:239
  50.7 8.6 %collective-permute-start.4 = (bf16[80,1536]{1,0:T(8,128)(2,1)}, bf16[80,1536]{1,0:T(8,128)(2,1)}, u32[]{:S(2)}, u32[]{:S(2)}) collective-permute-start(bf16[80,1536]{1,0:T(8,128)(2,1)} %get-tuple-element.48), channel_id=1, source_target_pairs={{0,7},{1,0},{2,1},{3,2},{4,3},{5,4},{6,5},{7,6},{8,15},{9,8},{10,9... | collective-permute-start | bytes 737288 | tf_op jit(solution)/shard_map/ppermute | solution.py:239
  59.3 1.9 %collective-permute-start.5 = (bf16[80,1536]{1,0:T(8,128)(2,1)}, bf16[80,1536]{1,0:T(8,128)(2,1)}, u32[]{:S(2)}, u32[]{:S(2)}) collective-permute-start(bf16[80,1536]{1,0:T(8,128)(2,1)} %get-tuple-element.49), channel_id=1, source_target_pairs={{0,2},{1,3},{2,4},{3,5},{4,6},{5,7},{6,0},{7,1},{8,14},{9,15},{10,... | collective-permute-start | bytes 737288 | tf_op jit(solution)/shard_map/ppermute | solution.py:247
  61.2 3.0 %collective-permute-start.1 = (bf16[80,1536]{1,0:T(8,128)(2,1)}, bf16[80,1536]{1,0:T(8,128)(2,1)S(1)}, u32[]{:S(2)}, u32[]{:S(2)}) collective-permute-start(bf16[80,1536]{1,0:T(8,128)(2,1)} %copy-done.15), channel_id=1, source_target_pairs={{0,1},{1,2},{2,3},{3,4},{4,5},{5,6},{6,7},{7,0},{8,9},{9,10},{10,1... | collective-permute-start | bytes 737288 | tf_op jit(solution)/shard_map/ppermute | solution.py:239
  64.3 4.1 %collective-permute-start.2 = (bf16[80,1536]{1,0:T(8,128)(2,1)}, bf16[80,1536]{1,0:T(8,128)(2,1)S(1)}, u32[]{:S(2)}, u32[]{:S(2)}) collective-permute-start(bf16[80,1536]{1,0:T(8,128)(2,1)} %copy-done.14), channel_id=1, source_target_pairs={{0,7},{1,0},{2,1},{3,2},{4,3},{5,4},{6,5},{7,6},{8,15},{9,8},{10,9... | collective-permute-start | bytes 737288 | tf_op jit(solution)/shard_map/ppermute | solution.py:239
  68.3 6.3 %collective-permute-done.5.four_ref = bf16[80,1536]{1,0:T(8,128)(2,1)} collective-permute-done((bf16[80,1536]{1,0:T(8,128)(2,1)}, bf16[80,1536]{1,0:T(8,128)(2,1)}, u32[]{:S(2)}, u32[]{:S(2)}) %collective-permute-start.5) | collective-permute-done | bytes 245792 | tf_op jit(solution)/shard_map/ppermute | solution.py:247
  76.0 1.9 %collective-permute-start.6 = (bf16[80,1536]{1,0:T(8,128)(2,1)S(1)}, bf16[80,1536]{1,0:T(8,128)(2,1)S(1)}, u32[]{:S(2)}, u32[]{:S(2)}) collective-permute-start(bf16[80,1536]{1,0:T(8,128)(2,1)S(1)} %get-tuple-element.50), channel_id=1, source_target_pairs={{0,2},{1,3},{2,4},{3,5},{4,6},{5,7},{6,0},{7,1},{8,10},{9,11},{10,... | collective-permute-start | bytes 737288 | tf_op jit(solution)/shard_map/ppermute | solution.py:239
  78.0 6.0 %collective-permute-start.7 = (bf16[80,1536]{1,0:T(8,128)(2,1)S(1)}, bf16[80,1536]{1,0:T(8,128)(2,1)S(1)}, u32[]{:S(2)}, u32[]{:S(2)}) collective-permute-start(bf16[80,1536]{1,0:T(8,128)(2,1)S(1)} %get-tuple-element.51), channel_id=1, source_target_pairs={{0,6},{1,7},{2,0},{3,1},{4,2},{5,3},{6,4},{7,5},{8,14},{9,15},{10,... | collective-permute-start | bytes 737288 | tf_op jit(solution)/shard_map/ppermute | solution.py:239
  84.0 3.3 %collective-permute-done.6.d_ref = bf16[80,1536]{1,0:T(8,128)(2,1)S(1)} collective-permute-done((bf16[80,1536]{1,0:T(8,128)(2,1)S(1)}, bf16[80,1536]{1,0:T(8,128)(2,1)S(1)}, u32[]{:S(2)}, u32[]{:S(2)}) %collective-permute-start.6) | collective-permute-done | bytes 245792 | tf_op jit(solution)/shard_map/ppermute | solution.py:239
  87.3 4.2 %collective-permute-done.7.e_ref = bf16[80,1536]{1,0:T(8,128)(2,1)S(1)} collective-permute-done((bf16[80,1536]{1,0:T(8,128)(2,1)S(1)}, bf16[80,1536]{1,0:T(8,128)(2,1)S(1)}, u32[]{:S(2)}, u32[]{:S(2)}) %collective-permute-start.7) | collective-permute-done | bytes 245792 | tf_op jit(solution)/shard_map/ppermute | solution.py:239
  91.8 5.3 %collective-permute-start.11 = (bf16[80,1664]{1,0:T(8,128)(2,1)S(1)}, bf16[80,1664]{1,0:T(8,128)(2,1)S(1)}, u32[]{:S(2)}, u32[]{:S(2)}) collective-permute-start(bf16[80,1664]{1,0:T(8,128)(2,1)S(1)} %shard_map.122.rest_0_), channel_id=1, source_target_pairs={{0,2},{1,3},{2,4},{3,5},{4,6},{5,7},{6,0},{7,1},{8,10},{9,11},{10,... | collective-permute-start | bytes 798728 | tf_op jit(solution)/shard_map/ppermute | solution.py:239
  97.1 2.6 %collective-permute-start.8 = (bf16[80,1664]{1,0:T(8,128)(2,1)S(1)}, bf16[80,1664]{1,0:T(8,128)(2,1)S(1)}, u32[]{:S(2)}, u32[]{:S(2)}) collective-permute-start(bf16[80,1664]{1,0:T(8,128)(2,1)S(1)} %shard_map.122.rest_0_), channel_id=1, source_target_pairs={{0,6},{1,7},{2,0},{3,1},{4,2},{5,3},{6,4},{7,5},{8,14},{9,15},{10,... | collective-permute-start | bytes 798728 | tf_op jit(solution)/shard_map/ppermute | solution.py:239
  99.8 2.2 %collective-permute-start.14 = (bf16[80,1664]{1,0:T(8,128)(2,1)S(1)}, bf16[80,1664]{1,0:T(8,128)(2,1)S(1)}, u32[]{:S(2)}, u32[]{:S(2)}) collective-permute-start(bf16[80,1664]{1,0:T(8,128)(2,1)S(1)} %shard_map.122.rest_0_), channel_id=1, source_target_pairs={{0,1},{1,2},{2,3},{3,4},{4,5},{5,6},{6,7},{7,0},{8,9},{9,10},{10,1... | collective-permute-start | bytes 798728 | tf_op jit(solution)/shard_map/ppermute | solution.py:239
  102.0 4.8 %collective-permute-start.9 = (bf16[80,1664]{1,0:T(8,128)(2,1)S(1)}, bf16[80,1664]{1,0:T(8,128)(2,1)S(1)}, u32[]{:S(2)}, u32[]{:S(2)}) collective-permute-start(bf16[80,1664]{1,0:T(8,128)(2,1)S(1)} %shard_map.122.rest_0_), channel_id=1, source_target_pairs={{0,7},{1,0},{2,1},{3,2},{4,3},{5,4},{6,5},{7,6},{8,15},{9,8},{10,9... | collective-permute-start | bytes 798728 | tf_op jit(solution)/shard_map/ppermute | solution.py:239
  106.8 4.4 %collective-permute-start.13 = (bf16[80,1664]{1,0:T(8,128)(2,1)S(1)}, bf16[80,1664]{1,0:T(8,128)(2,1)S(1)}, u32[]{:S(2)}, u32[]{:S(2)}) collective-permute-start(bf16[80,1664]{1,0:T(8,128)(2,1)S(1)} %collective-permute-done.11.rest_6_), channel_id=1, source_target_pairs={{0,1},{1,2},{2,3},{3,4},{4,5},{5,6},{6,7},{7,0},{8,9},{9,10},{10,1... | collective-permute-start | bytes 798728 | tf_op jit(solution)/shard_map/ppermute | solution.py:239
  111.3 3.7 %collective-permute-start.12 = (bf16[80,1664]{1,0:T(8,128)(2,1)S(1)}, bf16[80,1664]{1,0:T(8,128)(2,1)S(1)}, u32[]{:S(2)}, u32[]{:S(2)}) collective-permute-start(bf16[80,1664]{1,0:T(8,128)(2,1)S(1)} %broadcast_select_fusion), channel_id=1, source_target_pairs={{0,6},{1,7},{2,0},{3,1},{4,2},{5,3},{6,4},{7,5},{8,10},{9,11},{10,... | collective-permute-start | bytes 798728 | tf_op jit(solution)/shard_map/ppermute | solution.py:247
  115.0 5.4 %collective-permute-start.10 = (bf16[80,1664]{1,0:T(8,128)(2,1)S(1)}, bf16[80,1664]{1,0:T(8,128)(2,1)S(1)}, u32[]{:S(2)}, u32[]{:S(2)}) collective-permute-start(bf16[80,1664]{1,0:T(8,128)(2,1)S(1)} %collective-permute-done.8.rest_2_), channel_id=1, source_target_pairs={{0,7},{1,0},{2,1},{3,2},{4,3},{5,4},{6,5},{7,6},{8,15},{9,8},{10,9... | collective-permute-start | bytes 798728 | tf_op jit(solution)/shard_map/ppermute | solution.py:239
  123.2 3.1 %collective-permute-done.10.rest_3_ = bf16[80,1664]{1,0:T(8,128)(2,1)S(1)} collective-permute-done((bf16[80,1664]{1,0:T(8,128)(2,1)S(1)}, bf16[80,1664]{1,0:T(8,128)(2,1)S(1)}, u32[]{:S(2)}, u32[]{:S(2)}) %collective-permute-start.10) | collective-permute-done | bytes 266272 | tf_op jit(solution)/shard_map/ppermute | solution.py:239
  127.4 1.9 %collective-permute-start.15 = (bf16[320,1664]{1,0:T(8,128)(2,1)S(1)}, bf16[320,1664]{1,0:T(8,128)(2,1)S(1)}, u32[]{:S(2)}, u32[]{:S(2)}) collective-permute-start(bf16[320,1664]{1,0:T(8,128)(2,1)S(1)} %get-tuple-element.62), channel_id=1, source_target_pairs={{0,8},{8,0},{16,24},{24,16},{32,40},{40,32},{48,56},{56,48},{64,72... | collective-permute-start | bytes 3194888 | tf_op jit(solution)/shard_map/ppermute | solution.py:235
  130.3 1.7 collective-permute-done.15.far_ref
  133.6 4.9 %all-to-all-start.2 = ((bf16[8,40,1664]{2,1,0:T(8,128)(2,1)}), bf16[8,40,1664]{2,1,0:T(8,128)(2,1)S(1)}, u32[]{:S(2)}, u32[]{:S(2)}) async-start(bf16[8,40,1664]{2,1,0:T(8,128)(2,1)} %bitcast.5), calls=%async_computation.2 | async-start | bytes 2129920 | tf_op jit(solution)/shard_map/all_to_all | solution.py:230
  138.6 2.1 %fusion.7 = (bf16[320,768]{1,0:T(8,128)(2,1)}, bf16[320,768]{1,0:T(8,128)(2,1)S(1)}) fusion(bf16[320,1536]{1,0:T(8,128)(2,1)} %collective-permute-done.far_ref), kind=kLoop, calls=%fused_computation.12 | loop fusion | bytes 1966080 | tf_op jit(solution)/shard_map/slice | solution.py:314
  140.7 1.7 %convolution_convert_fusion.1 = bf16[768,512]{1,0:T(8,128)(2,1)} fusion(bf16[640,512]{1,0:T(8,128)(2,1)S(1)} %copy-done.7, bf16[320,768]{1,0:T(8,128)(2,1)S(1)} %get-tuple-element.69, bf16[320,768]{1,0:T(8,128)(2,1)S(1)} %get-tuple-element.67), kind=kOutput, calls=%fused_computation.1 | convolution fusion | flops 505675776 | bytes 2424832 | tf_op jit(solution)/shard_map/dot_general | solution.py:15
  142.4 1.7 %convolution_convert_fusion.2 = bf16[768,512]{1,0:T(8,128)(2,1)} fusion(bf16[640,512]{1,0:T(8,128)(2,1)S(1)} %copy-done.5, bf16[320,768]{1,0:T(8,128)(2,1)S(1)} %get-tuple-element.69, bf16[320,768]{1,0:T(8,128)(2,1)S(1)} %get-tuple-element.67), kind=kOutput, calls=%fused_computation.2 | convolution fusion | flops 505675776 | bytes 2424832 | tf_op jit(solution)/shard_map/dot_general | solution.py:15
  144.1 9.5 %all-to-all-done.2.blocks_ref = bf16[8,40,1664]{2,1,0:T(8,128)(2,1)S(1)} async-done(((bf16[8,40,1664]{2,1,0:T(8,128)(2,1)}), bf16[8,40,1664]{2,1,0:T(8,128)(2,1)S(1)}, u32[]{:S(2)}, u32[]{:S(2)}) %all-to-all-start.2) | async-done | bytes 1064992 | tf_op jit(solution)/shard_map/all_to_all | solution.py:230
  154.6 3.3 %all-to-all-start.3 = ((bf16[4,130,128]{2,1,0:T(8,128)(2,1)}), bf16[4,130,128]{2,1,0:T(8,128)(2,1)S(1)}, u32[]{:S(2)}, u32[]{:S(2)}) async-start(bf16[4,130,128]{2,1,0:T(8,128)(2,1)} %reshape.41), calls=%async_computation.3 | async-start | bytes 278528 | tf_op jit(solution)/shard_map/all_to_all | solution.py:230
  158.0 1.7 %convolution_convert_fusion = bf16[512,768]{1,0:T(8,128)(2,1)} fusion(bf16[640,512]{1,0:T(8,128)(2,1)S(1)} %get-tuple-element.58.refs_3_, bf16[320,768]{1,0:T(8,128)(2,1)S(1)} %copy-done.16, bf16[320,768]{1,0:T(8,128)(2,1)S(1)} %get-tuple-element.66), kind=kOutput, calls=%fused_computation | convolution fusion | flops 505675776 | bytes 2424832 | tf_op jit(solution)/shard_map/dot_general | solution.py:15
  159.7 6.9 %all-to-all-done.3 = bf16[4,130,128]{2,1,0:T(8,128)(2,1)S(1)} async-done(((bf16[4,130,128]{2,1,0:T(8,128)(2,1)}), bf16[4,130,128]{2,1,0:T(8,128)(2,1)S(1)}, u32[]{:S(2)}, u32[]{:S(2)}) %all-to-all-start.3) | async-done | bytes 133152 | tf_op jit(solution)/shard_map/all_to_all | solution.py:230
  (62 shorter events, 18.2 us)
Async XLA Ops:
  0.6 0.7 copy-start.8
  1.4 0.7 copy-start.9
  18.7 19.9 %copy-start = (bf16[768,512]{1,0:T(8,128)(2,1)S(1)}, bf16[768,512]{1,0:T(8,128)(2,1)}, u32[]{:S(2)}) copy-start(bf16[768,512]{1,0:T(8,128)(2,1)} %refs_0_.1) | copy-start | bytes 2359300
  18.7 19.9 %copy-start.1 = (bf16[768,512]{1,0:T(8,128)(2,1)S(1)}, bf16[768,512]{1,0:T(8,128)(2,1)}, u32[]{:S(2)}) copy-start(bf16[768,512]{1,0:T(8,128)(2,1)} %refs_1_.1) | copy-start | bytes 2359300
  36.6 4.6 %collective-permute-start = (bf16[320,1536]{1,0:T(8,128)(2,1)S(1)}, bf16[320,1536]{1,0:T(8,128)(2,1)}, u32[]{:S(2)}, u32[]{:S(2)}) collective-permute-start(bf16[320,1536]{1,0:T(8,128)(2,1)S(1)} %bitcast.10), channel_id=1, source_target_pairs={{0,8},{8,0},{16,24},{24,16},{32,40},{40,32},{48,56},{56,48},{64,72... | collective-permute-start | bytes 2949128 | tf_op jit(solution)/shard_map/ppermute | solution.py:235
  38.6 1.1 copy-start.2
  45.7 0.7 copy-start.15
  46.4 21.9 %collective-permute-start.3 = (bf16[80,1536]{1,0:T(8,128)(2,1)}, bf16[80,1536]{1,0:T(8,128)(2,1)}, u32[]{:S(2)}, u32[]{:S(2)}) collective-permute-start(bf16[80,1536]{1,0:T(8,128)(2,1)} %get-tuple-element.46), channel_id=1, source_target_pairs={{0,1},{1,2},{2,3},{3,4},{4,5},{5,6},{6,7},{7,0},{8,9},{9,10},{10,1... | collective-permute-start | bytes 737288 | tf_op jit(solution)/shard_map/ppermute | solution.py:239
  50.7 17.6 %collective-permute-start.4 = (bf16[80,1536]{1,0:T(8,128)(2,1)}, bf16[80,1536]{1,0:T(8,128)(2,1)}, u32[]{:S(2)}, u32[]{:S(2)}) collective-permute-start(bf16[80,1536]{1,0:T(8,128)(2,1)} %get-tuple-element.48), channel_id=1, source_target_pairs={{0,7},{1,0},{2,1},{3,2},{4,3},{5,4},{6,5},{7,6},{8,15},{9,8},{10,9... | collective-permute-start | bytes 737288 | tf_op jit(solution)/shard_map/ppermute | solution.py:239
  59.3 15.3 %collective-permute-start.5 = (bf16[80,1536]{1,0:T(8,128)(2,1)}, bf16[80,1536]{1,0:T(8,128)(2,1)}, u32[]{:S(2)}, u32[]{:S(2)}) collective-permute-start(bf16[80,1536]{1,0:T(8,128)(2,1)} %get-tuple-element.49), channel_id=1, source_target_pairs={{0,2},{1,3},{2,4},{3,5},{4,6},{5,7},{6,0},{7,1},{8,14},{9,15},{10,... | collective-permute-start | bytes 737288 | tf_op jit(solution)/shard_map/ppermute | solution.py:247
  61.2 22.8 %collective-permute-start.1 = (bf16[80,1536]{1,0:T(8,128)(2,1)}, bf16[80,1536]{1,0:T(8,128)(2,1)S(1)}, u32[]{:S(2)}, u32[]{:S(2)}) collective-permute-start(bf16[80,1536]{1,0:T(8,128)(2,1)} %copy-done.15), channel_id=1, source_target_pairs={{0,1},{1,2},{2,3},{3,4},{4,5},{5,6},{6,7},{7,0},{8,9},{9,10},{10,1... | collective-permute-start | bytes 737288 | tf_op jit(solution)/shard_map/ppermute | solution.py:239
  64.3 19.8 %collective-permute-start.2 = (bf16[80,1536]{1,0:T(8,128)(2,1)}, bf16[80,1536]{1,0:T(8,128)(2,1)S(1)}, u32[]{:S(2)}, u32[]{:S(2)}) collective-permute-start(bf16[80,1536]{1,0:T(8,128)(2,1)} %copy-done.14), channel_id=1, source_target_pairs={{0,7},{1,0},{2,1},{3,2},{4,3},{5,4},{6,5},{7,6},{8,15},{9,8},{10,9... | collective-permute-start | bytes 737288 | tf_op jit(solution)/shard_map/ppermute | solution.py:239
  76.0 11.3 %collective-permute-start.6 = (bf16[80,1536]{1,0:T(8,128)(2,1)S(1)}, bf16[80,1536]{1,0:T(8,128)(2,1)S(1)}, u32[]{:S(2)}, u32[]{:S(2)}) collective-permute-start(bf16[80,1536]{1,0:T(8,128)(2,1)S(1)} %get-tuple-element.50), channel_id=1, source_target_pairs={{0,2},{1,3},{2,4},{3,5},{4,6},{5,7},{6,0},{7,1},{8,10},{9,11},{10,... | collective-permute-start | bytes 737288 | tf_op jit(solution)/shard_map/ppermute | solution.py:239
  78.0 13.5 %collective-permute-start.7 = (bf16[80,1536]{1,0:T(8,128)(2,1)S(1)}, bf16[80,1536]{1,0:T(8,128)(2,1)S(1)}, u32[]{:S(2)}, u32[]{:S(2)}) collective-permute-start(bf16[80,1536]{1,0:T(8,128)(2,1)S(1)} %get-tuple-element.51), channel_id=1, source_target_pairs={{0,6},{1,7},{2,0},{3,1},{4,2},{5,3},{6,4},{7,5},{8,14},{9,15},{10,... | collective-permute-start | bytes 737288 | tf_op jit(solution)/shard_map/ppermute | solution.py:239
  91.8 15.0 %collective-permute-start.11 = (bf16[80,1664]{1,0:T(8,128)(2,1)S(1)}, bf16[80,1664]{1,0:T(8,128)(2,1)S(1)}, u32[]{:S(2)}, u32[]{:S(2)}) collective-permute-start(bf16[80,1664]{1,0:T(8,128)(2,1)S(1)} %shard_map.122.rest_0_), channel_id=1, source_target_pairs={{0,2},{1,3},{2,4},{3,5},{4,6},{5,7},{6,0},{7,1},{8,10},{9,11},{10,... | collective-permute-start | bytes 798728 | tf_op jit(solution)/shard_map/ppermute | solution.py:239
  97.1 14.1 %collective-permute-start.8 = (bf16[80,1664]{1,0:T(8,128)(2,1)S(1)}, bf16[80,1664]{1,0:T(8,128)(2,1)S(1)}, u32[]{:S(2)}, u32[]{:S(2)}) collective-permute-start(bf16[80,1664]{1,0:T(8,128)(2,1)S(1)} %shard_map.122.rest_0_), channel_id=1, source_target_pairs={{0,6},{1,7},{2,0},{3,1},{4,2},{5,3},{6,4},{7,5},{8,14},{9,15},{10,... | collective-permute-start | bytes 798728 | tf_op jit(solution)/shard_map/ppermute | solution.py:239
  99.8 22.0 %collective-permute-start.14 = (bf16[80,1664]{1,0:T(8,128)(2,1)S(1)}, bf16[80,1664]{1,0:T(8,128)(2,1)S(1)}, u32[]{:S(2)}, u32[]{:S(2)}) collective-permute-start(bf16[80,1664]{1,0:T(8,128)(2,1)S(1)} %shard_map.122.rest_0_), channel_id=1, source_target_pairs={{0,1},{1,2},{2,3},{3,4},{4,5},{5,6},{6,7},{7,0},{8,9},{9,10},{10,1... | collective-permute-start | bytes 798728 | tf_op jit(solution)/shard_map/ppermute | solution.py:239
  102.0 19.8 %collective-permute-start.9 = (bf16[80,1664]{1,0:T(8,128)(2,1)S(1)}, bf16[80,1664]{1,0:T(8,128)(2,1)S(1)}, u32[]{:S(2)}, u32[]{:S(2)}) collective-permute-start(bf16[80,1664]{1,0:T(8,128)(2,1)S(1)} %shard_map.122.rest_0_), channel_id=1, source_target_pairs={{0,7},{1,0},{2,1},{3,2},{4,3},{5,4},{6,5},{7,6},{8,15},{9,8},{10,9... | collective-permute-start | bytes 798728 | tf_op jit(solution)/shard_map/ppermute | solution.py:239
  106.8 14.9 %collective-permute-start.13 = (bf16[80,1664]{1,0:T(8,128)(2,1)S(1)}, bf16[80,1664]{1,0:T(8,128)(2,1)S(1)}, u32[]{:S(2)}, u32[]{:S(2)}) collective-permute-start(bf16[80,1664]{1,0:T(8,128)(2,1)S(1)} %collective-permute-done.11.rest_6_), channel_id=1, source_target_pairs={{0,1},{1,2},{2,3},{3,4},{4,5},{5,6},{6,7},{7,0},{8,9},{9,10},{10,1... | collective-permute-start | bytes 798728 | tf_op jit(solution)/shard_map/ppermute | solution.py:239
  111.3 11.9 %collective-permute-start.12 = (bf16[80,1664]{1,0:T(8,128)(2,1)S(1)}, bf16[80,1664]{1,0:T(8,128)(2,1)S(1)}, u32[]{:S(2)}, u32[]{:S(2)}) collective-permute-start(bf16[80,1664]{1,0:T(8,128)(2,1)S(1)} %broadcast_select_fusion), channel_id=1, source_target_pairs={{0,6},{1,7},{2,0},{3,1},{4,2},{5,3},{6,4},{7,5},{8,10},{9,11},{10,... | collective-permute-start | bytes 798728 | tf_op jit(solution)/shard_map/ppermute | solution.py:247
  115.0 11.2 %collective-permute-start.10 = (bf16[80,1664]{1,0:T(8,128)(2,1)S(1)}, bf16[80,1664]{1,0:T(8,128)(2,1)S(1)}, u32[]{:S(2)}, u32[]{:S(2)}) collective-permute-start(bf16[80,1664]{1,0:T(8,128)(2,1)S(1)} %collective-permute-done.8.rest_2_), channel_id=1, source_target_pairs={{0,7},{1,0},{2,1},{3,2},{4,3},{5,4},{6,5},{7,6},{8,15},{9,8},{10,9... | collective-permute-start | bytes 798728 | tf_op jit(solution)/shard_map/ppermute | solution.py:239
  120.4 1.1 copy-start.3
  127.4 2.9 %copy-start.4 = (bf16[640,512]{1,0:T(8,128)(2,1)}, bf16[640,512]{1,0:T(8,128)(2,1)S(1)}, u32[]{:S(2)}) copy-start(bf16[640,512]{1,0:T(8,128)(2,1)S(1)} %get-tuple-element.59.refs_4_) | copy-start | bytes 1966084
  127.4 2.9 %copy-start.6 = (bf16[640,512]{1,0:T(8,128)(2,1)}, bf16[640,512]{1,0:T(8,128)(2,1)S(1)}, u32[]{:S(2)}) copy-start(bf16[640,512]{1,0:T(8,128)(2,1)S(1)} %get-tuple-element.60.refs_5_) | copy-start | bytes 1966084
  127.4 4.6 %collective-permute-start.15 = (bf16[320,1664]{1,0:T(8,128)(2,1)S(1)}, bf16[320,1664]{1,0:T(8,128)(2,1)S(1)}, u32[]{:S(2)}, u32[]{:S(2)}) collective-permute-start(bf16[320,1664]{1,0:T(8,128)(2,1)S(1)} %get-tuple-element.62), channel_id=1, source_target_pairs={{0,8},{8,0},{16,24},{24,16},{32,40},{40,32},{48,56},{56,48},{64,72... | collective-permute-start | bytes 3194888 | tf_op jit(solution)/shard_map/ppermute | solution.py:235
  133.6 19.9 %all-to-all-start.2 = ((bf16[8,40,1664]{2,1,0:T(8,128)(2,1)}), bf16[8,40,1664]{2,1,0:T(8,128)(2,1)S(1)}, u32[]{:S(2)}, u32[]{:S(2)}) async-start(bf16[8,40,1664]{2,1,0:T(8,128)(2,1)} %bitcast.5), calls=%async_computation.2 | async-start | bytes 2129920 | tf_op jit(solution)/shard_map/all_to_all | solution.py:230
  138.6 2.1 %copy-start.7 = (bf16[640,512]{1,0:T(8,128)(2,1)S(1)}, bf16[640,512]{1,0:T(8,128)(2,1)}, u32[]{:S(2)}) copy-start(bf16[640,512]{1,0:T(8,128)(2,1)} %copy-done.6) | copy-start | bytes 1966084
  140.7 1.7 %copy-start.5 = (bf16[640,512]{1,0:T(8,128)(2,1)S(1)}, bf16[640,512]{1,0:T(8,128)(2,1)}, u32[]{:S(2)}) copy-start(bf16[640,512]{1,0:T(8,128)(2,1)} %copy-done.4) | copy-start | bytes 1966084
  144.1 13.9 %copy-start.16 = (bf16[320,768]{1,0:T(8,128)(2,1)S(1)}, bf16[320,768]{1,0:T(8,128)(2,1)}, u32[]{:S(2)}) copy-start(bf16[320,768]{1,0:T(8,128)(2,1)} %get-tuple-element.68) | copy-start | bytes 1474564
  154.6 12.0 %all-to-all-start.3 = ((bf16[4,130,128]{2,1,0:T(8,128)(2,1)}), bf16[4,130,128]{2,1,0:T(8,128)(2,1)S(1)}, u32[]{:S(2)}, u32[]{:S(2)}) async-start(bf16[4,130,128]{2,1,0:T(8,128)(2,1)} %reshape.41), calls=%async_computation.3 | async-start | bytes 278528 | tf_op jit(solution)/shard_map/all_to_all | solution.py:230
  158.0 8.8 %copy-start.11 = (s32[16,2]{0,1:T(2,128)S(1)}, s32[16,2]{0,1:T(2,128)}, u32[]{:S(2)}) copy-start(s32[16,2]{0,1:T(2,128)} %param.8) | copy-start | bytes 388
  158.0 8.8 %copy-start.13 = (f32[16,2]{0,1:T(2,128)S(1)}, f32[16,2]{0,1:T(2,128)}, u32[]{:S(2)}) copy-start(f32[16,2]{0,1:T(2,128)} %param.9) | copy-start | bytes 388
  (3 other events, 2.0 us)
